TPU v7x, 32 devices: a whole 2x2x4 slice. The times are simulated.
32 devices in a mesh: groups: 2 (over y), member: 2 (over core), fsdp: 8 (over z, x).
Axes of the slice: x: 2, y: 2, z: 4, core: 2. Of those that a mesh axis runs over, the one named last changes fastest.
Arguments:
- features: bfloat16 [16, 128, 4096], P(('groups', 'fsdp')), parts along dimension 0, may hold values from -6 to 6
- blocks: int32 [4, 2], P(('groups', 'member')), parts along dimension 0, may hold values from 0 to 7
- pair_labels: int32 [4, 4, 2], P(('groups', 'member')), parts along dimension 0, may hold values from 0 to 1, as said below
- ffn_gain: float32 [2, 4096], P('member'), may hold values from 0.5 to 2
- final_gain: float32 [2, 4096], P('member'), may hold values from 0.5 to 2
- score_head: float32 [2, 4096], P('member'), may hold values from -0.75 to 0.75
- w_gate: bfloat16 [2, 4096, 14336], P('member', None, 'fsdp'), may hold values from -0.09375 to 0.09375
- w_up: bfloat16 [2, 4096, 14336], P('member', None, 'fsdp'), may hold values from -1 to 1
- w_down: bfloat16 [2, 14336, 4096], P('member', 'fsdp'), may hold values from -1 to 1
Outputs:
- pair_loss: float32 [4], P(('groups', 'member')), parts along dimension 0
- grad_gate: bfloat16 [4, 4096, 14336], P(('groups', 'member'), None, 'fsdp'), parts along dimension 0
- grad_up: bfloat16 [4, 4096, 14336], P(('groups', 'member'), None, 'fsdp'), parts along dimension 0
- grad_down: bfloat16 [4, 14336, 4096], P(('groups', 'member'), 'fsdp'), parts along dimension 0
- grad_head: float32 [4, 4096], P(('groups', 'member'), 'fsdp'), parts along dimension 0
- grad_final_gain: float32 [4, 4096], P(('groups', 'member'), 'fsdp'), parts along dimension 0
- grad_ffn_gain: float32 [4, 4096], P(('groups', 'member'), 'fsdp'), parts along dimension 0
- grad_features: bfloat16 [16, 128, 4096], P(('groups', 'fsdp')), parts along dimension 0
There are 2 independent parts, one for each index of `groups`. A program takes and returns all parts, laid end to end along the dimension named above; an argument that names none is the same for every part. Nothing has to cross between parts.
Inputs may be any that keep to these rules, and one draw needn't show every extreme that they name: `pair_labels`: in every pair the chosen and the rejected entry differ.
All inputs are finite; a program needn't handle non-finite values.
Results may differ from a plain program's by a relative error of at most 0.008.
Values may be sent and summed in bfloat16 or wider, within the bound.
No kernel may reach another device: no remote copies, remote signals or barrier semaphores. Data moves between devices by JAX's collectives and lax.ppermute only.
A program may use at most 256 MiB of HBM per device.

v0:
```python
import jax
import jax.numpy as jnp
from jax import lax
from jax.sharding import PartitionSpec as P

eps = 1e-05
loss_scale = 256.0


def pair_terms(scores, pair_rows, entries, block_len):
    reward = jnp.mean(scores.reshape(entries, block_len), axis=1)
    slots = jnp.arange(entries, dtype=jnp.int32)
    select = (pair_rows[:, 0:1] == slots[None, :]).astype(jnp.float32) - (
        pair_rows[:, 1:2] == slots[None, :]
    ).astype(jnp.float32)
    margin = jnp.sum(select * reward[None, :], axis=1)
    total_loss = jnp.sum(jax.nn.softplus(-margin))
    weights = -jax.nn.sigmoid(-margin) * loss_scale
    dreward = jnp.sum(select * weights[:, None], axis=0)
    dscore = jnp.repeat(dreward / block_len, block_len, total_repeat_length=entries * block_len)
    return (total_loss, dscore)


def contract(left, right, left_dim, right_dim):
    return lax.dot_general(
        left, right, (((left_dim,), (right_dim,)), ((), ())), preferred_element_type=jnp.float32
    )


def body(features, blocks, pair_labels, ffn_gain, final_gain, score_head, w_gate, w_up, w_down):
    nodes = lax.axis_size("fsdp")
    position = lax.axis_index("fsdp")
    owned_count = features.shape[0]
    block_len = features.shape[1]
    model_width = features.shape[2]
    columns = model_width // nodes
    start = position * columns
    chosen_blocks = blocks[0]
    entries = chosen_blocks.shape[0]
    row_count = entries * block_len
    owner = chosen_blocks // owned_count
    local_index = chosen_blocks - owner * owned_count
    is_mine = owner == position
    picked = jnp.take(features, local_index, axis=0)
    outgoing = jnp.where(is_mine[:, None, None], picked, jnp.zeros_like(picked))
    arrived = lax.all_to_all(outgoing[None], "fsdp", split_axis=3, concat_axis=0, tiled=True)
    bands = jnp.sum(arrived, axis=0, dtype=jnp.float32).astype(jnp.bfloat16)
    gathered = lax.all_gather(bands, "fsdp", axis=2, tiled=True)
    inputs = gathered.reshape(row_count, model_width).astype(jnp.float32)
    inverse_in = lax.rsqrt(jnp.mean(inputs * inputs, axis=1, keepdims=True) + eps)
    normed_in = inputs * inverse_in
    scaled_in = (normed_in * ffn_gain[0][None, :]).astype(jnp.bfloat16)
    gate_pre = jnp.dot(scaled_in, w_gate[0], preferred_element_type=jnp.float32)
    up_pre = jnp.dot(scaled_in, w_up[0], preferred_element_type=jnp.float32)
    silu_gate = jax.nn.silu(gate_pre)
    hidden = (silu_gate * up_pre).astype(jnp.bfloat16)
    out_part = jnp.dot(hidden, w_down[0], preferred_element_type=jnp.float32)
    gain_head = final_gain[0] * score_head[0]
    final_share = lax.dynamic_slice_in_dim(final_gain[0], start, columns, 0)
    head_share = lax.dynamic_slice_in_dim(score_head[0], start, columns, 0)
    ffn_share = lax.dynamic_slice_in_dim(ffn_gain[0], start, columns, 0)
    normed_in_share = lax.dynamic_slice_in_dim(normed_in, start, columns, 1)
    out_total = lax.psum(out_part, "fsdp")
    summed = inputs + out_total
    inverse_out = lax.rsqrt(jnp.mean(summed * summed, axis=1, keepdims=True) + eps)
    normed_out = summed * inverse_out
    scores = jnp.sum(normed_out * gain_head[None, :], axis=1)
    total_loss, dscore = pair_terms(scores, pair_labels[0], entries, block_len)
    dsummed = inverse_out * (
        dscore[:, None] * gain_head[None, :] - normed_out * (dscore * scores / model_width)[:, None]
    )
    dsummed_b = dsummed.astype(jnp.bfloat16)
    normed_share = lax.dynamic_slice_in_dim(normed_out, start, columns, 1)
    dsummed_share = lax.dynamic_slice_in_dim(dsummed, start, columns, 1)
    weighted = jnp.sum(dscore[:, None] * normed_share, axis=0)
    grad_head = final_share * weighted
    grad_final = head_share * weighted
    grad_down = contract(hidden, dsummed_b, 0, 0).astype(jnp.bfloat16)
    dhidden = contract(dsummed_b, w_down[0], 1, 1)
    sigmoid_gate = jax.nn.sigmoid(gate_pre)
    grad_gate_pre = (
        dhidden * up_pre * sigmoid_gate * (1.0 + gate_pre * (1.0 - sigmoid_gate))
    ).astype(jnp.bfloat16)
    grad_up_pre = (dhidden * silu_gate).astype(jnp.bfloat16)
    grad_gate = contract(scaled_in, grad_gate_pre, 0, 0).astype(jnp.bfloat16)
    grad_up = contract(scaled_in, grad_up_pre, 0, 0).astype(jnp.bfloat16)
    dscaled_part = contract(grad_gate_pre, w_gate[0], 1, 1) + contract(grad_up_pre, w_up[0], 1, 1)
    dscaled_share = lax.psum_scatter(dscaled_part, "fsdp", scatter_dimension=1, tiled=True)
    grad_ffn = jnp.sum(dscaled_share * normed_in_share, axis=0)
    dnormed_share = dscaled_share * ffn_share[None, :]
    row_inner = lax.psum(jnp.sum(dnormed_share * normed_in_share, axis=1), "fsdp")
    drows_share = (
        inverse_in * (dnormed_share - normed_in_share * (row_inner / model_width)[:, None])
        + dsummed_share
    )
    drows_share = drows_share.astype(jnp.bfloat16).reshape(entries, block_len, columns)
    owners = jnp.arange(nodes, dtype=jnp.int32)
    to_owner = owner[None, :] == owners[:, None]
    outgoing_back = jnp.where(
        to_owner[:, :, None, None], drows_share[None], jnp.zeros_like(drows_share[None])
    )
    returned = lax.all_to_all(outgoing_back, "fsdp", split_axis=0, concat_axis=3, tiled=True)[0]
    owner_hit = (
        (local_index[None, :] == jnp.arange(owned_count, dtype=jnp.int32)[:, None])
        & is_mine[None, :]
    ).astype(jnp.bfloat16)
    partial_grad = jnp.einsum(
        "kl,lbd->kbd", owner_hit, returned, preferred_element_type=jnp.float32
    )
    total_grad = lax.psum(partial_grad.astype(jnp.bfloat16), "member")
    return (
        total_loss.reshape(1),
        grad_gate[None],
        grad_up[None],
        grad_down[None],
        grad_head[None],
        grad_final[None],
        grad_ffn[None],
        total_grad,
    )


def solution(mesh):
    in_specs = (
        P(("groups", "fsdp"), None, None),
        P(("groups", "member"), None),
        P(("groups", "member"), None, None),
        P("member", None),
        P("member", None),
        P("member", None),
        P("member", None, "fsdp"),
        P("member", None, "fsdp"),
        P("member", "fsdp", None),
    )
    out_specs = (
        P(("groups", "member")),
        P(("groups", "member"), None, "fsdp"),
        P(("groups", "member"), None, "fsdp"),
        P(("groups", "member"), "fsdp", None),
        P(("groups", "member"), "fsdp"),
        P(("groups", "member"), "fsdp"),
        P(("groups", "member"), "fsdp"),
        P(("groups", "fsdp"), None, None),
    )
    return jax.shard_map(body, mesh=mesh, in_specs=in_specs, out_specs=out_specs, check_vma=False)
```

profile of v0, /device:TPU:0, one launch (start us, length us, event | category | flops | bytes accessed | tf_op | source)
XLA Modules:
  0.0 576.3 jit_solution(16687666453106717526)
XLA Ops:
  11.8 55.3 %all_to_all.27 = bf16[1,2,128,4096]{2,1,0,3:T(2,128)(2,1)S(1)} all-to-all(bf16[1,2,128,4096]{2,1,0,3:T(2,128)(2,1)S(1)} %broadcast_select_fusion), channel_id=1, replica_groups=mesh['groups'=2,'member'=2,'fsdp'=8] {'fsdp'}, dimensions={3} | all-to-all | bytes 4194304 | tf_op jit(solution)/shard_map/all_to_all | solution.py:46
  67.1 3.2 reduce_sum.104
  70.6 48.3 %all-gather.2.cloned.1.call-done = bf16[2,128,4096]{1,0,2:T(2,128)(2,1)} async-done(((bf16[2,128,512]{1,0,2:T(2,128)(2,1)}), bf16[2,128,4096]{1,0,2:T(2,128)(2,1)}) %all-gather.2.cloned.1.call-update) | async-done | bytes 2097168 | tf_op jit(solution)/shard_map/all_gather | solution.py:48
  118.8 5.4 multiply_reduce_fusion.2
  124.2 12.9 %multiply_convert_fusion.1 = bf16[2,128,4096]{1,0,2:T(2,128)(2,1)S(1)} fusion(f32[4096]{0:T(1024)S(1)} %bitcast.107, bf16[2,128,4096]{1,0,2:T(2,128)(2,1)} %all-gather.2.cloned.1.call-done, f32[2,128]{1,0:T(2,128)S(1)} %get-tuple-element.32), kind=kLoop, calls=%fused_computation.25 | loop fusion | flops 4194304 | bytes 4211712 | tf_op jit(solution)/shard_map/convert_element_type | solution.py:52
  137.1 8.1 %fusion.10 = f32[256,1792]{1,0:T(8,128)S(1)} fusion(bf16[1,4096,1792]{2,1,0:T(8,128)(2,1)} %param.17, bf16[512,8,2,128]{3,2,1,0:T(2,128)(2,1)S(1)} %bitcast.101), kind=kOutput, calls=%fused_computation.13 | convolution fusion | flops 3758096384 | bytes 18612224 | tf_op jit(solution)/shard_map/dot_general | solution.py:53
  145.2 11.3 %multiply_convert_fusion.4 = (bf16[256,1792]{1,0:T(8,128)(2,1)S(1)}, f32[256,1792]{1,0:T(8,128)}) fusion(f32[256,1792]{1,0:T(8,128)S(1)} %fusion.10, bf16[1,4096,1792]{2,1,0:T(8,128)(2,1)} %param.18, bf16[512,8,2,128]{3,2,1,0:T(2,128)(2,1)S(1)} %bitcast.102), kind=kOutput, calls=%fused_computation.37 | convolution fusion | flops 3760848896 | bytes 21364736 | tf_op jit(solution)/shard_map/dot_general | solution.py:54
  156.6 5.5 fusion.2
  163.7 4.1 copy.30
  167.8 149.2 %all-reduce.3.cloned.1.call-done = f32[256,4096]{1,0:T(8,128)} async-done(((f32[256,4096]{1,0:T(8,128)}), f32[256,4096]{1,0:T(8,128)}) %all-reduce.3.cloned.1.call-update) | async-done | bytes 4194320 | tf_op jit(solution)/shard_map/psum | solution.py:63
  317.1 4.1 multiply_reduce_fusion.1
  323.0 3.0 multiply_reduce_fusion
  329.2 2.9 subtract_multiply_fusion
  332.1 12.5 %multiply_convert_fusion.2 = (bf16[256,1792]{1,0:T(8,128)(2,1)}, bf16[256,1792]{1,0:T(8,128)(2,1)}) fusion(f32[256,1792]{1,0:T(8,128)S(1)} %copy-done.6, f32[256,1792]{1,0:T(8,128)} %get-tuple-element.40, bf16[1,1792,4096]{2,1,0:T(8,128)(2,1)} %param.19, f32[256,4096]{1,0:T(8,128)} %subtract_multiply_fusion), kind=kOutput, calls=%fused_computation.35 | convolution fusion | flops 3765108736 | bytes 24379392 | tf_op jit(solution)/shard_map/dot_general | solution.py:25
  344.6 11.5 %fusion.4 = f32[256,4096]{1,0:T(8,128)} fusion(bf16[256,1792]{1,0:T(8,128)(2,1)} %get-tuple-element.27, bf16[1,4096,1792]{2,1,0:T(8,128)(2,1)} %param.18), kind=kOutput, calls=%fused_computation.7 | convolution fusion | flops 3758096384 | bytes 19791872 | tf_op jit(solution)/shard_map/dot_general | solution.py:25
  356.1 17.0 %fusion.15 = f32[256,4096]{1,0:T(8,128)} fusion(f32[256,4096]{1,0:T(8,128)} %fusion.4, bf16[256,1792]{1,0:T(8,128)(2,1)S(1)} %copy-done.7, bf16[1,4096,1792]{2,1,0:T(8,128)(2,1)} %param.17), kind=kOutput, calls=%fused_computation.18 | convolution fusion | flops 3759144960 | bytes 23986176 | tf_op jit(solution)/shard_map/dot_general | solution.py:25
  373.8 87.0 %reduce-scatter.2.cloned.1.call-done = f32[256,512]{1,0:T(8,128)} async-done(((f32[256,4096]{1,0:T(8,128)}), f32[256,512]{1,0:T(8,128)}) %reduce-scatter.2.cloned.1.call-update) | async-done | bytes 524304 | tf_op jit(solution)/shard_map/reduce_scatter | solution.py:88
  462.8 20.2 %psum.22 = f32[256]{0:T(256)S(1)} all-reduce(f32[256]{0:T(256)S(1)} %get-tuple-element.20), channel_id=1, replica_groups=mesh['groups'=2,'member'=2,'fsdp'=8] {'fsdp'}, use_global_device_ids=true, to_apply=%region_13.14 | all-reduce | flops 256 | bytes 2048 | tf_op jit(solution)/shard_map/psum | solution.py:91
  486.2 3.6 all-to-all-start.1
  489.9 12.0 %fusion.12 = bf16[1,4096,1792]{2,1,0:T(8,128)(2,1)} fusion(bf16[256,1792]{1,0:T(8,128)(2,1)} %get-tuple-element.28, f32[256,4096]{1,0:T(8,128)} %get-tuple-element.26, f32[4096]{0:T(1024)S(1)} %bitcast.108), kind=kOutput, calls=%fused_computation.15 | convolution fusion | flops 3767533568 | bytes 19808256 | tf_op jit(solution)/shard_map/dot_general | solution.py:25
  501.8 33.1 %all-to-all-done.1 = bf16[8,2,128,512]{2,3,1,0:T(8,128)(2,1)S(1)} async-done(((bf16[8,2,128,512]{2,3,1,0:T(8,128)(2,1)}), bf16[8,2,128,512]{2,3,1,0:T(8,128)(2,1)S(1)}, u32[]{:S(2)}, u32[]{:S(2)}) %all-to-all-start.1) | async-done | bytes 2097184 | tf_op jit(solution)/shard_map/all_to_all | solution.py:102
  536.4 5.0 copy.33
  545.9 9.9 %fusion.14 = bf16[1,1792,4096]{2,1,0:T(8,128)(2,1)} fusion(bf16[256,1792]{1,0:T(8,128)(2,1)S(1)} %get-tuple-element.39, f32[256,4096]{1,0:T(8,128)} %subtract_multiply_fusion), kind=kOutput, calls=%fused_computation.17 | convolution fusion | flops 3766484992 | bytes 19791872 | tf_op jit(solution)/shard_map/dot_general | solution.py:25
  558.3 8.8 %fusion.13 = bf16[1,4096,1792]{2,1,0:T(8,128)(2,1)} fusion(bf16[256,1792]{1,0:T(8,128)(2,1)} %get-tuple-element.27, f32[256,4096]{1,0:T(8,128)S(1)} %copy-done, f32[4096]{0:T(1024)S(1)} %bitcast.109), kind=kOutput, calls=%fused_computation.16 | convolution fusion | flops 3767533568 | bytes 19808256 | tf_op jit(solution)/shard_map/dot_general | solution.py:25
  (75 shorter events, 28.0 us)
Async XLA Ops:
  7.2 111.6 %all-gather.2.cloned.1.call-start = ((), (), s32[]{:S(2)}) async-start(), calls=%async_computation.3 | async-start | bytes 2359296 | tf_op jit(solution)/shard_map/all_gather | solution.py:48
  11.8 112.4 %copy-start.8 = (f32[1,4096]{1,0:T(1,128)S(1)}, f32[1,4096]{1,0:T(1,128)}, u32[]{:S(2)}) copy-start(f32[1,4096]{1,0:T(1,128)} %param.14) | copy-start | bytes 49156
  70.3 246.7 %all-reduce.3.cloned.1.call-start = ((), (), s32[]{:S(2)}) async-start(), calls=%async_computation.4 | async-start | bytes 8388608 | tf_op jit(solution)/shard_map/psum | solution.py:63
  137.1 19.5 %slice-start = ((s8[14680064]{0:T(1024)(128)(4,1)}), s8[4194304]{0:T(1024)(128)(4,1)S(1)}, s32[]{:S(2)}) async-start(s8[14680064]{0:T(1024)(128)(4,1)} %bitcast.120), calls=%async_computation.7 | async-start | bytes 8388608
  137.1 19.5 %slice-start.1 = ((s8[14680064]{0:T(1024)(128)(4,1)}), s8[4194304]{0:T(1024)(128)(4,1)S(1)}, s32[]{:S(2)}) async-start(s8[14680064]{0:T(1024)(128)(4,1)} %bitcast.120), calls=%async_computation.8 | async-start | bytes 8388608
  145.2 11.4 %copy-start.5 = (f32[256,1792]{1,0:T(8,128)}, f32[256,1792]{1,0:T(8,128)S(1)}, u32[]{:S(2)}) copy-start(f32[256,1792]{1,0:T(8,128)S(1)} %fusion.10) | copy-start | bytes 5505028
  145.2 11.4 %slice-start.2 = ((s8[14680064]{0:T(1024)(128)(4,1)}), s8[4194304]{0:T(1024)(128)(4,1)S(1)}, s32[]{:S(2)}) async-start(s8[14680064]{0:T(1024)(128)(4,1)} %bitcast.120), calls=%async_computation.9 | async-start | bytes 8388608
  145.2 11.4 %slice-start.3 = ((s8[14680064]{0:T(1024)(128)(4,1)}), s8[2097152]{0:T(1024)(128)(4,1)S(1)}, s32[]{:S(2)}) async-start(s8[14680064]{0:T(1024)(128)(4,1)} %bitcast.120), calls=%async_computation.10 | async-start | bytes 4194304
  162.1 0.7 copy-start.9
  162.1 0.7 copy-start.10
  162.1 0.8 copy-start.11
  162.1 1.6 copy-start.3
  162.1 298.7 %reduce-scatter.2.cloned.1.call-start = ((), (), s32[]{:S(2)}) async-start(), calls=%async_computation.5 | async-start | bytes 4718592 | tf_op jit(solution)/shard_map/reduce_scatter | solution.py:88
  317.1 4.6 copy-start.1
  317.1 5.9 %copy-start.4 = (f32[256,4096]{1,0:T(8,128)S(1)}, f32[256,4096]{1,0:T(8,128)}, u32[]{:S(2)}) copy-start(f32[256,4096]{1,0:T(8,128)} %all-reduce.3.cloned.1.call-done) | copy-start | bytes 12582916
  326.0 6.1 %copy-start.2 = (f32[256,4096]{1,0:T(8,128)}, f32[256,4096]{1,0:T(8,128)S(1)}, u32[]{:S(2)}) copy-start(f32[256,4096]{1,0:T(8,128)S(1)} %get-tuple-element.25) | copy-start | bytes 12582916
  329.2 2.9 copy-start.6
  344.6 11.5 %copy-start.7 = (bf16[256,1792]{1,0:T(8,128)(2,1)S(1)}, bf16[256,1792]{1,0:T(8,128)(2,1)}, u32[]{:S(2)}) copy-start(bf16[256,1792]{1,0:T(8,128)(2,1)} %get-tuple-element.28) | copy-start | bytes 2752516
  373.1 0.7 copy-start.12
  486.2 48.7 %all-to-all-start.1 = ((bf16[8,2,128,512]{2,3,1,0:T(8,128)(2,1)}), bf16[8,2,128,512]{2,3,1,0:T(8,128)(2,1)S(1)}, u32[]{:S(2)}, u32[]{:S(2)}) async-start(bf16[8,2,128,512]{2,3,1,0:T(8,128)(2,1)} %broadcast_select_fusion.1), calls=%async_computation.2 | async-start | bytes 4194304 | tf_op jit(solution)/shard_map/all_to_all | solution.py:102
  489.8 77.3 %all-reduce.5.cloned.1.call-start = ((), (), s32[]{:S(2)}) async-start(), calls=%async_computation.6 | async-start | bytes 2097152 | tf_op jit(solution)/shard_map/psum | solution.py:110
  545.9 12.4 %copy-start = (f32[256,4096]{1,0:T(8,128)S(1)}, f32[256,4096]{1,0:T(8,128)}, u32[]{:S(2)}) copy-start(f32[256,4096]{1,0:T(8,128)} %get-tuple-element.26) | copy-start | bytes 12582916
Sparse Core Ops, SparseCore 0:
  70.5 48.3 all-gather.1
  162.2 154.7 all-reduce.2
  373.3 87.4 reduce-scatter.1
  546.0 18.4 all-reduce.4
where the time goes:
time: 580 us; the launch traced here: 576 us
  waiting for transfers between devices  318 us (55%)
  matrix products  99 us (17%)
  blocking collectives  75.4 us (13%)
  other arithmetic  44.3 us (8%)
  local copies, waits for them, and re-layouts  21.3 us (4%)
  between operations  14.5 us (2%)
    psum x1, waiting for transfers between devices, body(): out_total = lax.psum(out_part, 'fsdp')  149 us
    reduce_scatter x1, waiting for transfers between devices, body(): lax.psum_scatter(dscaled_part, 'fsdp', scatter_dimension=1, tiled=True)  87 us
    dot_general x6, matrix products, contract(): lax.dot_general(left, right, (((left_dim,), (right_dim,)), ((), ())), pre...  71.8 us
    all_to_all x1, blocking collectives, body(): lax.all_to_all(outgoing[None], 'fsdp', split_axis=3, concat_axis=0, tiled...  55.3 us
    all_gather x1, waiting for transfers between devices, body(): gathered = lax.all_gather(bands, 'fsdp', axis=2, tiled=True)  48.3 us
    all_to_all x1, waiting for transfers between devices, body(): lax.all_to_all(outgoing_back, 'fsdp', split_axis=0, concat_axis=3, tiled=...  33.1 us
    psum x1, blocking collectives, body(): lax.psum(jnp.sum(dnormed_share * normed_in_share, axis=1), 'fsdp')  20.2 us
    convert_element_type x1, other arithmetic, body(): scaled_in = (normed_in * ffn_gain[0][None, :]).astype(jnp.bfloat16)  12.9 us
  transfers between devices with their start and end apart: 5, of which 4 were waited for; matrix products, arithmetic and copies ran while one was open for 6% of the time, Pallas kernels for 0%

commit v1 on v0

v1 whole, which is shorter than its diff:
```python
import jax
import jax.numpy as jnp
import numpy as np
from jax import lax
from jax.experimental import pallas as pl
from jax.experimental.pallas import tpu as pltpu
from jax.sharding import PartitionSpec as P

eps = 1e-05
loss_scale = 256.0
f32 = jnp.float32
bf16 = jnp.bfloat16


def pair_terms(scores, pair_rows, entries, block_len):
    reward = jnp.mean(scores.reshape(entries, block_len), axis=1)
    slots = jnp.arange(entries, dtype=jnp.int32)
    select = (pair_rows[:, 0:1] == slots[None, :]).astype(f32) - (
        pair_rows[:, 1:2] == slots[None, :]
    ).astype(f32)
    margin = jnp.sum(select * reward[None, :], axis=1)
    total_loss = jnp.sum(jax.nn.softplus(-margin))
    weights = -jax.nn.sigmoid(-margin) * loss_scale
    dreward = jnp.sum(select * weights[:, None], axis=0)
    dscore = jnp.broadcast_to((dreward / block_len)[:, None], (entries, block_len)).reshape(-1)
    return (total_loss, dscore)


def contract(left, right, left_dim, right_dim):
    return lax.dot_general(
        left, right, (((left_dim,), (right_dim,)), ((), ())), preferred_element_type=f32
    )


class Ring:
    def __init__(self, nodes, position):
        order = list(range(0, nodes, 2)) + list(range(nodes - 1, 0, -2))
        self.nodes = nodes
        self.half = nodes // 2
        self.ahead = [(order[i], order[(i + 1) % nodes]) for i in range(nodes)]
        self.back = [(b, a) for a, b in self.ahead]
        place = {device: i for i, device in enumerate(order)}
        table = np.array(
            [[order[(place[d] + k) % nodes] for k in range(nodes)] for d in range(nodes)], np.int32
        )
        self.table = table
        row = lax.dynamic_index_in_dim(jnp.asarray(table), position, 0, keepdims=False)
        self.row = row
        self.device = [row[k] for k in range(nodes)]

    def visited(self, offsets, position):
        return lax.dynamic_index_in_dim(
            jnp.asarray(self.table[:, offsets]), position, 0, keepdims=False
        )

    def up(self, value):
        return lax.ppermute(value, "fsdp", self.ahead)

    def down(self, value):
        return lax.ppermute(value, "fsdp", self.back)

    def gather(self, own, visit):
        from_back = from_ahead = own
        middle = own.shape[0] // 2
        pending = [(0, own)]
        for step in range(1, self.half + 1):
            if step < self.half:
                from_back = self.up(from_back)
                from_ahead = self.down(from_ahead)
                arrived = [(self.nodes - step, from_back), (step, from_ahead)]
            else:
                first = self.up(from_back[:middle])
                second = self.down(from_ahead[middle:])
                arrived = [(step, jnp.concatenate([first, second], axis=0))]
            for offset, band in pending:
                visit(self.device[offset], band)
            pending = arrived
        for offset, band in pending:
            visit(self.device[offset], band)

    def scatter(self, part):
        far = part(self.device[self.half]).astype(bf16)
        middle = far.shape[0] // 2
        first = self.up(far[:middle])
        second = self.down(far[middle:])
        near_up = part(self.device[self.half - 1])
        near_down = part(self.device[self.half + 1])
        going_up = jnp.concatenate(
            [near_up[:middle] + first.astype(f32), near_up[middle:]], axis=0
        ).astype(bf16)
        going_down = jnp.concatenate(
            [near_down[:middle], near_down[middle:] + second.astype(f32)], axis=0
        ).astype(bf16)
        for step in range(self.half - 2, -1, -1):
            going_up = self.up(going_up)
            going_down = self.down(going_down)
            if step:
                going_up = (part(self.device[step]) + going_up.astype(f32)).astype(bf16)
                going_down = (
                    part(self.device[self.nodes - step]) + going_down.astype(f32)
                ).astype(bf16)
        own = part(self.device[0])
        return own + (going_up.astype(f32) + going_down.astype(f32))


def three_terms(value):
    high = lax.reduce_precision(value, 8, 7)
    rest = value - high
    middle = lax.reduce_precision(rest, 8, 7)
    return [term.astype(bf16) for term in (high, middle, rest - middle)]


def to_bands(value, nodes):
    return value.reshape(value.shape[:-1] + (nodes, value.shape[-1] // nodes))


def plain_body(features, blocks, pair_labels, ffn_gain, final_gain, score_head, w_gate, w_up, w_down):
    nodes = lax.axis_size("fsdp")
    position = lax.axis_index("fsdp")
    member = lax.axis_index("member")
    swap = [(0, 1), (1, 0)]
    ring = Ring(nodes, position)
    owned, block_len, width = features.shape
    columns = width // nodes
    half_rows = block_len // 2
    half_columns = columns // 2
    ids = blocks[0]
    entries = ids.shape[0]
    rows = entries * block_len
    w_gate = w_gate[0]
    w_up = w_up[0]
    w_down = w_down[0]
    hidden_count = w_gate.shape[1]
    w_gate_bands = w_gate.reshape(nodes, columns, hidden_count)
    w_up_bands = w_up.reshape(nodes, columns, hidden_count)

    def share(vector, device):
        return lax.dynamic_slice_in_dim(vector, device * columns, columns, 0)

    def down_band(device):
        return lax.dynamic_slice_in_dim(w_down, device * columns, columns, 1)

    other_ids = lax.ppermute(ids, "member", swap)
    sent_rows = lax.dynamic_slice_in_dim(features, member * half_rows, half_rows, 1)
    outgoing = jnp.transpose(to_bands(sent_rows, nodes), (2, 0, 1, 3))
    arrived = lax.all_to_all(outgoing, "fsdp", split_axis=0, concat_axis=0, tiled=True)
    near_half = arrived.reshape(nodes * owned, half_rows, columns)
    far_half = lax.ppermute(near_half, "member", swap)
    picked = jnp.zeros((entries, 2, half_rows, columns), bf16)
    picked = lax.dynamic_update_slice_in_dim(
        picked, jnp.take(near_half, ids, axis=0)[:, None], member, 1
    )
    picked = lax.dynamic_update_slice_in_dim(
        picked, jnp.take(far_half, ids, axis=0)[:, None], 1 - member, 1
    )
    band = picked.reshape(rows, columns)

    stored = features.astype(f32)
    inverse_own = lax.rsqrt(jnp.mean(stored * stored, axis=2) + eps)
    inverse_all = lax.all_gather(inverse_own, "fsdp", axis=0, tiled=True)
    inverse_in = jnp.take(inverse_all, ids, axis=0).reshape(rows, 1)

    gain = ffn_gain[0]
    gain_head = final_gain[0] * score_head[0]
    head_parts = jnp.stack(three_terms(gain_head))
    head_down = jnp.sum(contract(head_parts, w_down, 1, 1), axis=0)

    state = {"gate": None, "up": None, "scaled": jnp.zeros((nodes, rows, columns), bf16)}

    def add(total, value):
        return value if total is None else total + value

    def forward(device, arrived_band):
        scaled = (
            arrived_band.astype(f32) * inverse_in * share(gain, device)[None, :]
        ).astype(bf16)
        gate_band = lax.dynamic_index_in_dim(w_gate_bands, device, 0, keepdims=False)
        up_band = lax.dynamic_index_in_dim(w_up_bands, device, 0, keepdims=False)
        state["gate"] = add(state["gate"], contract(scaled, gate_band, 1, 0))
        state["up"] = add(state["up"], contract(scaled, up_band, 1, 0))
        state["scaled"] = lax.dynamic_update_index_in_dim(state["scaled"], scaled, device, 0)

    ring.gather(band, forward)
    gate_pre = state["gate"]
    up_pre = state["up"]
    sigmoid_gate = jax.nn.sigmoid(gate_pre)
    silu_gate = gate_pre * sigmoid_gate
    hidden = (silu_gate * up_pre).astype(bf16)
    inputs_band = band.astype(f32)
    score_part = jnp.sum(hidden.astype(f32) * head_down[None, :], axis=1) + jnp.sum(
        inputs_band * share(gain_head, position)[None, :], axis=1
    )
    score_parts = lax.all_gather(
        score_part.reshape(1, entries, block_len), "fsdp", axis=0, tiled=True
    )

    out_band = ring.scatter(lambda device: contract(hidden, down_band(device), 1, 0))
    summed_band = inputs_band + out_band

    state2 = {"back": None, "square": None, "summed": jnp.zeros((nodes, rows, columns), bf16)}

    def backward(device, arrived_band):
        wide = arrived_band.astype(f32)
        state2["back"] = add(state2["back"], contract(arrived_band, down_band(device), 1, 1))
        state2["square"] = add(state2["square"], jnp.sum(wide * wide, axis=1))
        state2["summed"] = lax.dynamic_update_index_in_dim(
            state2["summed"], arrived_band, device, 0
        )

    ring.gather(summed_band.astype(bf16), backward)
    inverse_out = lax.rsqrt(state2["square"] / width + eps)
    scores = inverse_out * jnp.sum(score_parts, axis=0).reshape(rows)
    total_loss, dscore = pair_terms(scores, pair_labels[0], entries, block_len)
    head_scale = inverse_out * dscore
    summed_scale = inverse_out * inverse_out * dscore * scores / width
    dhidden = head_scale[:, None] * head_down[None, :] - summed_scale[:, None] * state2["back"]
    grad_gate_pre = (
        dhidden * up_pre * sigmoid_gate * (1.0 + gate_pre * (1.0 - sigmoid_gate))
    ).astype(bf16)
    grad_up_pre = (dhidden * silu_gate).astype(bf16)
    inner_part = jnp.sum(
        grad_gate_pre.astype(f32) * gate_pre + grad_up_pre.astype(f32) * up_pre, axis=1
    )
    inner_parts = lax.all_gather(
        inner_part.reshape(1, entries, block_len), "fsdp", axis=0, tiled=True
    )

    def scaled_part(device):
        gate_band = lax.dynamic_index_in_dim(w_gate_bands, device, 0, keepdims=False)
        up_band = lax.dynamic_index_in_dim(w_up_bands, device, 0, keepdims=False)
        return contract(grad_gate_pre, gate_band, 1, 1) + contract(grad_up_pre, up_band, 1, 1)

    dscaled_band = ring.scatter(scaled_part)

    scaled_in = jnp.transpose(state["scaled"], (1, 0, 2)).reshape(rows, width)
    summed = jnp.transpose(state2["summed"], (1, 0, 2)).reshape(rows, width)
    dsummed_b = (
        head_scale[:, None] * gain_head[None, :] - summed_scale[:, None] * summed.astype(f32)
    ).astype(bf16)
    grad_gate = contract(scaled_in, grad_gate_pre, 0, 0).astype(bf16)
    grad_up = contract(scaled_in, grad_up_pre, 0, 0).astype(bf16)
    grad_down = contract(hidden, dsummed_b, 0, 0).astype(bf16)

    weighted = jnp.sum(head_scale[:, None] * summed_band, axis=0)
    grad_head = share(final_gain[0], position) * weighted
    grad_final = share(score_head[0], position) * weighted
    dsummed_band = (
        head_scale[:, None] * share(gain_head, position)[None, :]
        - summed_scale[:, None] * summed_band
    )

    normed_in_band = inputs_band * inverse_in
    grad_ffn = jnp.sum(dscaled_band * normed_in_band, axis=0)
    row_inner = jnp.sum(inner_parts, axis=0).reshape(rows, 1)
    drows = (
        inverse_in
        * (dscaled_band * share(gain, position)[None, :] - normed_in_band * (row_inner / width))
        + dsummed_band
    ).astype(bf16)

    kept = lax.dynamic_slice_in_dim(drows, member * half_columns, half_columns, 1)
    given = lax.dynamic_slice_in_dim(drows, (1 - member) * half_columns, half_columns, 1)
    taken = lax.ppermute(given, "member", swap)

    def by_block(listed, value):
        hit = listed[None, :] == jnp.arange(nodes * owned, dtype=jnp.int32)[:, None]
        value = value.reshape(entries, block_len, half_columns).astype(f32)
        total = sum(
            jnp.where(hit[:, entry, None, None], value[entry][None], 0.0)
            for entry in range(entries)
        )
        return total.astype(bf16).astype(f32)

    returned = (by_block(ids, kept) + by_block(other_ids, taken)).astype(bf16)
    returned = returned.reshape(nodes, owned, block_len, half_columns)
    mine = lax.all_to_all(returned, "fsdp", split_axis=0, concat_axis=0, tiled=True)
    other = lax.ppermute(mine, "member", swap)
    whole = jnp.zeros((2, nodes, owned, block_len, half_columns), bf16)
    whole = lax.dynamic_update_index_in_dim(whole, mine, member, 0)
    whole = lax.dynamic_update_index_in_dim(whole, other, 1 - member, 0)
    grad_features = jnp.transpose(whole, (2, 3, 1, 0, 4)).reshape(owned, block_len, width)
    return (
        total_loss.reshape(1),
        grad_gate[None],
        grad_up[None],
        grad_down[None],
        grad_head[None],
        grad_final[None],
        grad_ffn[None],
        grad_features,
    )


AUX = 16
STRIPE = 32
IN_SMEM = pl.BlockSpec(memory_space=pltpu.SMEM)
IN_VMEM = pl.BlockSpec(memory_space=pltpu.VMEM)
IN_HBM = pl.BlockSpec(memory_space=pltpu.HBM)


def dot(left, right, left_dim, right_dim):
    return contract(left, right, left_dim, right_dim)


def call(kernel, operands, specs, outs, scratch=(), limit=8, aliases=None):
    operands = [
        pltpu.with_memory_space_constraint(value, pltpu.HBM) if spec is IN_HBM else value
        for value, spec in zip(operands, specs)
    ]
    return pl.pallas_call(
        kernel,
        out_shape=[jax.ShapeDtypeStruct(shape, dtype) for shape, dtype in outs],
        in_specs=specs,
        scratch_shapes=list(scratch),
        input_output_aliases=aliases or {},
        compiler_params=pltpu.CompilerParams(vmem_limit_bytes=limit << 20),
    )(*operands)


def band_number(row_ref, offsets, k):
    if len(offsets) == 1:
        return row_ref[offsets[0]]
    return row_ref[offsets[0] + k * (offsets[1] - offsets[0])]


def stream(count, sources, weights, done, use):
    ways = len(sources)

    def copy(k, w):
        slot = k * ways + w
        return pltpu.make_async_copy(sources[w](k), weights.at[slot], done.at[slot])

    for w in range(ways):
        copy(0, w).start()

    def step(k):
        for w in range(ways):
            copy(k, w).wait()
            if isinstance(k, int):
                if k + 1 < count:
                    copy(k + 1, w).start()
            else:

                @pl.when(k + 1 < count)
                def _():
                    copy(k + 1, w).start()

            use(k, w, weights.at[k * ways + w])

    if count == 1:
        return lambda: step(0)

    def run():
        def body(k, _):
            step(k)
            return 0

        lax.fori_loop(0, count, body, 0)

    return run


def rows_as_lanes(vectors):
    rows = vectors[0].shape[0]
    lane = lax.broadcasted_iota(jnp.int32, (rows, 128), 1)
    packed = jnp.zeros((rows, 128), f32)
    for k, vector in enumerate(vectors):
        packed = jnp.where(lane == k, vector, packed)
    return packed.T[:8]


def lanes_as_columns(vectors):
    rows = vectors[0].shape[1]
    line = lax.broadcasted_iota(jnp.int32, (128, rows), 0)
    packed = jnp.zeros((128, rows), f32)
    for k, vector in enumerate(vectors):
        packed = jnp.where(line == k, vector, packed)
    return packed.T


def split_terms(lanes):
    high = lanes.astype(bf16).astype(f32)
    rest = lanes - high
    middle = rest.astype(bf16).astype(f32)
    low = rest - middle
    top = jnp.concatenate([high, middle], axis=1)
    bottom = jnp.concatenate([low, jnp.zeros_like(low)], axis=1)
    return jnp.concatenate([top, bottom], axis=0).astype(bf16)


def joined_term(terms, k):
    half = terms.shape[1] // 2
    return terms[k : k + 1, :half] + terms[k : k + 1, half:] + terms[8 + k : 9 + k, :half]


def pieces_of(band):
    return band if isinstance(band, tuple) else (band,)


def pack_blocks(member, block, nodes):
    block_len, width = block.shape
    columns = width // nodes
    half = columns // 2

    def kernel(member_ref, block_ref, out):
        square = jnp.zeros((block_len, 1), f32)
        for d in range(nodes):
            part = block_ref[:, d * columns : (d + 1) * columns].astype(f32)
            square += jnp.sum(part * part, axis=1, keepdims=True)
        terms = split_terms(rows_as_lanes([lax.rsqrt(square / width + eps)]))
        for d in range(nodes):
            start = pl.multiple_of(d * columns + member_ref[0] * half, half)
            out[d, :block_len] = block_ref[:, pl.ds(start, half)]
            out[d, block_len:] = terms

    return call(
        kernel, [member, block], [IN_SMEM, IN_VMEM], [((nodes, block_len + AUX, half), bf16)]
    )[0]


def pick_blocks(ids, member, near, far):
    entries = ids.shape[0]
    block_len = near.shape[1] - AUX
    half = near.shape[2]

    def kernel(ids_ref, member_ref, near_ref, far_ref, band_out, inverse_out):
        first = member_ref[0] == 0
        for e in range(entries):
            mine, other = near_ref[ids_ref[e]], far_ref[ids_ref[e]]
            part = slice(e * block_len, (e + 1) * block_len)
            band_out[part, :half] = jnp.where(first, mine, other)[:block_len]
            band_out[part, half:] = jnp.where(first, other, mine)[:block_len]
            row = joined_term(mine[block_len:].astype(f32), 0)
            inverse_out[part] = lanes_as_columns([row])[:, 0:1]

    return call(
        kernel, [ids, member, near, far], [IN_SMEM, IN_SMEM, IN_VMEM, IN_VMEM],
        [((entries * block_len, 2 * half), bf16), ((entries * block_len, 1), f32)],
    )


def split_halves(back, ahead, middle):
    def kernel(back_ref, ahead_ref, first, second):
        first[...] = back_ref[:middle]
        second[...] = ahead_ref[middle:]

    columns = back.shape[1]
    return call(
        kernel, [back, ahead], [IN_VMEM] * 2,
        [((middle, columns), bf16), ((ahead.shape[0] - middle, columns), bf16)],
    )


def forward_bands(bands, row, offsets, gain_bands, inverse, gate_bands, up_bands, totals, head):
    bands = [pieces_of(band) for band in bands]
    flat = [piece for band in bands for piece in band]
    count = len(bands)
    rows, columns = inverse.shape[0], flat[0].shape[1]
    width = gate_bands.shape[2]
    last = head is not None

    def kernel(row_ref, *refs):
        refs = list(refs)
        take = lambda k: [refs.pop(0) for _ in range(k)]
        band_refs = [take(len(band)) for band in bands]
        gain_ref, inverse_ref, gate_hbm, up_hbm = take(4)
        if totals:
            take(2)
        head_ref = take(1)[0] if last else None
        totals_out = take(2)
        (scaled_out,) = take(1)
        hidden_out, score_out = take(2) if last else (None, None)
        weights, done = refs

        def use(k, w, block):
            totals_out[w][...] += dot(scaled_out[k], block[...], 1, 0)

        run = stream(
            count,
            [
                lambda k: gate_hbm.at[band_number(row_ref, offsets, k)],
                lambda k: up_hbm.at[band_number(row_ref, offsets, k)],
            ],
            weights, done, use,
        )
        for k in range(count):
            start = 0
            for ref in band_refs[k]:
                part = slice(start, start + ref.shape[0])
                scaled_out[k, part] = (
                    ref[...].astype(f32) * inverse_ref[part] * gain_ref[row_ref[offsets[k]]]
                ).astype(bf16)
                start += ref.shape[0]
        if not totals:
            for out in totals_out:
                out[...] = jnp.zeros_like(out)
        run()
        if last:
            gate_out, up_out = totals_out

            def finish(i, _):
                part = pl.ds(i * STRIPE, STRIPE)
                gate = gate_out[part]
                hidden = (gate * jax.nn.sigmoid(gate) * up_out[part]).astype(bf16)
                hidden_out[part] = hidden
                score_out[part] = jnp.sum(
                    hidden.astype(f32) * head_ref[...], axis=1, keepdims=True
                )
                return 0

            lax.fori_loop(0, rows // STRIPE, finish, 0)

    operands = [row] + flat + [gain_bands, inverse, gate_bands, up_bands]
    specs = [IN_SMEM] + [IN_VMEM] * (len(flat) + 2) + [IN_HBM, IN_HBM]
    aliases = {}
    if totals:
        aliases = {len(operands): 0, len(operands) + 1: 1}
        operands += list(totals)
        specs += [IN_VMEM] * 2
    if last:
        operands.append(head)
        specs.append(IN_VMEM)
    outs = [((rows, width), f32)] * 2 + [((count, rows, columns), bf16)]
    if last:
        outs += [((rows, width), bf16), ((rows, 1), f32)]
    scratch = [
        pltpu.VMEM((2 * count, columns, width), bf16), pltpu.SemaphoreType.DMA((2 * count,))
    ]
    out = call(kernel, operands, specs, outs, scratch, 8 + 4 * count, aliases)
    return out[:2], out[2], out[3:]


def pair_scales(notes, labels_ref, rows, entries, width):
    square, score = joined_term(notes, 0), joined_term(notes, 1)
    inverse_out = lax.rsqrt(square / width + eps)
    scores = inverse_out * score
    block_len = rows // entries
    rewards = [
        jnp.sum(scores[:, e * block_len : (e + 1) * block_len], axis=1, keepdims=True) / block_len
        for e in range(entries)
    ]
    drewards = [jnp.zeros((1, 1), f32) for _ in range(entries)]
    loss = jnp.zeros((1, 1), f32)
    for p in range(labels_ref.shape[0]):
        select = [
            (labels_ref[p, 0] == e).astype(f32) - (labels_ref[p, 1] == e).astype(f32)
            for e in range(entries)
        ]
        margin = sum(select[e] * rewards[e] for e in range(entries))
        loss += jnp.maximum(-margin, 0.0) + jnp.log1p(jnp.exp(-jnp.abs(margin)))
        weight = -jax.nn.sigmoid(-margin) * loss_scale
        drewards = [drewards[e] + select[e] * weight for e in range(entries)]
    lane = lax.broadcasted_iota(jnp.int32, (1, rows), 1)
    dscore = jnp.zeros((1, rows), f32)
    for e in range(entries):
        dscore = jnp.where(lane // block_len == e, drewards[e] / block_len, dscore)
    head_scale = inverse_out * dscore
    columns = lanes_as_columns([head_scale, inverse_out * head_scale * scores / width])
    return loss, columns[:, 0:1], columns[:, 1:2]


def backward_bands(bands, row, offsets, w_down, rows, total, final):
    bands = [pieces_of(band) for band in bands]
    flat = [piece for band in bands for piece in band]
    count = len(bands)
    columns = flat[0].shape[1]
    width, model_width = w_down.shape
    others = final[4] if final else []

    def kernel(row_ref, *refs):
        refs = list(refs)
        take = lambda k: [refs.pop(0) for _ in range(k)]
        band_refs = [take(len(band)) for band in bands]
        (down_hbm,) = take(1)
        if total is not None:
            take(1)
        if final:
            gate_ref, up_ref, head_ref, labels_ref = take(4)
            other_refs = take(len(others))
        (back_ref,) = take(1)
        if final:
            grads_out, inner_out, loss_out, head_scale, summed_scale = take(5)
        weights, done, kept = take(3)

        def use(k, w, block):
            back_ref[...] += dot(kept[k], block[...], 1, 1)

        def source(k):
            start = pl.multiple_of(band_number(row_ref, offsets, k) * columns, columns)
            return down_hbm.at[:, pl.ds(start, columns)]

        run = stream(count, [source], weights, done, use)
        for k in range(count):
            start = 0
            for ref in band_refs[k]:
                size = min(ref.shape[0], rows - start)
                kept[k, start : start + size] = ref[:size]
                start += size
        if total is None:
            back_ref[...] = jnp.zeros_like(back_ref)
        if final:
            tail = band_refs[-1][-1]
            notes = tail[tail.shape[0] - AUX :].astype(f32)
            for ref in other_refs:
                notes += ref[rows:].astype(f32)
            loss, head_column, summed_column = pair_scales(
                notes, labels_ref, rows, final[5], model_width
            )
            loss_out[...] = loss
            head_scale[...] = head_column
            summed_scale[...] = summed_column
        run()
        if not final:
            return
        (inner,) = refs

        def finish(i, _):
            part = pl.ds(i * STRIPE, STRIPE)
            gate, up = gate_ref[part], up_ref[part]
            sigmoid = jax.nn.sigmoid(gate)
            dhidden = head_scale[part] * head_ref[...] - summed_scale[part] * back_ref[part]
            dgate = (dhidden * up * sigmoid * (1.0 + gate * (1.0 - sigmoid))).astype(bf16)
            dup = (dhidden * (gate * sigmoid)).astype(bf16)
            grads_out[0, part] = dgate
            grads_out[1, part] = dup
            inner[part] = jnp.sum(
                dgate.astype(f32) * gate + dup.astype(f32) * up, axis=1, keepdims=True
            )
            return 0

        lax.fori_loop(0, rows // STRIPE, finish, 0)
        inner_out[...] = rows_as_lanes([inner[...]])

    operands = [row] + flat + [w_down]
    specs = [IN_SMEM] + [IN_VMEM] * len(flat) + [IN_HBM]
    aliases = {}
    if total is not None:
        aliases = {len(operands): 0}
        operands.append(total)
        specs.append(IN_VMEM)
    scratch = [
        pltpu.VMEM((count, width, columns), bf16), pltpu.SemaphoreType.DMA((count,)),
        pltpu.VMEM((count, rows, columns), bf16),
    ]
    outs = [((rows, width), f32)]
    if final:
        operands += list(final[:4]) + list(others)
        specs += [IN_VMEM] * 3 + [IN_SMEM] + [IN_VMEM] * len(others)
        outs += [
            ((2, rows, width), bf16), ((8, rows), f32), ((1, 1), f32), ((rows, 1), f32),
            ((rows, 1), f32),
        ]
        scratch += [pltpu.VMEM((rows, 1), f32)]
    return call(kernel, operands, specs, outs, scratch, 8 + 3 * count, aliases)


def out_parts(row, offsets, hidden, w_down, columns):
    count = len(offsets)
    rows, width = hidden.shape

    def kernel(row_ref, hidden_ref, down_hbm, out, weights, done):
        def use(k, w, block):
            out[k] = dot(hidden_ref[...], block[...], 1, 0)

        def source(k):
            start = pl.multiple_of(band_number(row_ref, offsets, k) * columns, columns)
            return down_hbm.at[:, pl.ds(start, columns)]

        stream(count, [source], weights, done, use)()

    return call(
        kernel, [row, hidden, w_down], [IN_SMEM, IN_VMEM, IN_HBM],
        [((count, rows, columns), f32)],
        [pltpu.VMEM((count, width, columns), bf16), pltpu.SemaphoreType.DMA((count,))],
        4 + 3 * count,
    )[0]


def scaled_parts(row, offsets, grads, gate_bands, up_bands):
    count = len(offsets)
    rows, width = grads.shape[1:]
    columns = gate_bands.shape[1]

    def kernel(row_ref, grads_ref, gate_hbm, up_hbm, out, weights, done):
        def use(k, w, block):
            term = dot(grads_ref[w], block[...], 1, 1)
            if w:
                out[k] += term
            else:
                out[k] = term

        stream(
            count,
            [
                lambda k: gate_hbm.at[band_number(row_ref, offsets, k)],
                lambda k: up_hbm.at[band_number(row_ref, offsets, k)],
            ],
            weights, done, use,
        )()

    return call(
        kernel, [row, grads, gate_bands, up_bands], [IN_SMEM, IN_VMEM, IN_HBM, IN_HBM],
        [((count, rows, columns), f32)],
        [pltpu.VMEM((2 * count, columns, width), bf16), pltpu.SemaphoreType.DMA((2 * count,))],
        4 + 5 * count,
    )[0]


def high_low(row):
    high = row.astype(bf16).astype(f32)
    return jnp.concatenate([high, row - high], axis=1)


def add_arrivals(parts, from_back, from_ahead, inner):
    rows, columns = parts.shape[1:]
    middle = rows // 2
    tail = 0 if inner is None else AUX
    early = from_back.shape[0] < rows

    def kernel(*refs):
        parts_ref, back_ref, ahead_ref = refs[:3]
        out_up, out_down = refs[-2:]
        if early:
            out_up[:middle] = (parts_ref[0, :middle] + back_ref[:middle].astype(f32)).astype(bf16)
            out_up[middle:rows] = parts_ref[0, middle:].astype(bf16)
            out_down[:middle] = parts_ref[1, :middle].astype(bf16)
            out_down[middle:rows] = (
                parts_ref[1, middle:] + ahead_ref[:middle].astype(f32)
            ).astype(bf16)
        else:
            out_up[:rows] = (parts_ref[0] + back_ref[:rows].astype(f32)).astype(bf16)
            out_down[:rows] = (parts_ref[1] + ahead_ref[:rows].astype(f32)).astype(bf16)
        if tail:
            row = refs[3][...]
            base = middle if early else rows
            pad = jnp.zeros((AUX - 8, columns), f32)

            def carry(ref):
                came = ref[base:].astype(f32)[:8]
                return row + came[:, : columns // 2] + came[:, columns // 2 :]

            up_row = carry(back_ref)
            down_row = row if early else carry(ahead_ref)
            out_up[rows:] = jnp.concatenate([high_low(up_row), pad], axis=0).astype(bf16)
            out_down[rows:] = jnp.concatenate([high_low(down_row), pad], axis=0).astype(bf16)

    operands = [parts, from_back, from_ahead] + ([] if inner is None else [inner])
    return call(
        kernel, operands, [IN_VMEM] * len(operands), [((rows + tail, columns), bf16)] * 2
    )


def first_messages(far, inner):
    rows, columns = far.shape[1:]
    middle = rows // 2
    tail = 0 if inner is None else AUX

    def kernel(far_ref, *refs):
        up_out, down_out = refs[-2:]
        up_out[:middle] = far_ref[0, :middle].astype(bf16)
        down_out[...] = far_ref[0, middle:].astype(bf16)
        if tail:
            pad = jnp.zeros((AUX - 8, columns), f32)
            up_out[middle:] = jnp.concatenate([high_low(refs[0][...]), pad], axis=0).astype(bf16)

    operands = [far] + ([] if inner is None else [inner])
    return call(
        kernel, operands, [IN_VMEM] * len(operands),
        [((middle + tail, columns), bf16), ((middle, columns), bf16)],
    )


def finish_summed(own, from_back, from_ahead, band, head_row, score):
    rows, columns = own.shape[1:]

    def kernel(own_ref, back_ref, ahead_ref, band_ref, head_ref, score_ref, summed_out, message):
        inputs = band_ref[...].astype(f32)
        summed = inputs + (
            own_ref[0] + (back_ref[...].astype(f32) + ahead_ref[...].astype(f32))
        )
        summed_out[...] = summed
        message[:rows] = summed.astype(bf16)
        square = jnp.sum(summed * summed, axis=1, keepdims=True)
        share = score_ref[...] + jnp.sum(inputs * head_ref[...], axis=1, keepdims=True)
        message[rows:] = split_terms(rows_as_lanes([square, share]))

    return call(
        kernel, [own, from_back, from_ahead, band, head_row, score], [IN_VMEM] * 6,
        [((rows, columns), f32), ((rows + AUX, columns), bf16)],
    )


def finish_rows(member, own, from_back, from_ahead, inner, band, summed, inverse, gain_row,
                head_row, head_scale, summed_scale, final_row, score_row, entries, width):
    rows, columns = own.shape[1:]
    block_len = rows // entries
    half = block_len // 2

    def kernel(member_ref, own_ref, back_ref, ahead_ref, inner_ref, band_ref, summed_ref,
               inverse_ref, gain_ref, head_ref, head_scale_ref, summed_scale_ref, final_ref,
               score_ref, kept_out, given_out, ffn_out, head_out, final_out, drows):
        dscaled = own_ref[0] + (back_ref[:rows].astype(f32) + ahead_ref[:rows].astype(f32))
        came = (back_ref[rows:].astype(f32) + ahead_ref[rows:].astype(f32))[:8]
        lanes = inner_ref[...] + came[:, : columns // 2] + came[:, columns // 2 :]
        inner_column = lanes_as_columns([lanes[0:1]])[:, 0:1]
        inverse_in = inverse_ref[...]
        normed = band_ref[...].astype(f32) * inverse_in
        ffn_out[...] = jnp.sum(dscaled * normed, axis=0, keepdims=True)
        summed = summed_ref[...]
        weighted = jnp.sum(head_scale_ref[...] * summed, axis=0, keepdims=True)
        head_out[...] = final_ref[...] * weighted
        final_out[...] = score_ref[...] * weighted
        dsummed = head_scale_ref[...] * head_ref[...] - summed_scale_ref[...] * summed
        drows[...] = (
            inverse_in * (dscaled * gain_ref[...] - normed * (inner_column / width)) + dsummed
        ).astype(bf16)
        for e in range(entries):
            for out, which in ((kept_out, member_ref[0]), (given_out, 1 - member_ref[0])):
                start = pl.multiple_of(e * block_len + which * half, half)
                out[e] = drows[pl.ds(start, half)]

    return call(
        kernel,
        [member, own, from_back, from_ahead, inner, band, summed, inverse, gain_row, head_row,
         head_scale, summed_scale, final_row, score_row],
        [IN_SMEM] + [IN_VMEM] * 13,
        [((entries, half, columns), bf16)] * 2 + [((1, columns), f32)] * 3,
        [pltpu.VMEM((rows, columns), bf16)],
    )


def route_rows(ids, other_ids, kept, taken, blocks):
    entries, half, columns = kept.shape

    def kernel(ids_ref, other_ref, kept_ref, taken_ref, out):
        for b in range(blocks):
            sums = []
            for listed, value in ((ids_ref, kept_ref), (other_ref, taken_ref)):
                total = jnp.zeros((half, columns), f32)
                for e in range(entries):
                    total += jnp.where(listed[e] == b, value[e].astype(f32), 0.0)
                sums.append(total.astype(bf16).astype(f32))
            out[b] = (sums[0] + sums[1]).astype(bf16)

    return call(
        kernel, [ids, other_ids, kept, taken], [IN_SMEM, IN_SMEM, IN_VMEM, IN_VMEM],
        [((blocks, half, columns), bf16)],
    )[0]


def assemble_block(member, mine, other):
    nodes, half, columns = mine.shape

    def kernel(member_ref, mine_ref, other_ref, out):
        for value, which in ((mine_ref, member_ref[0]), (other_ref, 1 - member_ref[0])):
            part = pl.ds(pl.multiple_of(which * half, half), half)
            for d in range(nodes):
                out[part, d * columns : (d + 1) * columns] = value[d]

    return call(
        kernel, [member, mine, other], [IN_SMEM, IN_VMEM, IN_VMEM],
        [((2 * half, nodes * columns), bf16)],
    )[0]


def turned(value):
    def kernel(value_ref, out):
        out[...] = value_ref[...].T

    return call(kernel, [value], [IN_VMEM], [(value.shape[::-1], value.dtype)])[0]


def whole(*shape):
    zeros = (0,) * len(shape)
    return pl.BlockSpec(shape, lambda *_: zeros)


def grid_call(kernel, index, operands, specs, outs, out_specs, steps, scratch, aliases=None):
    return pl.pallas_call(
        kernel,
        out_shape=[jax.ShapeDtypeStruct(shape, dtype) for shape, dtype in outs],
        grid_spec=pltpu.PrefetchScalarGridSpec(
            num_scalar_prefetch=1, grid=(steps,), in_specs=specs, out_specs=out_specs,
            scratch_shapes=list(scratch),
        ),
        input_output_aliases=aliases or {},
        compiler_params=pltpu.CompilerParams(vmem_limit_bytes=20 << 20),
    )(index, *operands)


def weight_grads(index, stacks, grads):
    nodes = sum(stack.shape[0] for stack in stacks)
    _, rows, columns = stacks[0].shape
    width = grads.shape[2]

    def kernel(index_ref, *refs):
        grads_ref, gate_out, up_out, kept = refs[len(stacks) :]

        @pl.when(pl.program_id(0) == 0)
        def _():
            start = 0
            for ref in refs[: len(stacks)]:
                kept[start : start + ref.shape[0]] = ref[...]
                start += ref.shape[0]

        scaled = kept[pl.program_id(0)].T
        gate_out[0] = dot(scaled, grads_ref[0], 1, 0).astype(bf16)
        up_out[0] = dot(scaled, grads_ref[1], 1, 0).astype(bf16)

    out = pl.BlockSpec((1, columns, width), lambda b, idx: (idx[b], 0, 0))
    return grid_call(
        kernel, index, list(stacks) + [grads], [IN_VMEM] * (len(stacks) + 1),
        [((nodes, columns, width), bf16)] * 2, [out, out], nodes,
        [pltpu.VMEM((nodes, rows, columns), bf16)],
    )


def down_grad(index, start, bands, hidden_t, head_bands, head_scale, summed_scale, before):
    flat = [piece for band in bands for piece in pieces_of(band)]
    columns = flat[0].shape[1]
    width, rows = hidden_t.shape
    nodes = head_bands.shape[0]

    def kernel(index_ref, *refs):
        hidden_ref, head_ref, head_scale_ref, summed_scale_ref = refs[len(flat) : len(flat) + 4]
        out, kept = refs[-2:]

        @pl.when(pl.program_id(0) == 0)
        def _():
            at = 0
            for k, band in enumerate(bands):
                line = 0
                for _ in pieces_of(band):
                    size = min(refs[at].shape[0], rows - line)
                    kept[k, line : line + size] = refs[at][:size]
                    line += size
                    at += 1

        step = pl.program_id(0)
        dsummed = (
            head_scale_ref[...] * head_ref[index_ref[start + step]]
            - summed_scale_ref[...] * kept[step].astype(f32)
        )
        out[...] = dot(hidden_ref[...], dsummed.astype(bf16), 1, 0).astype(bf16)

    operands = flat + [hidden_t, head_bands, head_scale, summed_scale]
    specs = [IN_VMEM] * len(operands)
    aliases = None
    if before is not None:
        aliases = {len(operands) + 1: 0}
        operands.append(before)
        specs.append(pl.BlockSpec(memory_space=pl.ANY))
    return grid_call(
        kernel, index, operands, specs, [((width, nodes * columns), bf16)],
        [pl.BlockSpec((width, columns), lambda b, idx: (0, idx[start + b]))], len(bands),
        [pltpu.VMEM((len(bands), rows, columns), bf16)], aliases,
    )[0]


def after(values, *others):
    return lax.optimization_barrier(tuple(values) + tuple(others))[: len(values)]


def ring_body(features, blocks, pair_labels, ffn_gain, final_gain, score_head, w_gate, w_up, w_down):
    nodes = lax.axis_size("fsdp")
    position = lax.axis_index("fsdp")
    member = lax.axis_index("member").reshape(1)
    swap = [(0, 1), (1, 0)]
    ring = Ring(nodes, position)
    half = ring.half
    block_len, width = features.shape[1:]
    columns = width // nodes
    ids = blocks[0]
    entries = ids.shape[0]
    rows = entries * block_len
    middle = rows // 2
    w_gate = w_gate[0]
    w_up = w_up[0]
    w_down = w_down[0]
    hidden_count = w_gate.shape[1]
    gate_bands = w_gate.reshape(nodes, columns, hidden_count)
    up_bands = w_up.reshape(nodes, columns, hidden_count)
    gain_head = final_gain[0] * score_head[0]
    gain_bands = ffn_gain.reshape(nodes, 1, columns)
    head_bands = gain_head.reshape(nodes, 1, columns)

    def share(vector):
        return lax.dynamic_slice_in_dim(vector, position * columns, columns, 0)[None]

    other_ids = lax.ppermute(ids, "member", swap)
    sent = pack_blocks(member, features[0], nodes)
    near = lax.all_to_all(sent, "fsdp", split_axis=0, concat_axis=0, tiled=True)
    head_parts = jnp.stack(three_terms(gain_head))
    head_down = jnp.sum(contract(head_parts, w_down, 1, 1), axis=0)[None]
    (near,) = after([near], head_down)
    far = lax.ppermute(near, "member", swap)
    band, inverse_in = pick_blocks(ids, member, near, far)

    def gather(own, visit, extra=None):
        back = ahead = own
        total = None
        pending, pending_offsets = [own], [0]
        order = []
        for step in range(1, half + 1):
            if step < half:
                back, ahead = ring.up(back), ring.down(ahead)
                arrived, offsets = [back, ahead], [nodes - step, step]
            else:
                first, second = split_halves(back, ahead, middle)
                arrived, offsets = [(ring.up(first), ring.down(second))], [step]
            total = visit(pending, pending_offsets, total)
            order += pending_offsets
            if step < half:
                done = list(total)
                if step == 1 and extra is not None:
                    done.append(extra)
                back, ahead = after([back, ahead], *done)
                arrived = [back, ahead]
            pending, pending_offsets = arrived, offsets
        order += pending_offsets
        return pending, pending_offsets, total, order

    scaled = []

    def forward(bands, offsets, total, head=None):
        total, new, rest = forward_bands(
            bands, ring.row, offsets, gain_bands, inverse_in, gate_bands, up_bands, total, head
        )
        scaled.append(new)
        return total if head is None else (total, rest)

    last, last_offsets, total, offsets = gather(band, forward)
    order = ring.visited(offsets, position)
    (gate_pre, up_pre), (hidden, score) = forward(last, last_offsets, total, head_down)

    far_part = out_parts(ring.row, [half], hidden, w_down, columns)
    up_message, down_message = first_messages(far_part, None)
    (held,) = after([hidden], up_message)
    back, ahead = ring.up(up_message), ring.down(down_message)
    for step in range(half - 1, 0, -1):
        parts = out_parts(ring.row, [step, nodes - step], held, w_down, columns)
        (held,) = after([held], back, ahead)
        back, ahead = add_arrivals(parts, back, ahead, None)
        back, ahead = ring.up(back), ring.down(ahead)
    own_part = out_parts(ring.row, [0], held, w_down, columns)
    summed_band, message = finish_summed(
        own_part, back, ahead, band, share(gain_head), score
    )

    messages = []

    def backward(bands, offsets, total, final=None):
        messages.extend(bands)
        return backward_bands(
            bands, ring.row, offsets, w_down, rows, None if total is None else total[0], final
        )

    (held,) = after([hidden], message)
    hidden_t = turned(held)
    last, last_offsets, total, _ = gather(message, backward, hidden_t)
    _, grads, inner, loss, head_scale, summed_scale = backward(
        last, last_offsets, total,
        (gate_pre, up_pre, head_down, pair_labels[0], list(messages), entries),
    )

    far_part = scaled_parts(ring.row, [half], grads, gate_bands, up_bands)
    up_message, down_message = first_messages(far_part, inner)
    (held,) = after([grads], up_message)
    back, ahead = ring.up(up_message), ring.down(down_message)
    grad_down = None
    bounds = [0, 3, 6, nodes]

    def grad_down_piece(piece, held_t):
        start, stop = bounds[piece], bounds[piece + 1]
        return down_grad(
            order, start, messages[start:stop], held_t, head_bands, head_scale, summed_scale,
            grad_down,
        )

    for step in range(half - 1, 0, -1):
        parts = scaled_parts(ring.row, [step, nodes - step], held, gate_bands, up_bands)
        if step < half - 1:
            grad_down = grad_down_piece(half - 2 - step, hidden_t)
            back, ahead = after([back, ahead], grad_down)
        held, hidden_t = after([held, hidden_t], back, ahead)
        back, ahead = add_arrivals(parts, back, ahead, inner)
        back, ahead = ring.up(back), ring.down(ahead)
    own_part = scaled_parts(ring.row, [0], held, gate_bands, up_bands)
    grad_down = grad_down_piece(2, hidden_t)
    back, ahead = after([back, ahead], grad_down)
    kept, given, grad_ffn, grad_head, grad_final = finish_rows(
        member, own_part, back, ahead, inner, band, summed_band, inverse_in,
        share(ffn_gain[0]), share(gain_head), head_scale, summed_scale, share(final_gain[0]),
        share(score_head[0]), entries, width,
    )

    (held,) = after([grads], given)
    taken = lax.ppermute(given, "member", swap)
    returned = route_rows(ids, other_ids, kept, taken, nodes)
    mine = lax.all_to_all(returned, "fsdp", split_axis=0, concat_axis=0, tiled=True)
    grad_gate, grad_up = weight_grads(order, scaled, held)
    (mine,) = after([mine], grad_gate, grad_up)
    other = lax.ppermute(mine, "member", swap)
    grad_features = assemble_block(member, mine, other)
    return (
        loss.reshape(1),
        grad_gate.reshape(1, width, hidden_count),
        grad_up.reshape(1, width, hidden_count),
        grad_down[None],
        grad_head,
        grad_final,
        grad_ffn,
        grad_features[None],
    )


def body(features, blocks, pair_labels, ffn_gain, final_gain, score_head, w_gate, w_up, w_down):
    nodes = lax.axis_size("fsdp")
    rows = blocks.shape[1] * features.shape[1]
    columns = features.shape[2] // nodes
    tiled = w_gate.shape[2] % 256 == 0 and columns == 2 * rows and rows % 256 == 0
    single = features.shape[0] == 1 and lax.axis_size("member") == 2
    chosen = ring_body if tiled and single and nodes == 8 else plain_body
    return chosen(
        features, blocks, pair_labels, ffn_gain, final_gain, score_head, w_gate, w_up, w_down
    )


def solution(mesh):
    in_specs = (
        P(("groups", "fsdp"), None, None),
        P(("groups", "member"), None),
        P(("groups", "member"), None, None),
        P("member", None),
        P("member", None),
        P("member", None),
        P("member", None, "fsdp"),
        P("member", None, "fsdp"),
        P("member", "fsdp", None),
    )
    out_specs = (
        P(("groups", "member")),
        P(("groups", "member"), None, "fsdp"),
        P(("groups", "member"), None, "fsdp"),
        P(("groups", "member"), "fsdp", None),
        P(("groups", "member"), "fsdp"),
        P(("groups", "member"), "fsdp"),
        P(("groups", "member"), "fsdp"),
        P(("groups", "fsdp"), None, None),
    )
    return jax.shard_map(body, mesh=mesh, in_specs=in_specs, out_specs=out_specs, check_vma=False)
```

time: 580 us -> 219 us (0.38)
  waiting for transfers between devices: 318 us -> 30.2 us
  Pallas kernels: 0 us -> 119 us
  matrix products: 99 us -> 9.08 us
  blocking collectives: 75.4 us -> 0 us
  other arithmetic: 44.3 us -> 0.06 us
  starting transfers between devices: 4.15 us -> 44.4 us
  between operations: 14.5 us -> 1.3 us
  local copies, waits for them, and re-layouts: 21.3 us -> 13.2 us
    psum x2 -> x0, waiting for transfers between devices: 149 us -> none  [the longest x1 149 us: body(): out_total = lax.psum(out_part, 'fsdp')]
    pallas_call x0 -> x41, Pallas kernels: none -> 119 us  [the longest x37 93.9 us: call(): pl.pallas_call(kernel, out_shape=[jax.ShapeDtypeStruct(shape, dtype) for...]
    reduce_scatter x1 -> x0, waiting for transfers between devices: 87 us -> none  [body(): lax.psum_scatter(dscaled_part, 'fsdp', scatter_dimension=1, tiled=True)]
    dot_general x6 -> x1, matrix products: 71.8 us -> 9.08 us  [contract(): lax.dot_general(left, right, (((left_dim,), (right_dim,)), ((), ())), pre...]
    all_to_all x1 -> x0, blocking collectives: 55.3 us -> none  [body(): lax.all_to_all(outgoing[None], 'fsdp', split_axis=3, concat_axis=0, tiled...]
    all_gather x1 -> x0, waiting for transfers between devices: 48.3 us -> none  [body(): gathered = lax.all_gather(bands, 'fsdp', axis=2, tiled=True)]
    ppermute x0 -> x36, starting transfers between devices: none -> 33.6 us  [the longest x16 18.8 us: down(): return lax.ppermute(value, 'fsdp', self.back)]
    dot_general x4 -> x0, matrix products: 27.2 us -> none  [the longest x1 11.3 us: body(): up_pre = jnp.dot(scaled_in, w_up[0], preferred_element_type=jnp.float32)]
  transfers between devices with their start and end apart: 5 -> 38, of which waited for: 4 -> 19; matrix products, arithmetic and copies ran while one was open for 6% -> 5% of each run, Pallas kernels for 0% -> 43%
where the time goes in v1:
time: 219 us; the launch traced here: 218 us
  Pallas kernels  119 us (54%)
  starting transfers between devices  44.4 us (20%)
  waiting for transfers between devices  30.2 us (14%)
  local copies, waits for them, and re-layouts  13.2 us (6%)
  matrix products  9.08 us (4%)
    pallas_call x37, Pallas kernels, call(): pl.pallas_call(kernel, out_shape=[jax.ShapeDtypeStruct(shape, dtype) for...  93.9 us
    pallas_call x4, Pallas kernels, grid_call(): pl.pallas_call(kernel, out_shape=[jax.ShapeDtypeStruct(shape, dtype) for...  25.5 us
    ppermute x16, starting transfers between devices, down(): return lax.ppermute(value, 'fsdp', self.back)  18.8 us
    ppermute x16, starting transfers between devices, up(): return lax.ppermute(value, 'fsdp', self.ahead)  14.2 us
    ppermute x16, waiting for transfers between devices, up(): return lax.ppermute(value, 'fsdp', self.ahead)  11.3 us
    unnamed x70, local copies, waits for them, and re-layouts  11 us
    dot_general x1, matrix products, contract(): lax.dot_general(left, right, (((left_dim,), (right_dim,)), ((), ())), pre...  9.08 us
    ppermute x16, waiting for transfers between devices, down(): return lax.ppermute(value, 'fsdp', self.back)  7.5 us
  transfers between devices with their start and end apart: 38, of which 19 were waited for; matrix products, arithmetic and copies ran while one was open for 5% of the time, Pallas kernels for 43%

profile of v1, /device:TPU:0, one launch (start us, length us, event | category | flops | bytes accessed | tf_op | source)
XLA Modules:
  0.0 217.6 jit_solution(3174884176573772601)
XLA Ops:
  3.0 7.3 %all-to-all-start = ((bf16[8,144,256]{2,1,0:T(8,128)(2,1)}), bf16[8,144,256]{2,1,0:T(8,128)(2,1)S(1)}, u32[]{:S(2)}, u32[]{:S(2)}) async-start(bf16[8,144,256]{2,1,0:T(8,128)(2,1)} %shard_map.170), calls=%async_computation | async-start | bytes 1179648 | tf_op jit(solution)/shard_map/all_to_all | solution.py:992
  10.4 9.1 %convolution_reduce_fusion = f32[1792]{0:T(1024)S(1)} fusion(bf16[1,4096]{1,0:T(2,128)(2,1)S(1)} %get-tuple-element.183, bf16[1,4096]{1,0:T(2,128)(2,1)S(1)} %get-tuple-element.182, bf16[1,4096]{1,0:T(2,128)(2,1)S(1)} %get-tuple-element.180, bf16[1,1792,4096]{2,1,0:T(8,128)(2,1)} %param.19), kind=kOutput, calls=%fused_computation | convolution fusion | flops 44117504 | bytes 14711808 | tf_op jit(solution)/shard_map/dot_general | solution.py:30
  19.5 6.7 %all-to-all-done.near_ref = bf16[8,144,256]{2,1,0:T(8,128)(2,1)S(1)} async-done(((bf16[8,144,256]{2,1,0:T(8,128)(2,1)}), bf16[8,144,256]{2,1,0:T(8,128)(2,1)S(1)}, u32[]{:S(2)}, u32[]{:S(2)}) %all-to-all-start) | async-done | bytes 589856 | tf_op jit(solution)/shard_map/all_to_all | solution.py:992
  31.6 3.5 %shard_map.172 = (f32[256,1792]{1,0:T(8,128)S(1)}, f32[256,1792]{1,0:T(8,128)S(1)}, bf16[1,256,512]{2,1,0:T(8,128)(2,1)S(1)}) custom-call(s32[8]{0:T(128)S(1)} %fusion.6.row_ref, bf16[256,512]{1,0:T(8,128)(2,1)S(1)} %get-tuple-element.95.refs_0_.band_ref, f32[8,1,512]{2,1,0:T(1,128)S(1)} %bitcast.23, ...), custom_call_target="tpu_custom_call" | custom-call | tf_op jit(solution)/shard_map/pallas_call | solution.py:310
  39.7 5.2 %shard_map.173 = (f32[256,1792]{1,0:T(8,128)S(1)}, f32[256,1792]{1,0:T(8,128)S(1)}, bf16[2,256,512]{2,1,0:T(8,128)(2,1)S(1)}) custom-call(s32[8]{0:T(128)S(1)} %fusion.6.row_ref, bf16[256,512]{1,0:T(8,128)(2,1)S(1)} %collective-permute-done.1.refs_0_, ...), custom_call_target="tpu_custom_call", output_to_operand_aliasing={{0}: (7, {}), {1}: (8, {})} | custom-call | tf_op jit(solution)/shard_map/pallas_call | solution.py:310
  47.7 5.2 %shard_map.174 = (f32[256,1792]{1,0:T(8,128)S(1)}, f32[256,1792]{1,0:T(8,128)S(1)}, bf16[2,256,512]{2,1,0:T(8,128)(2,1)S(1)}) custom-call(s32[8]{0:T(128)S(1)} %fusion.6.row_ref, bf16[256,512]{1,0:T(8,128)(2,1)S(1)} %collective-permute-done.3.refs_0_, ...), custom_call_target="tpu_custom_call", output_to_operand_aliasing={{0}: (7, {}), {1}: (8, {})} | custom-call | tf_op jit(solution)/shard_map/pallas_call | solution.py:310
  55.1 5.3 %shard_map.176 = (f32[256,1792]{1,0:T(8,128)S(1)}, f32[256,1792]{1,0:T(8,128)S(1)}, bf16[2,256,512]{2,1,0:T(8,128)(2,1)S(1)}) custom-call(s32[8]{0:T(128)S(1)} %fusion.6.row_ref, bf16[256,512]{1,0:T(8,128)(2,1)S(1)} %collective-permute-done.5.back_ref.refs_0_, ...), custom_call_target="tpu_custom_call", output_to_operand_aliasing={{0}: (7, {}), {1}: (8, {})} | custom-call | tf_op jit(solution)/shard_map/pallas_call | solution.py:310
  61.2 4.7 %shard_map.177 = (f32[256,1792]{1,0:T(8,128)S(1)}, f32[256,1792]{1,0:T(8,128)S(1)}, bf16[1,256,512]{2,1,0:T(8,128)(2,1)S(1)}, bf16[256,1792]{1,0:T(8,128)(2,1)S(1)}, f32[256,1]{1,0:T(8,128)S(1)}) custom-call(s32[8]{0:T(128)S(1)} %fusion.6.row_ref, bf16[128,512]{1,0:T(8,128)(2,1)S(1)} %collective-permute-done.7.refs_0_, ...), custom_call_target="tpu_custom_call", output_to_operand_aliasing={{0}: (7, {}), {1}: (8, {})} | custom-call | tf_op jit(solution)/shard_map/pallas_call | solution.py:310
  65.9 3.5 %shard_map.178.far_ref = f32[1,256,512]{2,1,0:T(8,128)S(1)} custom-call(s32[8]{0:T(128)S(1)} %fusion.6.row_ref, bf16[256,1792]{1,0:T(8,128)(2,1)S(1)} %get-tuple-element.128.hidden_ref.value_ref, bf16[1792,4096]{1,0:T(8,128)(2,1)} %bitcast.34), custom_call_target="tpu_custom_call" | custom-call | tf_op jit(solution)/shard_map/pallas_call | solution.py:310
  71.6 4.2 %shard_map.180.refs_0_ = f32[2,256,512]{2,1,0:T(8,128)S(1)} custom-call(s32[8]{0:T(128)S(1)} %fusion.6.row_ref, bf16[256,1792]{1,0:T(8,128)(2,1)S(1)} %get-tuple-element.128.hidden_ref.value_ref, bf16[1792,4096]{1,0:T(8,128)(2,1)} %bitcast.35), custom_call_target="tpu_custom_call" | custom-call | tf_op jit(solution)/shard_map/pallas_call | solution.py:310
  78.0 4.2 %shard_map.182.refs_0_ = f32[2,256,512]{2,1,0:T(8,128)S(1)} custom-call(s32[8]{0:T(128)S(1)} %fusion.6.row_ref, bf16[256,1792]{1,0:T(8,128)(2,1)S(1)} %get-tuple-element.128.hidden_ref.value_ref, bf16[1792,4096]{1,0:T(8,128)(2,1)} %bitcast.36), custom_call_target="tpu_custom_call" | custom-call | tf_op jit(solution)/shard_map/pallas_call | solution.py:310
  87.3 4.2 %shard_map.185.refs_0_ = f32[2,256,512]{2,1,0:T(8,128)S(1)} custom-call(s32[8]{0:T(128)S(1)} %fusion.6.row_ref, bf16[256,1792]{1,0:T(8,128)(2,1)S(1)} %get-tuple-element.128.hidden_ref.value_ref, bf16[1792,4096]{1,0:T(8,128)(2,1)} %bitcast.37), custom_call_target="tpu_custom_call" | custom-call | tf_op jit(solution)/shard_map/pallas_call | solution.py:310
  100.1 4.3 %collective-permute-done.15.back_ref = bf16[256,512]{1,0:T(8,128)(2,1)S(1)} collective-permute-done((bf16[256,512]{1,0:T(8,128)(2,1)S(1)}, bf16[256,512]{1,0:T(8,128)(2,1)S(1)}, u32[]{:S(2)}, u32[]{:S(2)}) %collective-permute-start.15) | collective-permute-done | bytes 262176 | tf_op jit(solution)/shard_map/ppermute | solution.py:57
  117.5 4.2 %shard_map.190.refs_3_ = f32[256,1792]{1,0:T(8,128)S(1)} custom-call(s32[8]{0:T(128)S(1)} %fusion.6.row_ref, bf16[272,512]{1,0:T(8,128)(2,1)S(1)} %collective-permute-done.17.refs_0_.refs_9_.refs_1_, bf16[272,512]{1,0:T(8,128)(2,1)S(1)} %collective-permute-done.18.refs_1_.refs_10_.refs_2_, ...), custom_call_target="tpu_custom_call", output_to_operand_aliasing={{}: (4, {})} | custom-call | tf_op jit(solution)/shard_map/pallas_call | solution.py:310
  125.0 4.2 %shard_map.191.refs_3_ = f32[256,1792]{1,0:T(8,128)S(1)} custom-call(s32[8]{0:T(128)S(1)} %fusion.6.row_ref, bf16[272,512]{1,0:T(8,128)(2,1)S(1)} %collective-permute-done.19.refs_0_.refs_11_, bf16[272,512]{1,0:T(8,128)(2,1)S(1)} %collective-permute-done.20.refs_1_.refs_12_, bf16[1792,4096]{1,0:T(8,128)(2,1)} %bitcast.41, ...), custom_call_target="tpu_custom_call", output_to_operand_aliasing={{}: (4, {})} | custom-call | tf_op jit(solution)/shard_map/pallas_call | solution.py:310
  133.2 4.5 %shard_map.193.refs_3_ = f32[256,1792]{1,0:T(8,128)S(1)} custom-call(s32[8]{0:T(128)S(1)} %fusion.6.row_ref, bf16[272,512]{1,0:T(8,128)(2,1)S(1)} %collective-permute-done.21.back_ref.refs_0_.refs_13_.refs_2_, bf16[272,512]{1,0:T(8,128)(2,1)S(1)} %collective-permute-done.22.ahead_ref.refs_1_.refs_14_.refs_0_, ...), custom_call_target="tpu_custom_call", output_to_operand_aliasing={{}: (4, {})} | custom-call | tf_op jit(solution)/shard_map/pallas_call | solution.py:310
  140.5 6.1 %shard_map.194 = (f32[256,1792]{1,0:T(8,128)S(1)}, bf16[2,256,1792]{2,1,0:T(8,128)(2,1)S(1)}, f32[8,256]{1,0:T(8,128)S(1)}, f32[1,1]{1,0:T(1,128)}, f32[256,1]{1,0:T(8,128)S(1)}, /*index=5*/f32[256,1]{1,0:T(8,128)S(1)}) custom-call(s32[8]{0:T(128)S(1)} %fusion.6.row_ref, ...), custom_call_target="tpu_custom_call", output_to_operand_aliasing={{0}: (4, {})} | custom-call | tf_op jit(solution)/shard_map/pallas_call | solution.py:310
  152.1 4.9 %shard_map.197.refs_0_ = f32[2,256,512]{2,1,0:T(8,128)S(1)} custom-call(s32[8]{0:T(128)S(1)} %fusion.6.row_ref, bf16[2,256,1792]{2,1,0:T(8,128)(2,1)S(1)} %get-tuple-element.172.grads_ref.refs_5_, bf16[8,512,1792]{2,1,0:T(8,128)(2,1)} %bitcast.50, bf16[8,512,1792]{2,1,0:T(8,128)(2,1)} %bitcast.60), custom_call_target="tpu_custom_call" | custom-call | tf_op jit(solution)/shard_map/pallas_call | solution.py:310
  159.9 4.9 %shard_map.200.refs_0_ = f32[2,256,512]{2,1,0:T(8,128)S(1)} custom-call(s32[8]{0:T(128)S(1)} %fusion.6.row_ref, bf16[2,256,1792]{2,1,0:T(8,128)(2,1)S(1)} %get-tuple-element.172.grads_ref.refs_5_, bf16[8,512,1792]{2,1,0:T(8,128)(2,1)} %bitcast.51, bf16[8,512,1792]{2,1,0:T(8,128)(2,1)} %bitcast.61), custom_call_target="tpu_custom_call" | custom-call | tf_op jit(solution)/shard_map/pallas_call | solution.py:310
  164.9 4.6 %shard_map.199.refs_7_ = bf16[1792,4096]{1,0:T(8,128)(2,1)} custom-call(s32[8]{0:T(128)S(1)} %fusion.7.index_ref, bf16[272,512]{1,0:T(8,128)(2,1)S(1)} %get-tuple-element.127.refs_0_.refs_8_, bf16[272,512]{1,0:T(8,128)(2,1)S(1)} %collective-permute-done.17.refs_0_.refs_9_.refs_1_, bf16[272,512]{1,0:T(8,128)(2,1)S(1)} %copy-done.9, ...), custom_call_target="tpu_custom_call" | custom-call | tf_op jit(solution)/shard_map/pallas_call | solution.py:879
  171.6 4.6 %shard_map.202.refs_7_ = bf16[1792,4096]{1,0:T(8,128)(2,1)} custom-call(s32[8]{0:T(128)S(1)} %fusion.7.index_ref, bf16[272,512]{1,0:T(8,128)(2,1)S(1)} %copy-done.11, bf16[272,512]{1,0:T(8,128)(2,1)S(1)} %copy-done.13, bf16[272,512]{1,0:T(8,128)(2,1)S(1)} %collective-permute-done.21.back_ref.refs_0_.refs_13_.refs_2_, ...), custom_call_target="tpu_custom_call", output_to_operand_aliasing={{}: (8, {})} | custom-call | tf_op jit(solution)/shard_map/pallas_call | solution.py:879
  176.2 4.9 %shard_map.204.refs_0_ = f32[2,256,512]{2,1,0:T(8,128)S(1)} custom-call(s32[8]{0:T(128)S(1)} %fusion.6.row_ref, bf16[2,256,1792]{2,1,0:T(8,128)(2,1)S(1)} %get-tuple-element.172.grads_ref.refs_5_, bf16[8,512,1792]{2,1,0:T(8,128)(2,1)} %bitcast.52, bf16[8,512,1792]{2,1,0:T(8,128)(2,1)} %bitcast.62), custom_call_target="tpu_custom_call" | custom-call | tf_op jit(solution)/shard_map/pallas_call | solution.py:310
  187.3 4.3 %shard_map.206 = bf16[1792,4096]{1,0:T(8,128)(2,1)} custom-call(s32[8]{0:T(128)S(1)} %fusion.7.index_ref, bf16[272,512]{1,0:T(8,128)(2,1)S(1)} %collective-permute-done.22.ahead_ref.refs_1_.refs_14_.refs_0_, bf16[128,512]{1,0:T(8,128)(2,1)} %collective-permute-done.23.refs_0_.refs_1_, ...), custom_call_target="tpu_custom_call", output_to_operand_aliasing={{}: (8, {})} | custom-call | tf_op jit(solution)/shard_map/pallas_call | solution.py:879
  202.4 12.0 %shard_map.208 = (bf16[8,512,1792]{2,1,0:T(8,128)(2,1)}, bf16[8,512,1792]{2,1,0:T(8,128)(2,1)}) custom-call(s32[8]{0:T(128)S(1)} %fusion.7.index_ref, bf16[1,256,512]{2,1,0:T(8,128)(2,1)S(1)} %copy-done.27, bf16[2,256,512]{2,1,0:T(8,128)(2,1)S(1)} %copy-done.18, bf16[2,256,512]{2,1,0:T(8,128)(2,1)S(1)} %copy-done.20, bf16[2,256,512]{2,1,0:T(8,128)(2,1)S(1)} %copy-done.22, ...), custom_call_target="tpu_custom_call" | custom-call | tf_op jit(solution)/shard_map/pallas_call | solution.py:879
  (173 shorter events, 89.6 us)
Async XLA Ops:
  3.0 23.1 %all-to-all-start = ((bf16[8,144,256]{2,1,0:T(8,128)(2,1)}), bf16[8,144,256]{2,1,0:T(8,128)(2,1)S(1)}, u32[]{:S(2)}, u32[]{:S(2)}) async-start(bf16[8,144,256]{2,1,0:T(8,128)(2,1)} %shard_map.170), calls=%async_computation | async-start | bytes 1179648 | tf_op jit(solution)/shard_map/all_to_all | solution.py:992
  28.8 8.4 %collective-permute-start.1 = (bf16[256,512]{1,0:T(8,128)(2,1)S(1)}, bf16[256,512]{1,0:T(8,128)(2,1)S(1)}, u32[]{:S(2)}, u32[]{:S(2)}) collective-permute-start(bf16[256,512]{1,0:T(8,128)(2,1)S(1)} %get-tuple-element.95.refs_0_.band_ref), channel_id=1, source_target_pairs={{0,2},{2,4},{4,6},{6,7},{7,5},{5,3},{3,1},{1,0},{8,10},{10,12},{12... | collective-permute-start | bytes 786440 | tf_op jit(solution)/shard_map/ppermute | solution.py:57
  29.6 8.1 %collective-permute-start.2 = (bf16[256,512]{1,0:T(8,128)(2,1)S(1)}, bf16[256,512]{1,0:T(8,128)(2,1)S(1)}, u32[]{:S(2)}, u32[]{:S(2)}) collective-permute-start(bf16[256,512]{1,0:T(8,128)(2,1)S(1)} %get-tuple-element.95.refs_0_.band_ref), channel_id=1, source_target_pairs={{2,0},{4,2},{6,4},{7,6},{5,7},{3,5},{1,3},{0,1},{10,8},{12,10},{14... | collective-permute-start | bytes 786440 | tf_op jit(solution)/shard_map/ppermute | solution.py:60
  37.6 8.1 %collective-permute-start.3 = (bf16[256,512]{1,0:T(8,128)(2,1)S(1)}, bf16[256,512]{1,0:T(8,128)(2,1)S(1)}, u32[]{:S(2)}, u32[]{:S(2)}) collective-permute-start(bf16[256,512]{1,0:T(8,128)(2,1)S(1)} %collective-permute-done.1.refs_0_), channel_id=1, source_target_pairs={{0,2},{2,4},{4,6},{6,7},{7,5},{5,3},{3,1},{1,0},{8,10},{10,12},{12... | collective-permute-start | bytes 786440 | tf_op jit(solution)/shard_map/ppermute | solution.py:57
  38.0 7.7 %collective-permute-start.4 = (bf16[256,512]{1,0:T(8,128)(2,1)S(1)}, bf16[256,512]{1,0:T(8,128)(2,1)S(1)}, u32[]{:S(2)}, u32[]{:S(2)}) collective-permute-start(bf16[256,512]{1,0:T(8,128)(2,1)S(1)} %collective-permute-done.2.refs_1_), channel_id=1, source_target_pairs={{2,0},{4,2},{6,4},{7,6},{5,7},{3,5},{1,3},{0,1},{10,8},{12,10},{14... | collective-permute-start | bytes 786440 | tf_op jit(solution)/shard_map/ppermute | solution.py:60
  45.7 7.3 %collective-permute-start.5 = (bf16[256,512]{1,0:T(8,128)(2,1)S(1)}, bf16[256,512]{1,0:T(8,128)(2,1)S(1)}, u32[]{:S(2)}, u32[]{:S(2)}) collective-permute-start(bf16[256,512]{1,0:T(8,128)(2,1)S(1)} %collective-permute-done.3.refs_0_), channel_id=1, source_target_pairs={{0,2},{2,4},{4,6},{6,7},{7,5},{5,3},{3,1},{1,0},{8,10},{10,12},{12... | collective-permute-start | bytes 786440 | tf_op jit(solution)/shard_map/ppermute | solution.py:57
  53.0 8.2 %collective-permute-start.7 = (bf16[128,512]{1,0:T(8,128)(2,1)S(1)}, bf16[128,512]{1,0:T(8,128)(2,1)S(1)}, u32[]{:S(2)}, u32[]{:S(2)}) collective-permute-start(bf16[128,512]{1,0:T(8,128)(2,1)S(1)} %get-tuple-element.109), channel_id=1, source_target_pairs={{0,2},{2,4},{4,6},{6,7},{7,5},{5,3},{3,1},{1,0},{8,10},{10,12},{12... | collective-permute-start | bytes 393224 | tf_op jit(solution)/shard_map/ppermute | solution.py:57
  75.9 7.2 %collective-permute-start.11 = (bf16[256,512]{1,0:T(8,128)(2,1)S(1)}, bf16[256,512]{1,0:T(8,128)(2,1)S(1)}, u32[]{:S(2)}, u32[]{:S(2)}) collective-permute-start(bf16[256,512]{1,0:T(8,128)(2,1)S(1)} %get-tuple-element.118), channel_id=1, source_target_pairs={{0,2},{2,4},{4,6},{6,7},{7,5},{5,3},{3,1},{1,0},{8,10},{10,12},{12... | collective-permute-start | bytes 786440 | tf_op jit(solution)/shard_map/ppermute | solution.py:57
  77.3 7.9 %collective-permute-start.12 = (bf16[256,512]{1,0:T(8,128)(2,1)S(1)}, bf16[256,512]{1,0:T(8,128)(2,1)S(1)}, u32[]{:S(2)}, u32[]{:S(2)}) collective-permute-start(bf16[256,512]{1,0:T(8,128)(2,1)S(1)} %get-tuple-element.119), channel_id=1, source_target_pairs={{2,0},{4,2},{6,4},{7,6},{5,7},{3,5},{1,3},{0,1},{10,8},{12,10},{14... | collective-permute-start | bytes 786440 | tf_op jit(solution)/shard_map/ppermute | solution.py:60
  85.3 9.1 %collective-permute-start.13 = (bf16[256,512]{1,0:T(8,128)(2,1)S(1)}, bf16[256,512]{1,0:T(8,128)(2,1)S(1)}, u32[]{:S(2)}, u32[]{:S(2)}) collective-permute-start(bf16[256,512]{1,0:T(8,128)(2,1)S(1)} %get-tuple-element.121), channel_id=1, source_target_pairs={{0,2},{2,4},{4,6},{6,7},{7,5},{5,3},{3,1},{1,0},{8,10},{10,12},{12... | collective-permute-start | bytes 786440 | tf_op jit(solution)/shard_map/ppermute | solution.py:57
  86.2 9.0 %collective-permute-start.14 = (bf16[256,512]{1,0:T(8,128)(2,1)S(1)}, bf16[256,512]{1,0:T(8,128)(2,1)S(1)}, u32[]{:S(2)}, u32[]{:S(2)}) collective-permute-start(bf16[256,512]{1,0:T(8,128)(2,1)S(1)} %get-tuple-element.122), channel_id=1, source_target_pairs={{2,0},{4,2},{6,4},{7,6},{5,7},{3,5},{1,3},{0,1},{10,8},{12,10},{14... | collective-permute-start | bytes 786440 | tf_op jit(solution)/shard_map/ppermute | solution.py:60
  95.3 9.0 %collective-permute-start.15 = (bf16[256,512]{1,0:T(8,128)(2,1)S(1)}, bf16[256,512]{1,0:T(8,128)(2,1)S(1)}, u32[]{:S(2)}, u32[]{:S(2)}) collective-permute-start(bf16[256,512]{1,0:T(8,128)(2,1)S(1)} %get-tuple-element.124), channel_id=1, source_target_pairs={{0,2},{2,4},{4,6},{6,7},{7,5},{5,3},{3,1},{1,0},{8,10},{10,12},{12... | collective-permute-start | bytes 786440 | tf_op jit(solution)/shard_map/ppermute | solution.py:57
  96.6 9.2 %collective-permute-start.16 = (bf16[256,512]{1,0:T(8,128)(2,1)S(1)}, bf16[256,512]{1,0:T(8,128)(2,1)S(1)}, u32[]{:S(2)}, u32[]{:S(2)}) collective-permute-start(bf16[256,512]{1,0:T(8,128)(2,1)S(1)} %get-tuple-element.125), channel_id=1, source_target_pairs={{2,0},{4,2},{6,4},{7,6},{5,7},{3,5},{1,3},{0,1},{10,8},{12,10},{14... | collective-permute-start | bytes 786440 | tf_op jit(solution)/shard_map/ppermute | solution.py:60
  107.0 7.5 %collective-permute-start.17 = (bf16[272,512]{1,0:T(8,128)(2,1)S(1)}, bf16[272,512]{1,0:T(8,128)(2,1)S(1)}, u32[]{:S(2)}, u32[]{:S(2)}) collective-permute-start(bf16[272,512]{1,0:T(8,128)(2,1)S(1)} %get-tuple-element.127.refs_0_.refs_8_), channel_id=1, source_target_pairs={{0,2},{2,4},{4,6},{6,7},{7,5},{5,3},{3,1},{1,0},{8,10},{10,12},{12... | collective-permute-start | bytes 835592 | tf_op jit(solution)/shard_map/ppermute | solution.py:57
  108.4 7.1 %collective-permute-start.18 = (bf16[272,512]{1,0:T(8,128)(2,1)S(1)}, bf16[272,512]{1,0:T(8,128)(2,1)S(1)}, u32[]{:S(2)}, u32[]{:S(2)}) collective-permute-start(bf16[272,512]{1,0:T(8,128)(2,1)S(1)} %get-tuple-element.127.refs_0_.refs_8_), channel_id=1, source_target_pairs={{2,0},{4,2},{6,4},{7,6},{5,7},{3,5},{1,3},{0,1},{10,8},{12,10},{14... | collective-permute-start | bytes 835592 | tf_op jit(solution)/shard_map/ppermute | solution.py:60
  131.1 7.9 %collective-permute-start.24 = (bf16[144,512]{1,0:T(8,128)(2,1)}, bf16[144,512]{1,0:T(8,128)(2,1)}, u32[]{:S(2)}, u32[]{:S(2)}) collective-permute-start(bf16[144,512]{1,0:T(8,128)(2,1)} %get-tuple-element.136), channel_id=1, source_target_pairs={{2,0},{4,2},{6,4},{7,6},{5,7},{3,5},{1,3},{0,1},{10,8},{12,10},{14... | collective-permute-start | bytes 442376 | tf_op jit(solution)/shard_map/ppermute | solution.py:60
  150.0 7.0 %collective-permute-start.25 = (bf16[144,512]{1,0:T(8,128)(2,1)S(1)}, bf16[144,512]{1,0:T(8,128)(2,1)S(1)}, u32[]{:S(2)}, u32[]{:S(2)}) collective-permute-start(bf16[144,512]{1,0:T(8,128)(2,1)S(1)} %get-tuple-element.147), channel_id=1, source_target_pairs={{0,2},{2,4},{4,6},{6,7},{7,5},{5,3},{3,1},{1,0},{8,10},{10,12},{12... | collective-permute-start | bytes 442376 | tf_op jit(solution)/shard_map/ppermute | solution.py:57
  157.1 12.3 %collective-permute-start.27 = (bf16[272,512]{1,0:T(8,128)(2,1)S(1)}, bf16[272,512]{1,0:T(8,128)(2,1)S(1)}, u32[]{:S(2)}, u32[]{:S(2)}) collective-permute-start(bf16[272,512]{1,0:T(8,128)(2,1)S(1)} %get-tuple-element.152), channel_id=1, source_target_pairs={{0,2},{2,4},{4,6},{6,7},{7,5},{5,3},{3,1},{1,0},{8,10},{10,12},{12... | collective-permute-start | bytes 835592 | tf_op jit(solution)/shard_map/ppermute | solution.py:57
  157.7 11.7 %collective-permute-start.28 = (bf16[272,512]{1,0:T(8,128)(2,1)S(1)}, bf16[272,512]{1,0:T(8,128)(2,1)S(1)}, u32[]{:S(2)}, u32[]{:S(2)}) collective-permute-start(bf16[272,512]{1,0:T(8,128)(2,1)S(1)} %get-tuple-element.153), channel_id=1, source_target_pairs={{2,0},{4,2},{6,4},{7,6},{5,7},{3,5},{1,3},{0,1},{10,8},{12,10},{14... | collective-permute-start | bytes 835592 | tf_op jit(solution)/shard_map/ppermute | solution.py:60
  169.5 11.6 %collective-permute-start.29 = (bf16[272,512]{1,0:T(8,128)(2,1)S(1)}, bf16[272,512]{1,0:T(8,128)(2,1)S(1)}, u32[]{:S(2)}, u32[]{:S(2)}) collective-permute-start(bf16[272,512]{1,0:T(8,128)(2,1)S(1)} %get-tuple-element.160), channel_id=1, source_target_pairs={{0,2},{2,4},{4,6},{6,7},{7,5},{5,3},{3,1},{1,0},{8,10},{10,12},{12... | collective-permute-start | bytes 835592 | tf_op jit(solution)/shard_map/ppermute | solution.py:57
  170.1 11.0 %collective-permute-start.30 = (bf16[272,512]{1,0:T(8,128)(2,1)S(1)}, bf16[272,512]{1,0:T(8,128)(2,1)S(1)}, u32[]{:S(2)}, u32[]{:S(2)}) collective-permute-start(bf16[272,512]{1,0:T(8,128)(2,1)S(1)} %get-tuple-element.161), channel_id=1, source_target_pairs={{2,0},{4,2},{6,4},{7,6},{5,7},{3,5},{1,3},{0,1},{10,8},{12,10},{14... | collective-permute-start | bytes 835592 | tf_op jit(solution)/shard_map/ppermute | solution.py:60
  181.3 10.4 %collective-permute-start.31 = (bf16[272,512]{1,0:T(8,128)(2,1)S(1)}, bf16[272,512]{1,0:T(8,128)(2,1)S(1)}, u32[]{:S(2)}, u32[]{:S(2)}) collective-permute-start(bf16[272,512]{1,0:T(8,128)(2,1)S(1)} %get-tuple-element.165), channel_id=1, source_target_pairs={{0,2},{2,4},{4,6},{6,7},{7,5},{5,3},{3,1},{1,0},{8,10},{10,12},{12... | collective-permute-start | bytes 835592 | tf_op jit(solution)/shard_map/ppermute | solution.py:57
  181.9 9.8 %collective-permute-start.32 = (bf16[272,512]{1,0:T(8,128)(2,1)S(1)}, bf16[272,512]{1,0:T(8,128)(2,1)S(1)}, u32[]{:S(2)}, u32[]{:S(2)}) collective-permute-start(bf16[272,512]{1,0:T(8,128)(2,1)S(1)} %get-tuple-element.166), channel_id=1, source_target_pairs={{2,0},{4,2},{6,4},{7,6},{5,7},{3,5},{1,3},{0,1},{10,8},{12,10},{14... | collective-permute-start | bytes 835592 | tf_op jit(solution)/shard_map/ppermute | solution.py:60
  196.0 18.6 %all-to-all-start.1 = ((bf16[8,64,512]{2,1,0:T(8,128)(2,1)}), bf16[8,64,512]{2,1,0:T(8,128)(2,1)S(1)}, u32[]{:S(2)}, u32[]{:S(2)}) async-start(bf16[8,64,512]{2,1,0:T(8,128)(2,1)} %shard_map.209), calls=%async_computation.1 | async-start | bytes 1048576 | tf_op jit(solution)/shard_map/all_to_all | solution.py:1100
  (49 other events, 315.9 us)

commit v2 on v1

--- a/solution.py
+++ b/solution.py
@@ -302,7 +302,7 @@
     return contract(left, right, left_dim, right_dim)
 
 
-def call(kernel, operands, specs, outs, scratch=(), limit=8, aliases=None):
+def call(kernel, operands, specs, outs, scratch=(), limit=8, aliases=None, out_specs=None):
     operands = [
         pltpu.with_memory_space_constraint(value, pltpu.HBM) if spec is IN_HBM else value
         for value, spec in zip(operands, specs)
@@ -311,6 +311,7 @@
         kernel,
         out_shape=[jax.ShapeDtypeStruct(shape, dtype) for shape, dtype in outs],
         in_specs=specs,
+        out_specs=out_specs or [IN_VMEM] * len(outs),
         scratch_shapes=list(scratch),
         input_output_aliases=aliases or {},
         compiler_params=pltpu.CompilerParams(vmem_limit_bytes=limit << 20),
@@ -330,21 +331,13 @@
         slot = k * ways + w
         return pltpu.make_async_copy(sources[w](k), weights.at[slot], done.at[slot])
 
-    for w in range(ways):
-        copy(0, w).start()
+    for k in range(count):
+        for w in range(ways):
+            copy(k, w).start()
 
     def step(k):
         for w in range(ways):
             copy(k, w).wait()
-            if isinstance(k, int):
-                if k + 1 < count:
-                    copy(k + 1, w).start()
-            else:
-
-                @pl.when(k + 1 < count)
-                def _():
-                    copy(k + 1, w).start()
-
             use(k, w, weights.at[k * ways + w])
 
     if count == 1:
@@ -451,13 +444,14 @@
     )
 
 
-def forward_bands(bands, row, offsets, gain_bands, inverse, gate_bands, up_bands, totals, head):
+def forward_bands(bands, row, offsets, gain_bands, inverse, gate_bands, up_bands, totals, final):
     bands = [pieces_of(band) for band in bands]
     flat = [piece for band in bands for piece in band]
     count = len(bands)
     rows, columns = inverse.shape[0], flat[0].shape[1]
     width = gate_bands.shape[2]
-    last = head is not None
+    last = final is not None
+    far_offset = row.shape[0] // 2
 
     def kernel(row_ref, *refs):
         refs = list(refs)
@@ -466,11 +460,12 @@
         gain_ref, inverse_ref, gate_hbm, up_hbm = take(4)
         if totals:
             take(2)
-        head_ref = take(1)[0] if last else None
+        head_ref, down_hbm = take(2) if last else (None, None)
         totals_out = take(2)
         (scaled_out,) = take(1)
-        hidden_out, score_out = take(2) if last else (None, None)
-        weights, done = refs
+        if last:
+            hidden_out, score_out, far_up, far_down = take(4)
+        weights, done = take(2)
 
         def use(k, w, block):
             totals_out[w][...] += dot(scaled_out[k], block[...], 1, 0)
@@ -483,6 +478,13 @@
             ],
             weights, done, use,
         )
+        if last:
+            far_weights, far_done = refs
+            start = pl.multiple_of(row_ref[far_offset] * columns, columns)
+            far_copy = pltpu.make_async_copy(
+                down_hbm.at[:, pl.ds(start, columns)], far_weights, far_done
+            )
+            far_copy.start()
         for k in range(count):
             start = 0
             for ref in band_refs[k]:
@@ -509,6 +511,10 @@
                 return 0
 
             lax.fori_loop(0, rows // STRIPE, finish, 0)
+            far_copy.wait()
+            far = dot(hidden_out[...], far_weights[...], 1, 0).astype(bf16)
+            far_up[...] = far[: rows // 2]
+            far_down[...] = far[rows // 2 :]
 
     operands = [row] + flat + [gain_bands, inverse, gate_bands, up_bands]
     specs = [IN_SMEM] + [IN_VMEM] * (len(flat) + 2) + [IN_HBM, IN_HBM]
@@ -517,15 +523,15 @@
         aliases = {len(operands): 0, len(operands) + 1: 1}
         operands += list(totals)
         specs += [IN_VMEM] * 2
-    if last:
-        operands.append(head)
-        specs.append(IN_VMEM)
     outs = [((rows, width), f32)] * 2 + [((count, rows, columns), bf16)]
-    if last:
-        outs += [((rows, width), bf16), ((rows, 1), f32)]
     scratch = [
         pltpu.VMEM((2 * count, columns, width), bf16), pltpu.SemaphoreType.DMA((2 * count,))
     ]
+    if last:
+        operands += list(final)
+        specs += [IN_VMEM, IN_HBM]
+        outs += [((rows, width), bf16), ((rows, 1), f32)] + [((rows // 2, columns), bf16)] * 2
+        scratch += [pltpu.VMEM((width, columns), bf16), pltpu.SemaphoreType.DMA]
     out = call(kernel, operands, specs, outs, scratch, 8 + 4 * count, aliases)
     return out[:2], out[2], out[3:]
 
@@ -565,7 +571,8 @@
     count = len(bands)
     columns = flat[0].shape[1]
     width, model_width = w_down.shape
-    others = final[4] if final else []
+    others = final[6] if final else []
+    far_offset = row.shape[0] // 2
 
     def kernel(row_ref, *refs):
         refs = list(refs)
@@ -575,11 +582,11 @@
         if total is not None:
             take(1)
         if final:
-            gate_ref, up_ref, head_ref, labels_ref = take(4)
+            gate_ref, up_ref, head_ref, labels_ref, gate_hbm, up_hbm = take(6)
             other_refs = take(len(others))
         (back_ref,) = take(1)
         if final:
-            grads_out, inner_out, loss_out, head_scale, summed_scale = take(5)
+            grads_out, inner_out, loss_out, head_scale, summed_scale, far_up, far_down = take(7)
         weights, done, kept = take(3)
 
         def use(k, w, block):
@@ -590,6 +597,16 @@
             return down_hbm.at[:, pl.ds(start, columns)]
 
         run = stream(count, [source], weights, done, use)
+        if final:
+            inner, far_weights, far_done = refs
+            far_copies = [
+                pltpu.make_async_copy(
+                    source.at[row_ref[far_offset]], far_weights.at[w], far_done.at[w]
+                )
+                for w, source in enumerate((gate_hbm, up_hbm))
+            ]
+            for one in far_copies:
+                one.start()
         for k in range(count):
             start = 0
             for ref in band_refs[k]:
@@ -604,7 +621,7 @@
             for ref in other_refs:
                 notes += ref[rows:].astype(f32)
             loss, head_column, summed_column = pair_scales(
-                notes, labels_ref, rows, final[5], model_width
+                notes, labels_ref, rows, final[7], model_width
             )
             loss_out[...] = loss
             head_scale[...] = head_column
@@ -612,7 +629,6 @@
         run()
         if not final:
             return
-        (inner,) = refs
 
         def finish(i, _):
             part = pl.ds(i * STRIPE, STRIPE)
@@ -629,7 +645,17 @@
             return 0
 
         lax.fori_loop(0, rows // STRIPE, finish, 0)
-        inner_out[...] = rows_as_lanes([inner[...]])
+        lanes = rows_as_lanes([inner[...]])
+        inner_out[...] = lanes
+        far_copies[0].wait()
+        far = dot(grads_out[0], far_weights[0], 1, 1)
+        far_copies[1].wait()
+        far += dot(grads_out[1], far_weights[1], 1, 1)
+        middle = rows // 2
+        far_up[:middle] = far[:middle].astype(bf16)
+        far_down[...] = far[middle:].astype(bf16)
+        pad = jnp.zeros((AUX - 8, columns), f32)
+        far_up[middle:] = jnp.concatenate([high_low(lanes), pad], axis=0).astype(bf16)
 
     operands = [row] + flat + [w_down]
     specs = [IN_SMEM] + [IN_VMEM] * len(flat) + [IN_HBM]
@@ -644,14 +670,17 @@
     ]
     outs = [((rows, width), f32)]
     if final:
-        operands += list(final[:4]) + list(others)
-        specs += [IN_VMEM] * 3 + [IN_SMEM] + [IN_VMEM] * len(others)
+        operands += list(final[:6]) + list(others)
+        specs += [IN_VMEM] * 3 + [IN_SMEM] + [IN_HBM] * 2 + [IN_VMEM] * len(others)
         outs += [
             ((2, rows, width), bf16), ((8, rows), f32), ((1, 1), f32), ((rows, 1), f32),
-            ((rows, 1), f32),
+            ((rows, 1), f32), ((rows // 2 + AUX, columns), bf16), ((rows // 2, columns), bf16),
         ]
-        scratch += [pltpu.VMEM((rows, 1), f32)]
-    return call(kernel, operands, specs, outs, scratch, 8 + 3 * count, aliases)
+        scratch += [
+            pltpu.VMEM((rows, 1), f32), pltpu.VMEM((2, columns, width), bf16),
+            pltpu.SemaphoreType.DMA((2,)),
+        ]
+    return call(kernel, operands, specs, outs, scratch, 10 + 3 * count, aliases)
 
 
 def out_parts(row, offsets, hidden, w_down, columns):
@@ -676,12 +705,20 @@
     )[0]
 
 
-def scaled_parts(row, offsets, grads, gate_bands, up_bands):
+def scaled_parts(row, offsets, grads, gate_bands, up_bands, down):
     count = len(offsets)
     rows, width = grads.shape[1:]
     columns = gate_bands.shape[1]
-
-    def kernel(row_ref, grads_ref, gate_hbm, up_hbm, out, weights, done):
+    order, first, bands, hidden_t, head_bands, head_scale, summed_scale, before = down
+    flat = [piece for band in bands for piece in pieces_of(band)]
+    extra = len(bands)
+    nodes = gate_bands.shape[0]
+
+    def kernel(row_ref, order_ref, grads_ref, gate_hbm, up_hbm, hidden_ref, head_ref,
+               head_scale_ref, summed_scale_ref, *refs):
+        band_refs = list(refs[: len(flat)])
+        out, down_hbm, weights, done, made, sent, kept = refs[-7:]
+
         def use(k, w, block):
             term = dot(grads_ref[w], block[...], 1, 1)
             if w:
@@ -689,21 +726,61 @@
             else:
                 out[k] = term
 
-        stream(
+        run = stream(
             count,
             [
                 lambda k: gate_hbm.at[band_number(row_ref, offsets, k)],
                 lambda k: up_hbm.at[band_number(row_ref, offsets, k)],
             ],
             weights, done, use,
-        )()
-
+        )
+        for j, band in enumerate(bands):
+            start = 0
+            for _ in pieces_of(band):
+                ref = band_refs.pop(0)
+                size = min(ref.shape[0], rows - start)
+                kept[j, start : start + size] = ref[:size]
+                start += size
+
+        def leave(j):
+            start = pl.multiple_of(order_ref[first + j] * columns, columns)
+            return pltpu.make_async_copy(
+                made.at[j], down_hbm.at[:, pl.ds(start, columns)], sent.at[j]
+            )
+
+        def make(j, _):
+            dsummed = (
+                head_scale_ref[...] * head_ref[order_ref[first + j]]
+                - summed_scale_ref[...] * kept[j].astype(f32)
+            )
+            made[j] = dot(hidden_ref[...], dsummed.astype(bf16), 1, 0).astype(bf16)
+            leave(j).start()
+            return 0
+
+        lax.fori_loop(0, extra, make, 0)
+        run()
+        for j in range(extra):
+            leave(j).wait()
+
+    operands = [row, order, grads, gate_bands, up_bands, hidden_t, head_bands, head_scale]
+    operands += [summed_scale] + flat
+    specs = [IN_SMEM, IN_SMEM, IN_VMEM, IN_HBM, IN_HBM] + [IN_VMEM] * (4 + len(flat))
+    aliases = None
+    if before is not None:
+        aliases = {len(operands): 1}
+        operands.append(before)
+        specs.append(IN_HBM)
     return call(
-        kernel, [row, grads, gate_bands, up_bands], [IN_SMEM, IN_VMEM, IN_HBM, IN_HBM],
-        [((count, rows, columns), f32)],
-        [pltpu.VMEM((2 * count, columns, width), bf16), pltpu.SemaphoreType.DMA((2 * count,))],
-        4 + 5 * count,
-    )[0]
+        kernel, operands, specs,
+        [((count, rows, columns), f32), ((width, nodes * columns), bf16)],
+        [
+            pltpu.VMEM((2 * count, columns, width), bf16),
+            pltpu.SemaphoreType.DMA((2 * count,)),
+            pltpu.VMEM((extra, width, columns), bf16), pltpu.SemaphoreType.DMA((extra,)),
+            pltpu.VMEM((extra, rows, columns), bf16),
+        ],
+        6 + 4 * count + 3 * extra, aliases, [IN_VMEM, IN_HBM],
+    )
 
 
 def high_low(row):
@@ -747,26 +824,6 @@
     operands = [parts, from_back, from_ahead] + ([] if inner is None else [inner])
     return call(
         kernel, operands, [IN_VMEM] * len(operands), [((rows + tail, columns), bf16)] * 2
-    )
-
-
-def first_messages(far, inner):
-    rows, columns = far.shape[1:]
-    middle = rows // 2
-    tail = 0 if inner is None else AUX
-
-    def kernel(far_ref, *refs):
-        up_out, down_out = refs[-2:]
-        up_out[:middle] = far_ref[0, :middle].astype(bf16)
-        down_out[...] = far_ref[0, middle:].astype(bf16)
-        if tail:
-            pad = jnp.zeros((AUX - 8, columns), f32)
-            up_out[middle:] = jnp.concatenate([high_low(refs[0][...]), pad], axis=0).astype(bf16)
-
-    operands = [far] + ([] if inner is None else [inner])
-    return call(
-        kernel, operands, [IN_VMEM] * len(operands),
-        [((middle + tail, columns), bf16), ((middle, columns), bf16)],
     )
 
 
@@ -833,14 +890,17 @@
     entries, half, columns = kept.shape
 
     def kernel(ids_ref, other_ref, kept_ref, taken_ref, out):
-        for b in range(blocks):
+        def route(b, _):
             sums = []
             for listed, value in ((ids_ref, kept_ref), (other_ref, taken_ref)):
-                total = jnp.zeros((half, columns), f32)
-                for e in range(entries):
-                    total += jnp.where(listed[e] == b, value[e].astype(f32), 0.0)
+                total = sum(
+                    jnp.where(listed[e] == b, value[e].astype(f32), 0.0) for e in range(entries)
+                )
                 sums.append(total.astype(bf16).astype(f32))
             out[b] = (sums[0] + sums[1]).astype(bf16)
+            return 0
+
+        lax.fori_loop(0, blocks, route, 0)
 
     return call(
         kernel, [ids, other_ids, kept, taken], [IN_SMEM, IN_SMEM, IN_VMEM, IN_VMEM],
@@ -894,67 +954,37 @@
     width = grads.shape[2]
 
     def kernel(index_ref, *refs):
-        grads_ref, gate_out, up_out, kept = refs[len(stacks) :]
+        grads_ref, gate_out, up_out, kept, done = refs[len(stacks) :]
 
         @pl.when(pl.program_id(0) == 0)
         def _():
+            copies = []
             start = 0
-            for ref in refs[: len(stacks)]:
-                kept[start : start + ref.shape[0]] = ref[...]
+            for n, ref in enumerate(refs[: len(stacks)]):
+                copies.append(
+                    pltpu.make_async_copy(
+                        ref, kept.at[pl.ds(start, ref.shape[0])], done.at[n]
+                    )
+                )
+                copies[-1].start()
                 start += ref.shape[0]
+            for one in copies:
+                one.wait()
 
         scaled = kept[pl.program_id(0)].T
         gate_out[0] = dot(scaled, grads_ref[0], 1, 0).astype(bf16)
         up_out[0] = dot(scaled, grads_ref[1], 1, 0).astype(bf16)
 
     out = pl.BlockSpec((1, columns, width), lambda b, idx: (idx[b], 0, 0))
+    stacks = [pltpu.with_memory_space_constraint(stack, pltpu.HBM) for stack in stacks]
     return grid_call(
-        kernel, index, list(stacks) + [grads], [IN_VMEM] * (len(stacks) + 1),
+        kernel, index, stacks + [grads], [IN_HBM] * len(stacks) + [IN_VMEM],
         [((nodes, columns, width), bf16)] * 2, [out, out], nodes,
-        [pltpu.VMEM((nodes, rows, columns), bf16)],
-    )
-
-
-def down_grad(index, start, bands, hidden_t, head_bands, head_scale, summed_scale, before):
-    flat = [piece for band in bands for piece in pieces_of(band)]
-    columns = flat[0].shape[1]
-    width, rows = hidden_t.shape
-    nodes = head_bands.shape[0]
-
-    def kernel(index_ref, *refs):
-        hidden_ref, head_ref, head_scale_ref, summed_scale_ref = refs[len(flat) : len(flat) + 4]
-        out, kept = refs[-2:]
-
-        @pl.when(pl.program_id(0) == 0)
-        def _():
-            at = 0
-            for k, band in enumerate(bands):
-                line = 0
-                for _ in pieces_of(band):
-                    size = min(refs[at].shape[0], rows - line)
-                    kept[k, line : line + size] = refs[at][:size]
-                    line += size
-                    at += 1
-
-        step = pl.program_id(0)
-        dsummed = (
-            head_scale_ref[...] * head_ref[index_ref[start + step]]
-            - summed_scale_ref[...] * kept[step].astype(f32)
-        )
-        out[...] = dot(hidden_ref[...], dsummed.astype(bf16), 1, 0).astype(bf16)
-
-    operands = flat + [hidden_t, head_bands, head_scale, summed_scale]
-    specs = [IN_VMEM] * len(operands)
-    aliases = None
-    if before is not None:
-        aliases = {len(operands) + 1: 0}
-        operands.append(before)
-        specs.append(pl.BlockSpec(memory_space=pl.ANY))
-    return grid_call(
-        kernel, index, operands, specs, [((width, nodes * columns), bf16)],
-        [pl.BlockSpec((width, columns), lambda b, idx: (0, idx[start + b]))], len(bands),
-        [pltpu.VMEM((len(bands), rows, columns), bf16)], aliases,
-    )[0]
+        [
+            pltpu.VMEM((nodes, rows, columns), bf16),
+            pltpu.SemaphoreType.DMA((len(stacks),)),
+        ],
+    )
 
 
 def after(values, *others):
@@ -992,7 +1022,7 @@
     near = lax.all_to_all(sent, "fsdp", split_axis=0, concat_axis=0, tiled=True)
     head_parts = jnp.stack(three_terms(gain_head))
     head_down = jnp.sum(contract(head_parts, w_down, 1, 1), axis=0)[None]
-    (near,) = after([near], head_down)
+    near, other_ids = after([near, other_ids], head_down)
     far = lax.ppermute(near, "member", swap)
     band, inverse_in = pick_blocks(ids, member, near, far)
 
@@ -1022,19 +1052,18 @@
 
     scaled = []
 
-    def forward(bands, offsets, total, head=None):
+    def forward(bands, offsets, total, final=None):
         total, new, rest = forward_bands(
-            bands, ring.row, offsets, gain_bands, inverse_in, gate_bands, up_bands, total, head
+            bands, ring.row, offsets, gain_bands, inverse_in, gate_bands, up_bands, total, final
         )
         scaled.append(new)
-        return total if head is None else (total, rest)
+        return total if final is None else (total, rest)
 
     last, last_offsets, total, offsets = gather(band, forward)
     order = ring.visited(offsets, position)
-    (gate_pre, up_pre), (hidden, score) = forward(last, last_offsets, total, head_down)
-
-    far_part = out_parts(ring.row, [half], hidden, w_down, columns)
-    up_message, down_message = first_messages(far_part, None)
+    (gate_pre, up_pre), (hidden, score, up_message, down_message) = forward(
+        last, last_offsets, total, (head_down, w_down)
+    )
     (held,) = after([hidden], up_message)
     back, ahead = ring.up(up_message), ring.down(down_message)
     for step in range(half - 1, 0, -1):
@@ -1058,36 +1087,37 @@
     (held,) = after([hidden], message)
     hidden_t = turned(held)
     last, last_offsets, total, _ = gather(message, backward, hidden_t)
-    _, grads, inner, loss, head_scale, summed_scale = backward(
+    _, grads, inner, loss, head_scale, summed_scale, up_message, down_message = backward(
         last, last_offsets, total,
-        (gate_pre, up_pre, head_down, pair_labels[0], list(messages), entries),
-    )
-
-    far_part = scaled_parts(ring.row, [half], grads, gate_bands, up_bands)
-    up_message, down_message = first_messages(far_part, inner)
+        (
+            gate_pre, up_pre, head_down, pair_labels[0], gate_bands, up_bands, list(messages),
+            entries,
+        ),
+    )
+
     (held,) = after([grads], up_message)
     back, ahead = ring.up(up_message), ring.down(down_message)
+    bounds = [0, 1, 3, 5, nodes]
+
+    def parts_and_down(offsets, held, piece, before):
+        start, stop = bounds[piece], bounds[piece + 1]
+        return scaled_parts(
+            ring.row, offsets, held, gate_bands, up_bands,
+            (
+                order, start, messages[start:stop], hidden_t, head_bands, head_scale,
+                summed_scale, before,
+            ),
+        )
+
     grad_down = None
-    bounds = [0, 3, 6, nodes]
-
-    def grad_down_piece(piece, held_t):
-        start, stop = bounds[piece], bounds[piece + 1]
-        return down_grad(
-            order, start, messages[start:stop], held_t, head_bands, head_scale, summed_scale,
-            grad_down,
+    for step in range(half - 1, 0, -1):
+        parts, grad_down = parts_and_down(
+            [step, nodes - step], held, half - 1 - step, grad_down
         )
-
-    for step in range(half - 1, 0, -1):
-        parts = scaled_parts(ring.row, [step, nodes - step], held, gate_bands, up_bands)
-        if step < half - 1:
-            grad_down = grad_down_piece(half - 2 - step, hidden_t)
-            back, ahead = after([back, ahead], grad_down)
-        held, hidden_t = after([held, hidden_t], back, ahead)
+        (held,) = after([held], back, ahead)
         back, ahead = add_arrivals(parts, back, ahead, inner)
         back, ahead = ring.up(back), ring.down(ahead)
-    own_part = scaled_parts(ring.row, [0], held, gate_bands, up_bands)
-    grad_down = grad_down_piece(2, hidden_t)
-    back, ahead = after([back, ahead], grad_down)
+    own_part, grad_down = parts_and_down([0], held, half - 1, grad_down)
     kept, given, grad_ffn, grad_head, grad_final = finish_rows(
         member, own_part, back, ahead, inner, band, summed_band, inverse_in,
         share(ffn_gain[0]), share(gain_head), head_scale, summed_scale, share(final_gain[0]),

time: 219 us -> 202 us (0.922)
  Pallas kernels: 119 us -> 100 us
  waiting for transfers between devices: 30.2 us -> 40.3 us
  local copies, waits for them, and re-layouts: 13.2 us -> 6.02 us
    pallas_call x4 -> x1, Pallas kernels: 25.5 us -> 13.4 us  [grid_call(): pl.pallas_call(kernel, out_shape=[jax.ShapeDtypeStruct(shape, dtype) for...]
    pallas_call x37 -> x33, Pallas kernels: 93.9 us -> 87 us  [call(): pl.pallas_call(kernel, out_shape=[jax.ShapeDtypeStruct(shape, dtype) for...]
    unnamed x70 -> x60, local copies, waits for them, and re-layouts: 11 us -> 4.54 us
    ppermute x16, waiting for transfers between devices: 11.3 us -> 16.8 us  [up(): return lax.ppermute(value, 'fsdp', self.ahead)]
    ppermute x16, waiting for transfers between devices: 7.5 us -> 10.3 us  [down(): return lax.ppermute(value, 'fsdp', self.back)]
    ppermute x16, starting transfers between devices: 18.8 us -> 16.4 us  [down(): return lax.ppermute(value, 'fsdp', self.back)]
    ppermute x16, starting transfers between devices: 14.2 us -> 16.5 us  [up(): return lax.ppermute(value, 'fsdp', self.ahead)]
  transfers between devices with their start and end apart: 38 -> 38, of which waited for: 19 -> 26; matrix products, arithmetic and copies ran while one was open for 5% -> 5% of each run, Pallas kernels for 43% -> 40%
where the time goes in v2:
time: 202 us
  Pallas kernels  100 us (50%)
  starting transfers between devices  44.3 us (22%)
  waiting for transfers between devices  40.3 us (20%)
  matrix products  9.08 us (4%)
  local copies, waits for them, and re-layouts  6.02 us (3%)
    pallas_call x33, Pallas kernels, call(): pl.pallas_call(kernel, out_shape=[jax.ShapeDtypeStruct(shape, dtype) for...  87 us
    ppermute x16, waiting for transfers between devices, up(): return lax.ppermute(value, 'fsdp', self.ahead)  16.8 us
    ppermute x16, starting transfers between devices, up(): return lax.ppermute(value, 'fsdp', self.ahead)  16.5 us
    ppermute x16, starting transfers between devices, down(): return lax.ppermute(value, 'fsdp', self.back)  16.4 us
    pallas_call x1, Pallas kernels, grid_call(): pl.pallas_call(kernel, out_shape=[jax.ShapeDtypeStruct(shape, dtype) for...  13.4 us
    ppermute x16, waiting for transfers between devices, down(): return lax.ppermute(value, 'fsdp', self.back)  10.3 us
    dot_general x1, matrix products, contract(): lax.dot_general(left, right, (((left_dim,), (right_dim,)), ((), ())), pre...  9.08 us
    all_to_all x1, starting transfers between devices, ring_body(): near = lax.all_to_all(sent, 'fsdp', split_axis=0, concat_axis=0, tiled=True)  7.25 us
  transfers between devices with their start and end apart: 38, of which 26 were waited for; matrix products, arithmetic and copies ran while one was open for 5% of the time, Pallas kernels for 40%

profile of v2, /device:TPU:0, one launch (start us, length us, event | category | flops | bytes accessed | tf_op | source)
XLA Modules:
  0.0 201.5 jit_solution(15821857002735805124)
XLA Ops:
  3.0 7.3 %all-to-all-start = ((bf16[8,144,256]{2,1,0:T(8,128)(2,1)}), bf16[8,144,256]{2,1,0:T(8,128)(2,1)S(1)}, u32[]{:S(2)}, u32[]{:S(2)}) async-start(bf16[8,144,256]{2,1,0:T(8,128)(2,1)} %shard_map.170), calls=%async_computation | async-start | bytes 1179648 | tf_op jit(solution)/shard_map/all_to_all | solution.py:1022
  10.5 9.1 %convolution_reduce_fusion = f32[1792]{0:T(1024)S(1)} fusion(bf16[1,4096]{1,0:T(2,128)(2,1)S(1)} %get-tuple-element.183, bf16[1,4096]{1,0:T(2,128)(2,1)S(1)} %get-tuple-element.182, bf16[1,4096]{1,0:T(2,128)(2,1)S(1)} %get-tuple-element.180, bf16[1,1792,4096]{2,1,0:T(8,128)(2,1)} %param.19), kind=kOutput, calls=%fused_computation | convolution fusion | flops 44117504 | bytes 14711808 | tf_op jit(solution)/shard_map/dot_general | solution.py:30
  19.6 6.6 %all-to-all-done.near_ref = bf16[8,144,256]{2,1,0:T(8,128)(2,1)S(1)} async-done(((bf16[8,144,256]{2,1,0:T(8,128)(2,1)}), bf16[8,144,256]{2,1,0:T(8,128)(2,1)S(1)}, u32[]{:S(2)}, u32[]{:S(2)}) %all-to-all-start) | async-done | bytes 589856 | tf_op jit(solution)/shard_map/all_to_all | solution.py:1022
  31.6 3.5 %shard_map.172 = (f32[256,1792]{1,0:T(8,128)S(1)}, f32[256,1792]{1,0:T(8,128)S(1)}, bf16[1,256,512]{2,1,0:T(8,128)(2,1)S(1)}) custom-call(s32[8]{0:T(128)S(1)} %fusion.6.row_ref, bf16[256,512]{1,0:T(8,128)(2,1)S(1)} %get-tuple-element.95.refs_0_.band_ref, f32[8,1,512]{2,1,0:T(1,128)S(1)} %bitcast.28, ...), custom_call_target="tpu_custom_call" | custom-call | tf_op jit(solution)/shard_map/pallas_call | solution.py:310
  39.7 5.0 %shard_map.173 = (f32[256,1792]{1,0:T(8,128)S(1)}, f32[256,1792]{1,0:T(8,128)S(1)}, bf16[2,256,512]{2,1,0:T(8,128)(2,1)S(1)}) custom-call(s32[8]{0:T(128)S(1)} %fusion.6.row_ref, bf16[256,512]{1,0:T(8,128)(2,1)S(1)} %collective-permute-done.2.refs_0_, ...), custom_call_target="tpu_custom_call", output_to_operand_aliasing={{0}: (7, {}), {1}: (8, {})} | custom-call | tf_op jit(solution)/shard_map/pallas_call | solution.py:310
  47.5 5.0 %shard_map.174 = (f32[256,1792]{1,0:T(8,128)S(1)}, f32[256,1792]{1,0:T(8,128)S(1)}, bf16[2,256,512]{2,1,0:T(8,128)(2,1)S(1)}) custom-call(s32[8]{0:T(128)S(1)} %fusion.6.row_ref, bf16[256,512]{1,0:T(8,128)(2,1)S(1)} %collective-permute-done.4.refs_0_, ...), custom_call_target="tpu_custom_call", output_to_operand_aliasing={{0}: (7, {}), {1}: (8, {})} | custom-call | tf_op jit(solution)/shard_map/pallas_call | solution.py:310
  54.7 5.0 %shard_map.176 = (f32[256,1792]{1,0:T(8,128)S(1)}, f32[256,1792]{1,0:T(8,128)S(1)}, bf16[2,256,512]{2,1,0:T(8,128)(2,1)S(1)}) custom-call(s32[8]{0:T(128)S(1)} %fusion.6.row_ref, bf16[256,512]{1,0:T(8,128)(2,1)S(1)} %collective-permute-done.6.back_ref.refs_0_, ...), custom_call_target="tpu_custom_call", output_to_operand_aliasing={{0}: (7, {}), {1}: (8, {})} | custom-call | tf_op jit(solution)/shard_map/pallas_call | solution.py:310
  59.8 5.3 %shard_map.177 = (f32[256,1792]{1,0:T(8,128)S(1)}, f32[256,1792]{1,0:T(8,128)S(1)}, bf16[1,256,512]{2,1,0:T(8,128)(2,1)S(1)}, bf16[256,1792]{1,0:T(8,128)(2,1)S(...) custom-call(s32[8]{0:T(128)S(1)} %fusion.6.row_ref, ...), custom_call_target="tpu_custom_call", output_to_operand_aliasing={{0}: (7, {}), {1}: (8, {})} | custom-call | tf_op jit(solution)/shard_map/pallas_call | solution.py:310
  67.2 3.3 %shard_map.178.refs_0_ = f32[2,256,512]{2,1,0:T(8,128)S(1)} custom-call(s32[8]{0:T(128)S(1)} %fusion.6.row_ref, bf16[256,1792]{1,0:T(8,128)(2,1)S(1)} %get-tuple-element.128.hidden_ref.value_ref, bf16[1792,4096]{1,0:T(8,128)(2,1)} %bitcast.37), custom_call_target="tpu_custom_call" | custom-call | tf_op jit(solution)/shard_map/pallas_call | solution.py:310
  75.3 3.3 %shard_map.180.refs_0_ = f32[2,256,512]{2,1,0:T(8,128)S(1)} custom-call(s32[8]{0:T(128)S(1)} %fusion.6.row_ref, bf16[256,1792]{1,0:T(8,128)(2,1)S(1)} %get-tuple-element.128.hidden_ref.value_ref, bf16[1792,4096]{1,0:T(8,128)(2,1)} %bitcast.38), custom_call_target="tpu_custom_call" | custom-call | tf_op jit(solution)/shard_map/pallas_call | solution.py:310
  78.6 3.4 %collective-permute-done.12.refs_1_ = bf16[256,512]{1,0:T(8,128)(2,1)S(1)} collective-permute-done((bf16[256,512]{1,0:T(8,128)(2,1)S(1)}, bf16[256,512]{1,0:T(8,128)(2,1)S(1)}, u32[]{:S(2)}, u32[]{:S(2)}) %collective-permute-start.12) | collective-permute-done | bytes 262176 | tf_op jit(solution)/shard_map/ppermute | solution.py:57
  84.9 3.3 %shard_map.183.refs_0_ = f32[2,256,512]{2,1,0:T(8,128)S(1)} custom-call(s32[8]{0:T(128)S(1)} %fusion.6.row_ref, bf16[256,1792]{1,0:T(8,128)(2,1)S(1)} %get-tuple-element.128.hidden_ref.value_ref, bf16[1792,4096]{1,0:T(8,128)(2,1)} %bitcast.39), custom_call_target="tpu_custom_call" | custom-call | tf_op jit(solution)/shard_map/pallas_call | solution.py:310
  88.3 3.0 %collective-permute-done.14.refs_1_ = bf16[256,512]{1,0:T(8,128)(2,1)S(1)} collective-permute-done((bf16[256,512]{1,0:T(8,128)(2,1)S(1)}, bf16[256,512]{1,0:T(8,128)(2,1)S(1)}, u32[]{:S(2)}, u32[]{:S(2)}) %collective-permute-start.14) | collective-permute-done | bytes 262176 | tf_op jit(solution)/shard_map/ppermute | solution.py:57
  97.3 4.0 %collective-permute-done.16.back_ref = bf16[256,512]{1,0:T(8,128)(2,1)S(1)} collective-permute-done((bf16[256,512]{1,0:T(8,128)(2,1)S(1)}, bf16[256,512]{1,0:T(8,128)(2,1)S(1)}, u32[]{:S(2)}, u32[]{:S(2)}) %collective-permute-start.16) | collective-permute-done | bytes 262176 | tf_op jit(solution)/shard_map/ppermute | solution.py:57
  112.9 3.4 %shard_map.188.refs_3_ = f32[256,1792]{1,0:T(8,128)S(1)} custom-call(s32[8]{0:T(128)S(1)} %fusion.6.row_ref, bf16[272,512]{1,0:T(8,128)(2,1)S(1)} %collective-permute-done.18.refs_0_.refs_11_, bf16[272,512]{1,0:T(8,128)(2,1)S(1)} %collective-permute-done.19.refs_1_.refs_12_, bf16[1792,4096]{1,0:T(8,128)(2,1)} %bitcast.42, ...), custom_call_target="tpu_custom_call", output_to_operand_aliasing={{}: (4, {})} | custom-call | tf_op jit(solution)/shard_map/pallas_call | solution.py:310
  120.4 3.4 %shard_map.189.refs_3_ = f32[256,1792]{1,0:T(8,128)S(1)} custom-call(s32[8]{0:T(128)S(1)} %fusion.6.row_ref, bf16[272,512]{1,0:T(8,128)(2,1)S(1)} %collective-permute-done.20.refs_0_.refs_13_, bf16[272,512]{1,0:T(8,128)(2,1)S(1)} %collective-permute-done.21.refs_1_.refs_14_, bf16[1792,4096]{1,0:T(8,128)(2,1)} %bitcast.43, ...), custom_call_target="tpu_custom_call", output_to_operand_aliasing={{}: (4, {})} | custom-call | tf_op jit(solution)/shard_map/pallas_call | solution.py:310
  128.5 3.7 %shard_map.191.refs_3_ = f32[256,1792]{1,0:T(8,128)S(1)} custom-call(s32[8]{0:T(128)S(1)} %fusion.6.row_ref, bf16[272,512]{1,0:T(8,128)(2,1)S(1)} %collective-permute-done.22.back_ref.refs_0_.refs_15_, bf16[272,512]{1,0:T(8,128)(2,1)S(1)} %collective-permute-done.23.ahead_ref.refs_1_.refs_16_, ...), custom_call_target="tpu_custom_call", output_to_operand_aliasing={{}: (4, {})} | custom-call | tf_op jit(solution)/shard_map/pallas_call | solution.py:310
  133.2 7.4 %shard_map.192 = (f32[256,1792]{1,0:T(8,128)S(1)}, bf16[2,256,1792]{2,1,0:T(8,128)(2,1)S(1)}, f32[8,256]{1,0:T(8,128)S(1)}, f32[1,1]{1,0:T(1,128)}, f32[256,1]{1...) custom-call(s32[8]{0:T(128)S(1)} %fusion.6.row_ref, ...), custom_call_target="tpu_custom_call", output_to_operand_aliasing={{0}: (4, {})} | custom-call | tf_op jit(solution)/shard_map/pallas_call | solution.py:310
  143.3 5.8 %shard_map.193 = (f32[2,256,512]{2,1,0:T(8,128)S(1)}, bf16[1792,4096]{1,0:T(8,128)(2,1)}) custom-call(s32[8]{0:T(128)S(1)} %fusion.6.row_ref, s32[8]{0:T(128)S(1)} %fusion.7.order_ref.index_ref, bf16[2,256,1792]{2,1,0:T(8,128)(2,1)S(1)} %get-tuple-element.170.grads_ref.refs_5_, bf16[8,512,1792]{2,1,0:T(8,128)(2,1)} %bitcast.52, ...), custom_call_target="tpu_custom_call" | custom-call | tf_op jit(solution)/shard_map/pallas_call | solution.py:310
  151.3 5.8 %shard_map.195 = (f32[2,256,512]{2,1,0:T(8,128)S(1)}, bf16[1792,4096]{1,0:T(8,128)(2,1)}) custom-call(s32[8]{0:T(128)S(1)} %fusion.6.row_ref, s32[8]{0:T(128)S(1)} %fusion.7.order_ref.index_ref, bf16[2,256,1792]{2,1,0:T(8,128)(2,1)S(1)} %get-tuple-element.170.grads_ref.refs_5_, bf16[8,512,1792]{2,1,0:T(8,128)(2,1)} %bitcast.53, ...), custom_call_target="tpu_custom_call", output_to_operand_aliasing={{1}: (11, {})} | custom-call | tf_op jit(solution)/shard_map/pallas_call | solution.py:310
  161.6 5.8 %shard_map.197 = (f32[2,256,512]{2,1,0:T(8,128)S(1)}, bf16[1792,4096]{1,0:T(8,128)(2,1)}) custom-call(s32[8]{0:T(128)S(1)} %fusion.6.row_ref, s32[8]{0:T(128)S(1)} %fusion.7.order_ref.index_ref, bf16[2,256,1792]{2,1,0:T(8,128)(2,1)S(1)} %get-tuple-element.170.grads_ref.refs_5_, bf16[8,512,1792]{2,1,0:T(8,128)(2,1)} %bitcast.54, ...), custom_call_target="tpu_custom_call", output_to_operand_aliasing={{1}: (11, {})} | custom-call | tf_op jit(solution)/shard_map/pallas_call | solution.py:310
  169.6 4.6 %shard_map.198 = (f32[1,256,512]{2,1,0:T(8,128)S(1)}, bf16[1792,4096]{1,0:T(8,128)(2,1)}) custom-call(s32[8]{0:T(128)S(1)} %fusion.6.row_ref, s32[8]{0:T(128)S(1)} %fusion.7.order_ref.index_ref, bf16[2,256,1792]{2,1,0:T(8,128)(2,1)S(1)} %get-tuple-element.170.grads_ref.refs_5_, bf16[8,512,1792]{2,1,0:T(8,128)(2,1)} %bitcast.55, ...), custom_call_target="tpu_custom_call", output_to_operand_aliasing={{1}: (13, {})} | custom-call | tf_op jit(solution)/shard_map/pallas_call | solution.py:310
  179.7 4.1 %all-to-all-start.1 = ((bf16[8,64,512]{2,1,0:T(8,128)(2,1)}), bf16[8,64,512]{2,1,0:T(8,128)(2,1)S(1)}, u32[]{:S(2)}, u32[]{:S(2)}) async-start(bf16[8,64,512]{2,1,0:T(8,128)(2,1)} %shard_map.202), calls=%async_computation.1 | async-start | bytes 1048576 | tf_op jit(solution)/shard_map/all_to_all | solution.py:1130
  183.8 13.4 %shard_map.201 = (bf16[8,512,1792]{2,1,0:T(8,128)(2,1)}, bf16[8,512,1792]{2,1,0:T(8,128)(2,1)}) custom-call(s32[8]{0:T(128)S(1)} %fusion.7.order_ref.index_ref, bf16[1,256,512]{2,1,0:T(8,128)(2,1)} %copy-done.21, bf16[2,256,512]{2,1,0:T(8,128)(2,1)} %copy-done.15, bf16[2,256,512]{2,1,0:T(8,128)(2,1)} %copy-done.16, bf16[2,256,512]{2,1,0:T(8,128)(2,1)} %copy-done.17, ...), custom_call_target="tpu_custom_call" | custom-call | tf_op jit(solution)/shard_map/pallas_call | solution.py:939
  (156 shorter events, 75.8 us)
Async XLA Ops:
  3.0 23.1 %all-to-all-start = ((bf16[8,144,256]{2,1,0:T(8,128)(2,1)}), bf16[8,144,256]{2,1,0:T(8,128)(2,1)S(1)}, u32[]{:S(2)}, u32[]{:S(2)}) async-start(bf16[8,144,256]{2,1,0:T(8,128)(2,1)} %shard_map.170), calls=%async_computation | async-start | bytes 1179648 | tf_op jit(solution)/shard_map/all_to_all | solution.py:1022
  10.3 9.3 %collective-permute-start = (s32[2]{0:T(128)S(1)}, s32[2]{0:T(128)S(1)}, u32[]{:S(2)}, u32[]{:S(2)}) collective-permute-start(s32[2]{0:T(128)S(1)} %bitcast.33), channel_id=1, source_target_pairs={{0,8},{8,0},{1,9},{9,1},{2,10},{10,2},{3,11},{11,3},{4,12},{12,4},... | collective-permute-start | bytes 32 | tf_op jit(solution)/shard_map/ppermute | solution.py:1020
  28.9 8.4 %collective-permute-start.2 = (bf16[256,512]{1,0:T(8,128)(2,1)S(1)}, bf16[256,512]{1,0:T(8,128)(2,1)S(1)}, u32[]{:S(2)}, u32[]{:S(2)}) collective-permute-start(bf16[256,512]{1,0:T(8,128)(2,1)S(1)} %get-tuple-element.95.refs_0_.band_ref), channel_id=1, source_target_pairs={{0,2},{2,4},{4,6},{6,7},{7,5},{5,3},{3,1},{1,0},{8,10},{10,12},{12... | collective-permute-start | bytes 786440 | tf_op jit(solution)/shard_map/ppermute | solution.py:57
  29.6 8.1 %collective-permute-start.3 = (bf16[256,512]{1,0:T(8,128)(2,1)S(1)}, bf16[256,512]{1,0:T(8,128)(2,1)S(1)}, u32[]{:S(2)}, u32[]{:S(2)}) collective-permute-start(bf16[256,512]{1,0:T(8,128)(2,1)S(1)} %get-tuple-element.95.refs_0_.band_ref), channel_id=1, source_target_pairs={{2,0},{4,2},{6,4},{7,6},{5,7},{3,5},{1,3},{0,1},{10,8},{12,10},{14... | collective-permute-start | bytes 786440 | tf_op jit(solution)/shard_map/ppermute | solution.py:60
  37.7 7.8 %collective-permute-start.4 = (bf16[256,512]{1,0:T(8,128)(2,1)S(1)}, bf16[256,512]{1,0:T(8,128)(2,1)S(1)}, u32[]{:S(2)}, u32[]{:S(2)}) collective-permute-start(bf16[256,512]{1,0:T(8,128)(2,1)S(1)} %collective-permute-done.2.refs_0_), channel_id=1, source_target_pairs={{0,2},{2,4},{4,6},{6,7},{7,5},{5,3},{3,1},{1,0},{8,10},{10,12},{12... | collective-permute-start | bytes 786440 | tf_op jit(solution)/shard_map/ppermute | solution.py:57
  38.0 7.5 %collective-permute-start.5 = (bf16[256,512]{1,0:T(8,128)(2,1)S(1)}, bf16[256,512]{1,0:T(8,128)(2,1)S(1)}, u32[]{:S(2)}, u32[]{:S(2)}) collective-permute-start(bf16[256,512]{1,0:T(8,128)(2,1)S(1)} %collective-permute-done.3.refs_1_), channel_id=1, source_target_pairs={{2,0},{4,2},{6,4},{7,6},{5,7},{3,5},{1,3},{0,1},{10,8},{12,10},{14... | collective-permute-start | bytes 786440 | tf_op jit(solution)/shard_map/ppermute | solution.py:60
  45.5 7.0 %collective-permute-start.6 = (bf16[256,512]{1,0:T(8,128)(2,1)S(1)}, bf16[256,512]{1,0:T(8,128)(2,1)S(1)}, u32[]{:S(2)}, u32[]{:S(2)}) collective-permute-start(bf16[256,512]{1,0:T(8,128)(2,1)S(1)} %collective-permute-done.4.refs_0_), channel_id=1, source_target_pairs={{0,2},{2,4},{4,6},{6,7},{7,5},{5,3},{3,1},{1,0},{8,10},{10,12},{12... | collective-permute-start | bytes 786440 | tf_op jit(solution)/shard_map/ppermute | solution.py:57
  52.6 7.1 %collective-permute-start.8 = (bf16[128,512]{1,0:T(8,128)(2,1)S(1)}, bf16[128,512]{1,0:T(8,128)(2,1)S(1)}, u32[]{:S(2)}, u32[]{:S(2)}) collective-permute-start(bf16[128,512]{1,0:T(8,128)(2,1)S(1)} %get-tuple-element.109), channel_id=1, source_target_pairs={{0,2},{2,4},{4,6},{6,7},{7,5},{5,3},{3,1},{1,0},{8,10},{10,12},{12... | collective-permute-start | bytes 393224 | tf_op jit(solution)/shard_map/ppermute | solution.py:57
  73.2 8.9 %collective-permute-start.12 = (bf16[256,512]{1,0:T(8,128)(2,1)S(1)}, bf16[256,512]{1,0:T(8,128)(2,1)S(1)}, u32[]{:S(2)}, u32[]{:S(2)}) collective-permute-start(bf16[256,512]{1,0:T(8,128)(2,1)S(1)} %get-tuple-element.118), channel_id=1, source_target_pairs={{0,2},{2,4},{4,6},{6,7},{7,5},{5,3},{3,1},{1,0},{8,10},{10,12},{12... | collective-permute-start | bytes 786440 | tf_op jit(solution)/shard_map/ppermute | solution.py:57
  73.9 8.8 %collective-permute-start.13 = (bf16[256,512]{1,0:T(8,128)(2,1)S(1)}, bf16[256,512]{1,0:T(8,128)(2,1)S(1)}, u32[]{:S(2)}, u32[]{:S(2)}) collective-permute-start(bf16[256,512]{1,0:T(8,128)(2,1)S(1)} %get-tuple-element.119), channel_id=1, source_target_pairs={{2,0},{4,2},{6,4},{7,6},{5,7},{3,5},{1,3},{0,1},{10,8},{12,10},{14... | collective-permute-start | bytes 786440 | tf_op jit(solution)/shard_map/ppermute | solution.py:60
  82.8 8.4 %collective-permute-start.14 = (bf16[256,512]{1,0:T(8,128)(2,1)S(1)}, bf16[256,512]{1,0:T(8,128)(2,1)S(1)}, u32[]{:S(2)}, u32[]{:S(2)}) collective-permute-start(bf16[256,512]{1,0:T(8,128)(2,1)S(1)} %get-tuple-element.121), channel_id=1, source_target_pairs={{0,2},{2,4},{4,6},{6,7},{7,5},{5,3},{3,1},{1,0},{8,10},{10,12},{12... | collective-permute-start | bytes 786440 | tf_op jit(solution)/shard_map/ppermute | solution.py:57
  84.0 8.5 %collective-permute-start.15 = (bf16[256,512]{1,0:T(8,128)(2,1)S(1)}, bf16[256,512]{1,0:T(8,128)(2,1)S(1)}, u32[]{:S(2)}, u32[]{:S(2)}) collective-permute-start(bf16[256,512]{1,0:T(8,128)(2,1)S(1)} %get-tuple-element.122), channel_id=1, source_target_pairs={{2,0},{4,2},{6,4},{7,6},{5,7},{3,5},{1,3},{0,1},{10,8},{12,10},{14... | collective-permute-start | bytes 786440 | tf_op jit(solution)/shard_map/ppermute | solution.py:60
  92.6 8.8 %collective-permute-start.16 = (bf16[256,512]{1,0:T(8,128)(2,1)S(1)}, bf16[256,512]{1,0:T(8,128)(2,1)S(1)}, u32[]{:S(2)}, u32[]{:S(2)}) collective-permute-start(bf16[256,512]{1,0:T(8,128)(2,1)S(1)} %get-tuple-element.124), channel_id=1, source_target_pairs={{0,2},{2,4},{4,6},{6,7},{7,5},{5,3},{3,1},{1,0},{8,10},{10,12},{12... | collective-permute-start | bytes 786440 | tf_op jit(solution)/shard_map/ppermute | solution.py:57
  94.4 8.1 %collective-permute-start.17 = (bf16[256,512]{1,0:T(8,128)(2,1)S(1)}, bf16[256,512]{1,0:T(8,128)(2,1)S(1)}, u32[]{:S(2)}, u32[]{:S(2)}) collective-permute-start(bf16[256,512]{1,0:T(8,128)(2,1)S(1)} %get-tuple-element.125), channel_id=1, source_target_pairs={{2,0},{4,2},{6,4},{7,6},{5,7},{3,5},{1,3},{0,1},{10,8},{12,10},{14... | collective-permute-start | bytes 786440 | tf_op jit(solution)/shard_map/ppermute | solution.py:60
  104.3 6.6 %collective-permute-start.19 = (bf16[272,512]{1,0:T(8,128)(2,1)S(1)}, bf16[272,512]{1,0:T(8,128)(2,1)S(1)}, u32[]{:S(2)}, u32[]{:S(2)}) collective-permute-start(bf16[272,512]{1,0:T(8,128)(2,1)S(1)} %get-tuple-element.127.refs_0_.refs_10_), channel_id=1, source_target_pairs={{2,0},{4,2},{6,4},{7,6},{5,7},{3,5},{1,3},{0,1},{10,8},{12,10},{14... | collective-permute-start | bytes 835592 | tf_op jit(solution)/shard_map/ppermute | solution.py:60
  111.3 7.1 %collective-permute-start.21 = (bf16[272,512]{1,0:T(8,128)(2,1)S(1)}, bf16[272,512]{1,0:T(8,128)(2,1)S(1)}, u32[]{:S(2)}, u32[]{:S(2)}) collective-permute-start(bf16[272,512]{1,0:T(8,128)(2,1)S(1)} %collective-permute-done.19.refs_1_.refs_12_), channel_id=1, source_target_pairs={{2,0},{4,2},{6,4},{7,6},{5,7},{3,5},{1,3},{0,1},{10,8},{12,10},{14... | collective-permute-start | bytes 835592 | tf_op jit(solution)/shard_map/ppermute | solution.py:60
  126.4 6.7 %collective-permute-start.25 = (bf16[144,512]{1,0:T(8,128)(2,1)}, bf16[144,512]{1,0:T(8,128)(2,1)}, u32[]{:S(2)}, u32[]{:S(2)}) collective-permute-start(bf16[144,512]{1,0:T(8,128)(2,1)} %get-tuple-element.136), channel_id=1, source_target_pairs={{2,0},{4,2},{6,4},{7,6},{5,7},{3,5},{1,3},{0,1},{10,8},{12,10},{14... | collective-permute-start | bytes 442376 | tf_op jit(solution)/shard_map/ppermute | solution.py:60
  140.5 8.6 %collective-permute-start.26 = (bf16[144,512]{1,0:T(8,128)(2,1)S(1)}, bf16[144,512]{1,0:T(8,128)(2,1)S(1)}, u32[]{:S(2)}, u32[]{:S(2)}) collective-permute-start(bf16[144,512]{1,0:T(8,128)(2,1)S(1)} %get-tuple-element.146), channel_id=1, source_target_pairs={{0,2},{2,4},{4,6},{6,7},{7,5},{5,3},{3,1},{1,0},{8,10},{10,12},{12... | collective-permute-start | bytes 442376 | tf_op jit(solution)/shard_map/ppermute | solution.py:57
  141.7 7.4 %collective-permute-start.27 = (bf16[128,512]{1,0:T(8,128)(2,1)S(1)}, bf16[128,512]{1,0:T(8,128)(2,1)S(1)}, u32[]{:S(2)}, u32[]{:S(2)}) collective-permute-start(bf16[128,512]{1,0:T(8,128)(2,1)S(1)} %get-tuple-element.148), channel_id=1, source_target_pairs={{2,0},{4,2},{6,4},{7,6},{5,7},{3,5},{1,3},{0,1},{10,8},{12,10},{14... | collective-permute-start | bytes 393224 | tf_op jit(solution)/shard_map/ppermute | solution.py:60
  149.2 9.4 %collective-permute-start.28 = (bf16[272,512]{1,0:T(8,128)(2,1)S(1)}, bf16[272,512]{1,0:T(8,128)(2,1)S(1)}, u32[]{:S(2)}, u32[]{:S(2)}) collective-permute-start(bf16[272,512]{1,0:T(8,128)(2,1)S(1)} %get-tuple-element.154), channel_id=1, source_target_pairs={{0,2},{2,4},{4,6},{6,7},{7,5},{5,3},{3,1},{1,0},{8,10},{10,12},{12... | collective-permute-start | bytes 835592 | tf_op jit(solution)/shard_map/ppermute | solution.py:57
  150.5 9.0 %collective-permute-start.29 = (bf16[272,512]{1,0:T(8,128)(2,1)S(1)}, bf16[272,512]{1,0:T(8,128)(2,1)S(1)}, u32[]{:S(2)}, u32[]{:S(2)}) collective-permute-start(bf16[272,512]{1,0:T(8,128)(2,1)S(1)} %get-tuple-element.155), channel_id=1, source_target_pairs={{2,0},{4,2},{6,4},{7,6},{5,7},{3,5},{1,3},{0,1},{10,8},{12,10},{14... | collective-permute-start | bytes 835592 | tf_op jit(solution)/shard_map/ppermute | solution.py:60
  159.5 7.8 %collective-permute-start.30 = (bf16[272,512]{1,0:T(8,128)(2,1)S(1)}, bf16[272,512]{1,0:T(8,128)(2,1)S(1)}, u32[]{:S(2)}, u32[]{:S(2)}) collective-permute-start(bf16[272,512]{1,0:T(8,128)(2,1)S(1)} %get-tuple-element.159), channel_id=1, source_target_pairs={{0,2},{2,4},{4,6},{6,7},{7,5},{5,3},{3,1},{1,0},{8,10},{10,12},{12... | collective-permute-start | bytes 835592 | tf_op jit(solution)/shard_map/ppermute | solution.py:57
  167.5 6.8 %collective-permute-start.32 = (bf16[272,512]{1,0:T(8,128)(2,1)S(1)}, bf16[272,512]{1,0:T(8,128)(2,1)S(1)}, u32[]{:S(2)}, u32[]{:S(2)}) collective-permute-start(bf16[272,512]{1,0:T(8,128)(2,1)S(1)} %get-tuple-element.166), channel_id=1, source_target_pairs={{0,2},{2,4},{4,6},{6,7},{7,5},{5,3},{3,1},{1,0},{8,10},{10,12},{12... | collective-permute-start | bytes 835592 | tf_op jit(solution)/shard_map/ppermute | solution.py:57
  179.7 18.9 %all-to-all-start.1 = ((bf16[8,64,512]{2,1,0:T(8,128)(2,1)}), bf16[8,64,512]{2,1,0:T(8,128)(2,1)S(1)}, u32[]{:S(2)}, u32[]{:S(2)}) async-start(bf16[8,64,512]{2,1,0:T(8,128)(2,1)} %shard_map.202), calls=%async_computation.1 | async-start | bytes 1048576 | tf_op jit(solution)/shard_map/all_to_all | solution.py:1130
  (44 other events, 345.6 us)

commit v3 on v2

--- a/solution.py
+++ b/solution.py
@@ -292,7 +292,8 @@
 
 
 AUX = 16
-STRIPE = 32
+STRIPE = 128
+CHUNK = 256
 IN_SMEM = pl.BlockSpec(memory_space=pltpu.SMEM)
 IN_VMEM = pl.BlockSpec(memory_space=pltpu.VMEM)
 IN_HBM = pl.BlockSpec(memory_space=pltpu.HBM)
@@ -501,13 +502,15 @@
             gate_out, up_out = totals_out
 
             def finish(i, _):
-                part = pl.ds(i * STRIPE, STRIPE)
-                gate = gate_out[part]
-                hidden = (gate * jax.nn.sigmoid(gate) * up_out[part]).astype(bf16)
-                hidden_out[part] = hidden
-                score_out[part] = jnp.sum(
-                    hidden.astype(f32) * head_ref[...], axis=1, keepdims=True
-                )
+                part = pl.ds(pl.multiple_of(i * STRIPE, STRIPE), STRIPE)
+                share = jnp.zeros((STRIPE, CHUNK), f32)
+                for c in range(0, width, CHUNK):
+                    some = slice(c, c + CHUNK)
+                    gate = gate_out[part, some]
+                    hidden = (gate * jax.nn.sigmoid(gate) * up_out[part, some]).astype(bf16)
+                    hidden_out[part, some] = hidden
+                    share += hidden.astype(f32) * head_ref[:, some]
+                score_out[part] = jnp.sum(share, axis=1, keepdims=True)
                 return 0
 
             lax.fori_loop(0, rows // STRIPE, finish, 0)
@@ -631,17 +634,20 @@
             return
 
         def finish(i, _):
-            part = pl.ds(i * STRIPE, STRIPE)
-            gate, up = gate_ref[part], up_ref[part]
-            sigmoid = jax.nn.sigmoid(gate)
-            dhidden = head_scale[part] * head_ref[...] - summed_scale[part] * back_ref[part]
-            dgate = (dhidden * up * sigmoid * (1.0 + gate * (1.0 - sigmoid))).astype(bf16)
-            dup = (dhidden * (gate * sigmoid)).astype(bf16)
-            grads_out[0, part] = dgate
-            grads_out[1, part] = dup
-            inner[part] = jnp.sum(
-                dgate.astype(f32) * gate + dup.astype(f32) * up, axis=1, keepdims=True
-            )
+            part = pl.ds(pl.multiple_of(i * STRIPE, STRIPE), STRIPE)
+            head_factor, summed_factor = head_scale[part], summed_scale[part]
+            share = jnp.zeros((STRIPE, CHUNK), f32)
+            for c in range(0, width, CHUNK):
+                some = slice(c, c + CHUNK)
+                gate, up = gate_ref[part, some], up_ref[part, some]
+                sigmoid = jax.nn.sigmoid(gate)
+                dhidden = head_factor * head_ref[:, some] - summed_factor * back_ref[part, some]
+                dgate = (dhidden * up * sigmoid * (1.0 + gate * (1.0 - sigmoid))).astype(bf16)
+                dup = (dhidden * (gate * sigmoid)).astype(bf16)
+                grads_out[0, part, some] = dgate
+                grads_out[1, part, some] = dup
+                share += dgate.astype(f32) * gate + dup.astype(f32) * up
+            inner[part] = jnp.sum(share, axis=1, keepdims=True)
             return 0
 
         lax.fori_loop(0, rows // STRIPE, finish, 0)
@@ -788,43 +794,33 @@
     return jnp.concatenate([high, row - high], axis=1)
 
 
-def add_arrivals(parts, from_back, from_ahead, inner):
+def add_arrival(parts, way, came, inner):
     rows, columns = parts.shape[1:]
     middle = rows // 2
     tail = 0 if inner is None else AUX
-    early = from_back.shape[0] < rows
-
-    def kernel(*refs):
-        parts_ref, back_ref, ahead_ref = refs[:3]
-        out_up, out_down = refs[-2:]
-        if early:
-            out_up[:middle] = (parts_ref[0, :middle] + back_ref[:middle].astype(f32)).astype(bf16)
-            out_up[middle:rows] = parts_ref[0, middle:].astype(bf16)
-            out_down[:middle] = parts_ref[1, :middle].astype(bf16)
-            out_down[middle:rows] = (
-                parts_ref[1, middle:] + ahead_ref[:middle].astype(f32)
-            ).astype(bf16)
-        else:
-            out_up[:rows] = (parts_ref[0] + back_ref[:rows].astype(f32)).astype(bf16)
-            out_down[:rows] = (parts_ref[1] + ahead_ref[:rows].astype(f32)).astype(bf16)
+    size = min(came.shape[0] // middle * middle, rows)
+    has_inner = came.shape[0] > size
+
+    def kernel(parts_ref, came_ref, *refs):
+        out = refs[-1]
+        start = 0 if size == rows or way == 0 else middle
+        part = slice(start, start + size)
+        out[part] = (parts_ref[way, part] + came_ref[:size].astype(f32)).astype(bf16)
+        if size < rows:
+            rest = slice(middle - start, rows - start)
+            out[rest] = parts_ref[way, rest].astype(bf16)
         if tail:
-            row = refs[3][...]
-            base = middle if early else rows
+            row = refs[0][...]
+            if has_inner:
+                terms = came_ref[size:].astype(f32)[:8]
+                row = row + terms[:, : columns // 2] + terms[:, columns // 2 :]
             pad = jnp.zeros((AUX - 8, columns), f32)
-
-            def carry(ref):
-                came = ref[base:].astype(f32)[:8]
-                return row + came[:, : columns // 2] + came[:, columns // 2 :]
-
-            up_row = carry(back_ref)
-            down_row = row if early else carry(ahead_ref)
-            out_up[rows:] = jnp.concatenate([high_low(up_row), pad], axis=0).astype(bf16)
-            out_down[rows:] = jnp.concatenate([high_low(down_row), pad], axis=0).astype(bf16)
-
-    operands = [parts, from_back, from_ahead] + ([] if inner is None else [inner])
+            out[rows:] = jnp.concatenate([high_low(row), pad], axis=0).astype(bf16)
+
+    operands = [parts, came] + ([] if inner is None else [inner])
     return call(
-        kernel, operands, [IN_VMEM] * len(operands), [((rows + tail, columns), bf16)] * 2
-    )
+        kernel, operands, [IN_VMEM] * len(operands), [((rows + tail, columns), bf16)]
+    )[0]
 
 
 def finish_summed(own, from_back, from_ahead, band, head_row, score):
@@ -1022,7 +1018,16 @@
     near = lax.all_to_all(sent, "fsdp", split_axis=0, concat_axis=0, tiled=True)
     head_parts = jnp.stack(three_terms(gain_head))
     head_down = jnp.sum(contract(head_parts, w_down, 1, 1), axis=0)[None]
-    near, other_ids = after([near, other_ids], head_down)
+    visits = [0]
+    for step in range(1, half):
+        visits += [nodes - step, step]
+    order = ring.visited(visits + [half], position)
+    gain_row, head_row, final_row, score_row = (
+        share(vector) for vector in (ffn_gain[0], gain_head, final_gain[0], score_head[0])
+    )
+    near, other_ids, ring.row, order, gain_row, head_row, final_row, score_row = after(
+        [near, other_ids, ring.row, order, gain_row, head_row, final_row, score_row], head_down
+    )
     far = lax.ppermute(near, "member", swap)
     band, inverse_in = pick_blocks(ids, member, near, far)
 
@@ -1044,7 +1049,7 @@
                 done = list(total)
                 if step == 1 and extra is not None:
                     done.append(extra)
-                back, ahead = after([back, ahead], *done)
+                (back,), (ahead,) = after([back], *done), after([ahead], *done)
                 arrived = [back, ahead]
             pending, pending_offsets = arrived, offsets
         order += pending_offsets
@@ -1059,8 +1064,7 @@
         scaled.append(new)
         return total if final is None else (total, rest)
 
-    last, last_offsets, total, offsets = gather(band, forward)
-    order = ring.visited(offsets, position)
+    last, last_offsets, total, _ = gather(band, forward)
     (gate_pre, up_pre), (hidden, score, up_message, down_message) = forward(
         last, last_offsets, total, (head_down, w_down)
     )
@@ -1069,11 +1073,11 @@
     for step in range(half - 1, 0, -1):
         parts = out_parts(ring.row, [step, nodes - step], held, w_down, columns)
         (held,) = after([held], back, ahead)
-        back, ahead = add_arrivals(parts, back, ahead, None)
-        back, ahead = ring.up(back), ring.down(ahead)
+        back = ring.up(add_arrival(parts, 0, back, None))
+        ahead = ring.down(add_arrival(parts, 1, ahead, None))
     own_part = out_parts(ring.row, [0], held, w_down, columns)
     summed_band, message = finish_summed(
-        own_part, back, ahead, band, share(gain_head), score
+        own_part, back, ahead, band, head_row, score
     )
 
     messages = []
@@ -1115,13 +1119,12 @@
             [step, nodes - step], held, half - 1 - step, grad_down
         )
         (held,) = after([held], back, ahead)
-        back, ahead = add_arrivals(parts, back, ahead, inner)
-        back, ahead = ring.up(back), ring.down(ahead)
+        back = ring.up(add_arrival(parts, 0, back, inner))
+        ahead = ring.down(add_arrival(parts, 1, ahead, inner))
     own_part, grad_down = parts_and_down([0], held, half - 1, grad_down)
     kept, given, grad_ffn, grad_head, grad_final = finish_rows(
         member, own_part, back, ahead, inner, band, summed_band, inverse_in,
-        share(ffn_gain[0]), share(gain_head), head_scale, summed_scale, share(final_gain[0]),
-        share(score_head[0]), entries, width,
+        gain_row, head_row, head_scale, summed_scale, final_row, score_row, entries, width,
     )
 
     (held,) = after([grads], given)

time: 202 us -> 193 us (0.955)
  waiting for transfers between devices: 40.3 us -> 35.3 us
  local copies, waits for them, and re-layouts: 6.02 us -> 3.67 us
    ppermute x16, starting transfers between devices: 16.4 us -> 24 us  [down(): return lax.ppermute(value, 'fsdp', self.back)]
    ppermute x16, starting transfers between devices: 16.5 us -> 9.09 us  [up(): return lax.ppermute(value, 'fsdp', self.ahead)]
    ppermute x16, waiting for transfers between devices: 10.3 us -> 4.67 us  [down(): return lax.ppermute(value, 'fsdp', self.back)]
    pallas_call x33 -> x39, Pallas kernels: 87 us -> 85.1 us  [call(): pl.pallas_call(kernel, out_shape=[jax.ShapeDtypeStruct(shape, dtype) for...]
    unnamed x60 -> x68, local copies, waits for them, and re-layouts: 4.54 us -> 2.84 us
  transfers between devices with their start and end apart: 38 -> 38, of which waited for: 26 -> 21; matrix products, arithmetic and copies ran while one was open for 5% -> 5% of each run, Pallas kernels for 40% -> 42%
where the time goes in v3:
time: 193 us; the launch traced here: 192 us
  Pallas kernels  98.6 us (51%)
  starting transfers between devices  43.9 us (23%)
  waiting for transfers between devices  35.3 us (18%)
  matrix products  9.08 us (5%)
  local copies, waits for them, and re-layouts  3.67 us (2%)
    pallas_call x39, Pallas kernels, call(): pl.pallas_call(kernel, out_shape=[jax.ShapeDtypeStruct(shape, dtype) for...  85.1 us
    ppermute x16, starting transfers between devices, down(): return lax.ppermute(value, 'fsdp', self.back)  24 us
    ppermute x16, waiting for transfers between devices, up(): return lax.ppermute(value, 'fsdp', self.ahead)  18 us
    pallas_call x1, Pallas kernels, grid_call(): pl.pallas_call(kernel, out_shape=[jax.ShapeDtypeStruct(shape, dtype) for...  13.4 us
    ppermute x16, starting transfers between devices, up(): return lax.ppermute(value, 'fsdp', self.ahead)  9.09 us
    dot_general x1, matrix products, contract(): lax.dot_general(left, right, (((left_dim,), (right_dim,)), ((), ())), pre...  9.08 us
    all_to_all x1, starting transfers between devices, ring_body(): near = lax.all_to_all(sent, 'fsdp', split_axis=0, concat_axis=0, tiled=True)  7.25 us
    all_to_all x1, waiting for transfers between devices, ring_body(): near = lax.all_to_all(sent, 'fsdp', split_axis=0, concat_axis=0, tiled=True)  5.83 us
  transfers between devices with their start and end apart: 38, of which 21 were waited for; matrix products, arithmetic and copies ran while one was open for 5% of the time, Pallas kernels for 42%

profile of v3, /device:TPU:0, one launch (start us, length us, event | category | flops | bytes accessed | tf_op | source)
XLA Modules:
  0.0 192.0 jit_solution(9754810752872277093)
XLA Ops:
  3.0 7.3 %all-to-all-start = ((bf16[8,144,256]{2,1,0:T(8,128)(2,1)}), bf16[8,144,256]{2,1,0:T(8,128)(2,1)S(1)}, u32[]{:S(2)}, u32[]{:S(2)}) async-start(bf16[8,144,256]{2,1,0:T(8,128)(2,1)} %shard_map.170), calls=%async_computation | async-start | bytes 1179648 | tf_op jit(solution)/shard_map/all_to_all | solution.py:1018
  10.5 9.1 %convolution_reduce_fusion = f32[1792]{0:T(1024)S(1)} fusion(bf16[1,4096]{1,0:T(2,128)(2,1)S(1)} %get-tuple-element.171, bf16[1,4096]{1,0:T(2,128)(2,1)S(1)} %get-tuple-element.170, bf16[1,4096]{1,0:T(2,128)(2,1)S(1)} %get-tuple-element.168, bf16[1,1792,4096]{2,1,0:T(8,128)(2,1)} %param.19), kind=kOutput, calls=%fused_computation | convolution fusion | flops 44117504 | bytes 14711808 | tf_op jit(solution)/shard_map/dot_general | solution.py:30
  20.3 5.8 %all-to-all-done.near_ref = bf16[8,144,256]{2,1,0:T(8,128)(2,1)S(1)} async-done(((bf16[8,144,256]{2,1,0:T(8,128)(2,1)}), bf16[8,144,256]{2,1,0:T(8,128)(2,1)S(1)}, u32[]{:S(2)}, u32[]{:S(2)}) %all-to-all-start) | async-done | bytes 589856 | tf_op jit(solution)/shard_map/all_to_all | solution.py:1018
  30.9 3.5 %shard_map.172 = (f32[256,1792]{1,0:T(8,128)S(1)}, f32[256,1792]{1,0:T(8,128)S(1)}, bf16[1,256,512]{2,1,0:T(8,128)(2,1)S(1)}) custom-call(s32[8]{0:T(128)S(1)} %get-tuple-element.88.row_ref, bf16[256,512]{1,0:T(8,128)(2,1)S(1)} %get-tuple-element.90.refs_0_.band_ref, f32[8,1,512]{2,1,0:T(1,128)S(1)} %bitcast.28, ...), custom_call_target="tpu_custom_call" | custom-call | tf_op jit(solution)/shard_map/pallas_call | solution.py:311
  39.3 4.9 %shard_map.173 = (f32[256,1792]{1,0:T(8,128)S(1)}, f32[256,1792]{1,0:T(8,128)S(1)}, bf16[2,256,512]{2,1,0:T(8,128)(2,1)S(1)}) custom-call(s32[8]{0:T(128)S(1)} %get-tuple-element.88.row_ref, bf16[256,512]{1,0:T(8,128)(2,1)S(1)} %collective-permute-done.2.refs_0_, ...), custom_call_target="tpu_custom_call", output_to_operand_aliasing={{0}: (7, {}), {1}: (8, {})} | custom-call | tf_op jit(solution)/shard_map/pallas_call | solution.py:311
  47.0 4.9 %shard_map.174 = (f32[256,1792]{1,0:T(8,128)S(1)}, f32[256,1792]{1,0:T(8,128)S(1)}, bf16[2,256,512]{2,1,0:T(8,128)(2,1)S(1)}) custom-call(s32[8]{0:T(128)S(1)} %get-tuple-element.88.row_ref, bf16[256,512]{1,0:T(8,128)(2,1)S(1)} %collective-permute-done.3.refs_0_, ...), custom_call_target="tpu_custom_call", output_to_operand_aliasing={{0}: (7, {}), {1}: (8, {})} | custom-call | tf_op jit(solution)/shard_map/pallas_call | solution.py:311
  54.5 4.9 %shard_map.176 = (f32[256,1792]{1,0:T(8,128)S(1)}, f32[256,1792]{1,0:T(8,128)S(1)}, bf16[2,256,512]{2,1,0:T(8,128)(2,1)S(1)}) custom-call(s32[8]{0:T(128)S(1)} %get-tuple-element.88.row_ref, bf16[256,512]{1,0:T(8,128)(2,1)S(1)} %collective-permute-done.5.back_ref.refs_0_, ...), custom_call_target="tpu_custom_call", output_to_operand_aliasing={{0}: (7, {}), {1}: (8, {})} | custom-call | tf_op jit(solution)/shard_map/pallas_call | solution.py:311
  59.4 4.8 %shard_map.177 = (f32[256,1792]{1,0:T(8,128)S(1)}, f32[256,1792]{1,0:T(8,128)S(1)}, bf16[1,256,512]{2,1,0:T(8,128)(2,1)S(1)}, bf16[256,1792]{1,0:T(8,128)(2,1)S(...) custom-call(s32[8]{0:T(128)S(1)} %get-tuple-element.88.row_ref, ...), custom_call_target="tpu_custom_call", output_to_operand_aliasing={{0}: (7, {}), {1}: (8, {})} | custom-call | tf_op jit(solution)/shard_map/pallas_call | solution.py:311
  66.4 3.3 %shard_map.178.parts_ref = f32[2,256,512]{2,1,0:T(8,128)S(1)} custom-call(s32[8]{0:T(128)S(1)} %get-tuple-element.88.row_ref, bf16[256,1792]{1,0:T(8,128)(2,1)S(1)} %get-tuple-element.118.hidden_ref.value_ref, bf16[1792,4096]{1,0:T(8,128)(2,1)} %bitcast.37), custom_call_target="tpu_custom_call" | custom-call | tf_op jit(solution)/shard_map/pallas_call | solution.py:311
  72.0 3.3 %shard_map.181.parts_ref = f32[2,256,512]{2,1,0:T(8,128)S(1)} custom-call(s32[8]{0:T(128)S(1)} %get-tuple-element.88.row_ref, bf16[256,1792]{1,0:T(8,128)(2,1)S(1)} %get-tuple-element.118.hidden_ref.value_ref, bf16[1792,4096]{1,0:T(8,128)(2,1)} %bitcast.38), custom_call_target="tpu_custom_call" | custom-call | tf_op jit(solution)/shard_map/pallas_call | solution.py:311
  80.0 3.3 %shard_map.185.parts_ref = f32[2,256,512]{2,1,0:T(8,128)S(1)} custom-call(s32[8]{0:T(128)S(1)} %get-tuple-element.88.row_ref, bf16[256,1792]{1,0:T(8,128)(2,1)S(1)} %get-tuple-element.118.hidden_ref.value_ref, bf16[1792,4096]{1,0:T(8,128)(2,1)} %bitcast.39), custom_call_target="tpu_custom_call" | custom-call | tf_op jit(solution)/shard_map/pallas_call | solution.py:311
  83.4 3.1 %collective-permute-done.14.came_ref = bf16[256,512]{1,0:T(8,128)(2,1)S(1)} collective-permute-done((bf16[256,512]{1,0:T(8,128)(2,1)S(1)}, bf16[256,512]{1,0:T(8,128)(2,1)S(1)}, u32[]{:S(2)}, u32[]{:S(2)}) %collective-permute-start.14) | collective-permute-done | bytes 262176 | tf_op jit(solution)/shard_map/ppermute | solution.py:57
  92.0 3.1 %collective-permute-done.16.back_ref = bf16[256,512]{1,0:T(8,128)(2,1)S(1)} collective-permute-done((bf16[256,512]{1,0:T(8,128)(2,1)S(1)}, bf16[256,512]{1,0:T(8,128)(2,1)S(1)}, u32[]{:S(2)}, u32[]{:S(2)}) %collective-permute-start.16) | collective-permute-done | bytes 262176 | tf_op jit(solution)/shard_map/ppermute | solution.py:57
  99.6 2.8 %shard_map.189.refs_3_ = f32[256,1792]{1,0:T(8,128)S(1)} custom-call(s32[8]{0:T(128)S(1)} %get-tuple-element.88.row_ref, bf16[272,512]{1,0:T(8,128)(2,1)S(1)} %get-tuple-element.117.refs_0_.refs_10_, bf16[1792,4096]{1,0:T(8,128)(2,1)} %bitcast.41), custom_call_target="tpu_custom_call" | custom-call | tf_op jit(solution)/shard_map/pallas_call | solution.py:311
  107.1 3.4 %shard_map.191.refs_3_ = f32[256,1792]{1,0:T(8,128)S(1)} custom-call(s32[8]{0:T(128)S(1)} %get-tuple-element.88.row_ref, bf16[272,512]{1,0:T(8,128)(2,1)S(1)} %collective-permute-done.18.refs_0_.refs_11_, bf16[272,512]{1,0:T(8,128)(2,1)S(1)} %collective-permute-done.20.refs_1_.refs_12_, bf16[1792,4096]{1,0:T(8,128)(2,1)} %bitcast.42, ...), custom_call_target="tpu_custom_call", output_to_operand_aliasing={{}: (4, {})} | custom-call | tf_op jit(solution)/shard_map/pallas_call | solution.py:311
  113.7 3.4 %shard_map.192.refs_3_ = f32[256,1792]{1,0:T(8,128)S(1)} custom-call(s32[8]{0:T(128)S(1)} %get-tuple-element.88.row_ref, bf16[272,512]{1,0:T(8,128)(2,1)S(1)} %collective-permute-done.19.refs_0_.refs_13_, bf16[272,512]{1,0:T(8,128)(2,1)S(1)} %collective-permute-done.22.refs_1_.refs_14_, bf16[1792,4096]{1,0:T(8,128)(2,1)} %bitcast.43, ...), custom_call_target="tpu_custom_call", output_to_operand_aliasing={{}: (4, {})} | custom-call | tf_op jit(solution)/shard_map/pallas_call | solution.py:311
  121.9 3.7 %shard_map.194.refs_3_ = f32[256,1792]{1,0:T(8,128)S(1)} custom-call(s32[8]{0:T(128)S(1)} %get-tuple-element.88.row_ref, bf16[272,512]{1,0:T(8,128)(2,1)S(1)} %collective-permute-done.21.back_ref.refs_0_.refs_15_, bf16[272,512]{1,0:T(8,128)(2,1)S(1)} %collective-permute-done.23.ahead_ref.refs_1_.refs_16_, ...), custom_call_target="tpu_custom_call", output_to_operand_aliasing={{}: (4, {})} | custom-call | tf_op jit(solution)/shard_map/pallas_call | solution.py:311
  127.3 6.3 %shard_map.195 = (f32[256,1792]{1,0:T(8,128)S(1)}, bf16[2,256,1792]{2,1,0:T(8,128)(2,1)S(1)}, f32[8,256]{1,0:T(8,128)S(1)}, f32[1,1]{1,0:T(1,128)}, f32[256,1]{1...) custom-call(s32[8]{0:T(128)S(1)} %get-tuple-element.88.row_ref, ...), custom_call_target="tpu_custom_call", output_to_operand_aliasing={{0}: (4, {})} | custom-call | tf_op jit(solution)/shard_map/pallas_call | solution.py:311
  135.7 5.8 %shard_map.196 = (f32[2,256,512]{2,1,0:T(8,128)S(1)}, bf16[1792,4096]{1,0:T(8,128)(2,1)}) custom-call(s32[8]{0:T(128)S(1)} %get-tuple-element.88.row_ref, s32[8]{0:T(128)S(1)} %get-tuple-element.130.order_ref.index_ref, bf16[2,256,1792]{2,1,0:T(8,128)(2,1)S(1)} %get-tuple-element.158.grads_ref.refs_5_, bf16[8,512,1792]{2,1,0:T(8,128)(2,1)} %bitcast.52, ...), custom_call_target="tpu_custom_call" | custom-call | tf_op jit(solution)/shard_map/pallas_call | solution.py:311
  143.7 5.8 %shard_map.199 = (f32[2,256,512]{2,1,0:T(8,128)S(1)}, bf16[1792,4096]{1,0:T(8,128)(2,1)}) custom-call(s32[8]{0:T(128)S(1)} %get-tuple-element.88.row_ref, s32[8]{0:T(128)S(1)} %get-tuple-element.130.order_ref.index_ref, bf16[2,256,1792]{2,1,0:T(8,128)(2,1)S(1)} %get-tuple-element.158.grads_ref.refs_5_, ...), custom_call_target="tpu_custom_call", output_to_operand_aliasing={{1}: (11, {})} | custom-call | tf_op jit(solution)/shard_map/pallas_call | solution.py:311
  151.8 5.8 %shard_map.202 = (f32[2,256,512]{2,1,0:T(8,128)S(1)}, bf16[1792,4096]{1,0:T(8,128)(2,1)}) custom-call(s32[8]{0:T(128)S(1)} %get-tuple-element.88.row_ref, s32[8]{0:T(128)S(1)} %get-tuple-element.130.order_ref.index_ref, bf16[2,256,1792]{2,1,0:T(8,128)(2,1)S(1)} %get-tuple-element.158.grads_ref.refs_5_, ...), custom_call_target="tpu_custom_call", output_to_operand_aliasing={{1}: (11, {})} | custom-call | tf_op jit(solution)/shard_map/pallas_call | solution.py:311
  159.8 4.6 %shard_map.203 = (f32[1,256,512]{2,1,0:T(8,128)S(1)}, bf16[1792,4096]{1,0:T(8,128)(2,1)}) custom-call(s32[8]{0:T(128)S(1)} %get-tuple-element.88.row_ref, s32[8]{0:T(128)S(1)} %get-tuple-element.130.order_ref.index_ref, bf16[2,256,1792]{2,1,0:T(8,128)(2,1)S(1)} %get-tuple-element.158.grads_ref.refs_5_, ...), custom_call_target="tpu_custom_call", output_to_operand_aliasing={{1}: (13, {})} | custom-call | tf_op jit(solution)/shard_map/pallas_call | solution.py:311
  170.6 3.5 %all-to-all-start.1 = ((bf16[8,64,512]{2,1,0:T(8,128)(2,1)}), bf16[8,64,512]{2,1,0:T(8,128)(2,1)S(1)}, u32[]{:S(2)}, u32[]{:S(2)}) async-start(bf16[8,64,512]{2,1,0:T(8,128)(2,1)} %shard_map.208), calls=%async_computation.1 | async-start | bytes 1048576 | tf_op jit(solution)/shard_map/all_to_all | solution.py:1133
  174.1 13.4 %shard_map.207 = (bf16[8,512,1792]{2,1,0:T(8,128)(2,1)}, bf16[8,512,1792]{2,1,0:T(8,128)(2,1)}) custom-call(s32[8]{0:T(128)S(1)} %get-tuple-element.130.order_ref.index_ref, bf16[1,256,512]{2,1,0:T(8,128)(2,1)} %copy-done.25, bf16[2,256,512]{2,1,0:T(8,128)(2,1)} %copy-done.19, bf16[2,256,512]{2,1,0:T(8,128)(2,1)} %copy-done.20, ...), custom_call_target="tpu_custom_call" | custom-call | tf_op jit(solution)/shard_map/pallas_call | solution.py:935
  (168 shorter events, 70.7 us)
Async XLA Ops:
  3.0 23.1 %all-to-all-start = ((bf16[8,144,256]{2,1,0:T(8,128)(2,1)}), bf16[8,144,256]{2,1,0:T(8,128)(2,1)S(1)}, u32[]{:S(2)}, u32[]{:S(2)}) async-start(bf16[8,144,256]{2,1,0:T(8,128)(2,1)} %shard_map.170), calls=%async_computation | async-start | bytes 1179648 | tf_op jit(solution)/shard_map/all_to_all | solution.py:1018
  10.3 10.0 %collective-permute-start = (s32[2]{0:T(128)S(1)}, s32[2]{0:T(128)S(1)}, u32[]{:S(2)}, u32[]{:S(2)}) collective-permute-start(s32[2]{0:T(128)S(1)} %bitcast.33), channel_id=1, source_target_pairs={{0,8},{8,0},{1,9},{9,1},{2,10},{10,2},{3,11},{11,3},{4,12},{12,4},... | collective-permute-start | bytes 32 | tf_op jit(solution)/shard_map/ppermute | solution.py:1016
  28.9 8.4 %collective-permute-start.2 = (bf16[256,512]{1,0:T(8,128)(2,1)S(1)}, bf16[256,512]{1,0:T(8,128)(2,1)S(1)}, u32[]{:S(2)}, u32[]{:S(2)}) collective-permute-start(bf16[256,512]{1,0:T(8,128)(2,1)S(1)} %get-tuple-element.90.refs_0_.band_ref), channel_id=1, source_target_pairs={{0,2},{2,4},{4,6},{6,7},{7,5},{5,3},{3,1},{1,0},{8,10},{10,12},{12... | collective-permute-start | bytes 786440 | tf_op jit(solution)/shard_map/ppermute | solution.py:57
  29.6 8.4 %collective-permute-start.4 = (bf16[256,512]{1,0:T(8,128)(2,1)S(1)}, bf16[256,512]{1,0:T(8,128)(2,1)S(1)}, u32[]{:S(2)}, u32[]{:S(2)}) collective-permute-start(bf16[256,512]{1,0:T(8,128)(2,1)S(1)} %get-tuple-element.90.refs_0_.band_ref), channel_id=1, source_target_pairs={{2,0},{4,2},{6,4},{7,6},{5,7},{3,5},{1,3},{0,1},{10,8},{12,10},{14... | collective-permute-start | bytes 786440 | tf_op jit(solution)/shard_map/ppermute | solution.py:60
  37.3 7.8 %collective-permute-start.3 = (bf16[256,512]{1,0:T(8,128)(2,1)S(1)}, bf16[256,512]{1,0:T(8,128)(2,1)S(1)}, u32[]{:S(2)}, u32[]{:S(2)}) collective-permute-start(bf16[256,512]{1,0:T(8,128)(2,1)S(1)} %collective-permute-done.2.refs_0_), channel_id=1, source_target_pairs={{0,2},{2,4},{4,6},{6,7},{7,5},{5,3},{3,1},{1,0},{8,10},{10,12},{12... | collective-permute-start | bytes 786440 | tf_op jit(solution)/shard_map/ppermute | solution.py:57
  37.9 7.8 %collective-permute-start.6 = (bf16[256,512]{1,0:T(8,128)(2,1)S(1)}, bf16[256,512]{1,0:T(8,128)(2,1)S(1)}, u32[]{:S(2)}, u32[]{:S(2)}) collective-permute-start(bf16[256,512]{1,0:T(8,128)(2,1)S(1)} %collective-permute-done.4.refs_1_), channel_id=1, source_target_pairs={{2,0},{4,2},{6,4},{7,6},{5,7},{3,5},{1,3},{0,1},{10,8},{12,10},{14... | collective-permute-start | bytes 786440 | tf_op jit(solution)/shard_map/ppermute | solution.py:60
  52.4 7.0 %collective-permute-start.8 = (bf16[128,512]{1,0:T(8,128)(2,1)S(1)}, bf16[128,512]{1,0:T(8,128)(2,1)S(1)}, u32[]{:S(2)}, u32[]{:S(2)}) collective-permute-start(bf16[128,512]{1,0:T(8,128)(2,1)S(1)} %get-tuple-element.104), channel_id=1, source_target_pairs={{0,2},{2,4},{4,6},{6,7},{7,5},{5,3},{3,1},{1,0},{8,10},{10,12},{12... | collective-permute-start | bytes 393224 | tf_op jit(solution)/shard_map/ppermute | solution.py:57
  69.8 7.7 %collective-permute-start.12 = (bf16[256,512]{1,0:T(8,128)(2,1)S(1)}, bf16[256,512]{1,0:T(8,128)(2,1)S(1)}, u32[]{:S(2)}, u32[]{:S(2)}) collective-permute-start(bf16[256,512]{1,0:T(8,128)(2,1)S(1)} %shard_map.179), channel_id=1, source_target_pairs={{0,2},{2,4},{4,6},{6,7},{7,5},{5,3},{3,1},{1,0},{8,10},{10,12},{12... | collective-permute-start | bytes 786440 | tf_op jit(solution)/shard_map/ppermute | solution.py:57
  70.5 8.1 %collective-permute-start.13 = (bf16[256,512]{1,0:T(8,128)(2,1)S(1)}, bf16[256,512]{1,0:T(8,128)(2,1)S(1)}, u32[]{:S(2)}, u32[]{:S(2)}) collective-permute-start(bf16[256,512]{1,0:T(8,128)(2,1)S(1)} %shard_map.180), channel_id=1, source_target_pairs={{2,0},{4,2},{6,4},{7,6},{5,7},{3,5},{1,3},{0,1},{10,8},{12,10},{14... | collective-permute-start | bytes 786440 | tf_op jit(solution)/shard_map/ppermute | solution.py:60
  77.6 9.0 %collective-permute-start.14 = (bf16[256,512]{1,0:T(8,128)(2,1)S(1)}, bf16[256,512]{1,0:T(8,128)(2,1)S(1)}, u32[]{:S(2)}, u32[]{:S(2)}) collective-permute-start(bf16[256,512]{1,0:T(8,128)(2,1)S(1)} %shard_map.182), channel_id=1, source_target_pairs={{0,2},{2,4},{4,6},{6,7},{7,5},{5,3},{3,1},{1,0},{8,10},{10,12},{12... | collective-permute-start | bytes 786440 | tf_op jit(solution)/shard_map/ppermute | solution.py:57
  78.6 9.2 %collective-permute-start.15 = (bf16[256,512]{1,0:T(8,128)(2,1)S(1)}, bf16[256,512]{1,0:T(8,128)(2,1)S(1)}, u32[]{:S(2)}, u32[]{:S(2)}) collective-permute-start(bf16[256,512]{1,0:T(8,128)(2,1)S(1)} %shard_map.183), channel_id=1, source_target_pairs={{2,0},{4,2},{6,4},{7,6},{5,7},{3,5},{1,3},{0,1},{10,8},{12,10},{14... | collective-permute-start | bytes 786440 | tf_op jit(solution)/shard_map/ppermute | solution.py:60
  86.6 8.4 %collective-permute-start.16 = (bf16[256,512]{1,0:T(8,128)(2,1)S(1)}, bf16[256,512]{1,0:T(8,128)(2,1)S(1)}, u32[]{:S(2)}, u32[]{:S(2)}) collective-permute-start(bf16[256,512]{1,0:T(8,128)(2,1)S(1)} %shard_map.186), channel_id=1, source_target_pairs={{0,2},{2,4},{4,6},{6,7},{7,5},{5,3},{3,1},{1,0},{8,10},{10,12},{12... | collective-permute-start | bytes 786440 | tf_op jit(solution)/shard_map/ppermute | solution.py:57
  87.9 9.2 %collective-permute-start.17 = (bf16[256,512]{1,0:T(8,128)(2,1)S(1)}, bf16[256,512]{1,0:T(8,128)(2,1)S(1)}, u32[]{:S(2)}, u32[]{:S(2)}) collective-permute-start(bf16[256,512]{1,0:T(8,128)(2,1)S(1)} %shard_map.187), channel_id=1, source_target_pairs={{2,0},{4,2},{6,4},{7,6},{5,7},{3,5},{1,3},{0,1},{10,8},{12,10},{14... | collective-permute-start | bytes 786440 | tf_op jit(solution)/shard_map/ppermute | solution.py:60
  97.5 7.2 %collective-permute-start.18 = (bf16[272,512]{1,0:T(8,128)(2,1)S(1)}, bf16[272,512]{1,0:T(8,128)(2,1)S(1)}, u32[]{:S(2)}, u32[]{:S(2)}) collective-permute-start(bf16[272,512]{1,0:T(8,128)(2,1)S(1)} %get-tuple-element.117.refs_0_.refs_10_), channel_id=1, source_target_pairs={{0,2},{2,4},{4,6},{6,7},{7,5},{5,3},{3,1},{1,0},{8,10},{10,12},{12... | collective-permute-start | bytes 835592 | tf_op jit(solution)/shard_map/ppermute | solution.py:57
  97.6 8.2 %collective-permute-start.20 = (bf16[272,512]{1,0:T(8,128)(2,1)S(1)}, bf16[272,512]{1,0:T(8,128)(2,1)S(1)}, u32[]{:S(2)}, u32[]{:S(2)}) collective-permute-start(bf16[272,512]{1,0:T(8,128)(2,1)S(1)} %get-tuple-element.117.refs_0_.refs_10_), channel_id=1, source_target_pairs={{2,0},{4,2},{6,4},{7,6},{5,7},{3,5},{1,3},{0,1},{10,8},{12,10},{14... | collective-permute-start | bytes 835592 | tf_op jit(solution)/shard_map/ppermute | solution.py:60
  111.3 7.2 %collective-permute-start.21 = (bf16[272,512]{1,0:T(8,128)(2,1)S(1)}, bf16[272,512]{1,0:T(8,128)(2,1)S(1)}, u32[]{:S(2)}, u32[]{:S(2)}) collective-permute-start(bf16[272,512]{1,0:T(8,128)(2,1)S(1)} %collective-permute-done.19.refs_0_.refs_13_), channel_id=1, source_target_pairs={{0,2},{2,4},{4,6},{6,7},{7,5},{5,3},{3,1},{1,0},{8,10},{10,12},{12... | collective-permute-start | bytes 835592 | tf_op jit(solution)/shard_map/ppermute | solution.py:57
  119.7 7.5 %collective-permute-start.25 = (bf16[144,512]{1,0:T(8,128)(2,1)}, bf16[144,512]{1,0:T(8,128)(2,1)}, u32[]{:S(2)}, u32[]{:S(2)}) collective-permute-start(bf16[144,512]{1,0:T(8,128)(2,1)} %get-tuple-element.126), channel_id=1, source_target_pairs={{2,0},{4,2},{6,4},{7,6},{5,7},{3,5},{1,3},{0,1},{10,8},{12,10},{14... | collective-permute-start | bytes 442376 | tf_op jit(solution)/shard_map/ppermute | solution.py:60
  133.6 9.7 %collective-permute-start.26 = (bf16[144,512]{1,0:T(8,128)(2,1)S(1)}, bf16[144,512]{1,0:T(8,128)(2,1)S(1)}, u32[]{:S(2)}, u32[]{:S(2)}) collective-permute-start(bf16[144,512]{1,0:T(8,128)(2,1)S(1)} %get-tuple-element.137), channel_id=1, source_target_pairs={{0,2},{2,4},{4,6},{6,7},{7,5},{5,3},{3,1},{1,0},{8,10},{10,12},{12... | collective-permute-start | bytes 442376 | tf_op jit(solution)/shard_map/ppermute | solution.py:57
  134.2 7.3 %collective-permute-start.27 = (bf16[128,512]{1,0:T(8,128)(2,1)S(1)}, bf16[128,512]{1,0:T(8,128)(2,1)S(1)}, u32[]{:S(2)}, u32[]{:S(2)}) collective-permute-start(bf16[128,512]{1,0:T(8,128)(2,1)S(1)} %get-tuple-element.139), channel_id=1, source_target_pairs={{2,0},{4,2},{6,4},{7,6},{5,7},{3,5},{1,3},{0,1},{10,8},{12,10},{14... | collective-permute-start | bytes 393224 | tf_op jit(solution)/shard_map/ppermute | solution.py:60
  141.6 7.9 %collective-permute-start.29 = (bf16[272,512]{1,0:T(8,128)(2,1)S(1)}, bf16[272,512]{1,0:T(8,128)(2,1)S(1)}, u32[]{:S(2)}, u32[]{:S(2)}) collective-permute-start(bf16[272,512]{1,0:T(8,128)(2,1)S(1)} %shard_map.198), channel_id=1, source_target_pairs={{2,0},{4,2},{6,4},{7,6},{5,7},{3,5},{1,3},{0,1},{10,8},{12,10},{14... | collective-permute-start | bytes 835592 | tf_op jit(solution)/shard_map/ppermute | solution.py:60
  143.3 8.0 %collective-permute-start.28 = (bf16[272,512]{1,0:T(8,128)(2,1)S(1)}, bf16[272,512]{1,0:T(8,128)(2,1)S(1)}, u32[]{:S(2)}, u32[]{:S(2)}) collective-permute-start(bf16[272,512]{1,0:T(8,128)(2,1)S(1)} %shard_map.197), channel_id=1, source_target_pairs={{0,2},{2,4},{4,6},{6,7},{7,5},{5,3},{3,1},{1,0},{8,10},{10,12},{12... | collective-permute-start | bytes 835592 | tf_op jit(solution)/shard_map/ppermute | solution.py:57
  149.6 8.0 %collective-permute-start.31 = (bf16[272,512]{1,0:T(8,128)(2,1)S(1)}, bf16[272,512]{1,0:T(8,128)(2,1)S(1)}, u32[]{:S(2)}, u32[]{:S(2)}) collective-permute-start(bf16[272,512]{1,0:T(8,128)(2,1)S(1)} %shard_map.201), channel_id=1, source_target_pairs={{2,0},{4,2},{6,4},{7,6},{5,7},{3,5},{1,3},{0,1},{10,8},{12,10},{14... | collective-permute-start | bytes 835592 | tf_op jit(solution)/shard_map/ppermute | solution.py:60
  151.3 8.3 %collective-permute-start.30 = (bf16[272,512]{1,0:T(8,128)(2,1)S(1)}, bf16[272,512]{1,0:T(8,128)(2,1)S(1)}, u32[]{:S(2)}, u32[]{:S(2)}) collective-permute-start(bf16[272,512]{1,0:T(8,128)(2,1)S(1)} %shard_map.200), channel_id=1, source_target_pairs={{0,2},{2,4},{4,6},{6,7},{7,5},{5,3},{3,1},{1,0},{8,10},{10,12},{12... | collective-permute-start | bytes 835592 | tf_op jit(solution)/shard_map/ppermute | solution.py:57
  170.6 18.5 %all-to-all-start.1 = ((bf16[8,64,512]{2,1,0:T(8,128)(2,1)}), bf16[8,64,512]{2,1,0:T(8,128)(2,1)S(1)}, u32[]{:S(2)}, u32[]{:S(2)}) async-start(bf16[8,64,512]{2,1,0:T(8,128)(2,1)} %shard_map.208), calls=%async_computation.1 | async-start | bytes 1048576 | tf_op jit(solution)/shard_map/all_to_all | solution.py:1133
  (48 other events, 354.9 us)
